TPU v7x, 32 devices: a whole 2x2x4 slice. The times are simulated.
32 devices in a mesh: drift: 16 (over z, x, core), radius: 2 (over y).
Axes of the slice: x: 2, y: 2, z: 4, core: 2. Of those that a mesh axis runs over, the one named last changes fastest.
Arguments:
- ions: float32 [256, 128, 256], P('drift', 'radius'), may hold values from 0 to 2
- potential_guess: float32 [256, 128, 256], P('drift', 'radius'), may hold values from -6 to 6
- permittivity: float32 [256, 128, 256], P('drift', 'radius'), may hold values from 0.5 to 2
- recombination: float32 [128, 256], P('radius'), may hold values from 0.1 to 1
- rate_index: int32 [128, 256], P('radius'), may hold values from 0 to 15
- gap_mask: int32 [128, 256], P('radius'), may hold values 0 or 1
- rate_table: float32 [16], replicated, may hold values from 0.2 to 2
Outputs:
- charge: float32 [256, 128, 256], P('drift', 'radius')
- potential: float32 [256, 128, 256], P('drift', 'radius')
- distortion: float32 [2, 256, 128, 256], P(None, 'drift', 'radius')
All inputs are finite; a program needn't handle non-finite values. No bound on the sum of `gap_mask` on one device may be relied on, other than what follows from the above.
Results may differ from a plain program's by a relative error of at most 0.0003.
Values sent between devices are 32-bit elements; how exact they have to be, the bound alone decides.
No kernel may reach another device: no remote copies, remote signals or barrier semaphores. Data moves between devices by JAX's collectives and lax.ppermute only.
A program may use at most 64 MiB of HBM per device.

v0:
```python
import jax
import jax.numpy as jnp
from jax import lax
from jax.sharding import PartitionSpec as P

TRANSITS = 2
SWEEPS = 4


def passed_along(block, axis, distance):
    devices = range(lax.axis_size(axis))
    route = [(i - distance, i) for i in devices if i - distance in devices]
    return lax.ppermute(block, axis, route)


def with_halo(cells, sides, width):
    for axis, dim in sides:
        count = lax.axis_size(axis)
        ends = count - 1
        head = lax.slice_in_dim(cells, 0, width, axis=dim)
        tail = lax.slice_in_dim(cells, cells.shape[dim] - width, cells.shape[dim], axis=dim)
        cells = jnp.concatenate(
            [
                lax.ppermute(tail, axis, [(i, (i + 1) % count) for i in range(ends)]),
                cells,
                lax.ppermute(head, axis, [((i + 1) % count, i) for i in range(ends)]),
            ],
            axis=dim,
        )
    return cells


def prefix(value, axis, join, neutral):
    count, mine = (lax.axis_size(axis), lax.axis_index(axis))
    pieces = lax.all_gather(value, axis)
    total = jnp.full_like(value, 0) + jnp.asarray(neutral, value.dtype)

    def lap(position, total):
        longer = join(total, pieces[position])
        return jnp.where(position < mine, longer, total)

    return lax.fori_loop(0, count - 1, lap, total)


def relax(phi_x, rho_x, eps_x, rpos_x, inside_x, half):
    phi_a = jnp.pad(phi_x, ((0, 0), (0, 0), (1, 1)))
    eps_a = jnp.pad(eps_x, ((0, 0), (0, 0), (1, 1)))
    center = eps_x[1:-1, 1:-1]
    radial = rpos_x[1:-1][:, None]
    z_up = 0.5 * (center + eps_x[2:, 1:-1])
    z_down = 0.5 * (center + eps_x[:-2, 1:-1])
    r_up = 0.5 * (center + eps_x[1:-1, 2:]) * ((radial + half) / radial)
    r_down = 0.5 * (center + eps_x[1:-1, :-2]) * ((radial - half) / radial)
    a_up = 0.5 * (center + eps_a[1:-1, 1:-1, 2:]) / (radial * radial)
    a_down = 0.5 * (center + eps_a[1:-1, 1:-1, :-2]) / (radial * radial)
    total = z_up * phi_x[2:, 1:-1] + z_down * phi_x[:-2, 1:-1]
    total = total + r_up * phi_x[1:-1, 2:] + r_down * phi_x[1:-1, :-2]
    total = total + a_up * phi_a[1:-1, 1:-1, 2:] + a_down * phi_a[1:-1, 1:-1, :-2]
    diag = z_up + z_down + r_up + r_down + a_up + a_down
    inner = inside_x[1:-1, 1:-1]
    safe = jnp.where(inner > 0, diag, 1.0)
    return (rho_x[1:-1, 1:-1] + total) / safe * inner


def body(ions, potential_guess, permittivity, recombination, rate_index, gap_mask, rate_table):
    slab_z, band_r, sector = ions.shape
    total_z = slab_z * lax.axis_size("drift")
    total_r = band_r * lax.axis_size("radius")
    z_first = lax.axis_index("drift") * slab_z
    r_first = lax.axis_index("radius") * band_r
    levels = jnp.arange(rate_table.shape[0], dtype=jnp.int32)
    picked = jnp.sum(jnp.where(rate_index[:, :, None] == levels, rate_table, 0.0), axis=2)
    inject = picked * (1 - gap_mask).astype(jnp.float32)
    charge = ions
    for step in range(TRANSITS):
        slab = passed_along(charge, "drift", 1)
        charge = slab / (1.0 + recombination * slab) + inject
    half = 0.5 / total_r
    extended = with_halo(
        jnp.stack([potential_guess, charge, permittivity]), (("drift", 1), ("radius", 2)), SWEEPS
    )
    z_cells = z_first - SWEEPS + jnp.arange(slab_z + 2 * SWEEPS, dtype=jnp.int32)
    r_cells = r_first - SWEEPS + jnp.arange(band_r + 2 * SWEEPS, dtype=jnp.int32)
    inside = ((z_cells >= 0) & (z_cells < total_z))[:, None] & (
        (r_cells >= 0) & (r_cells < total_r)
    )[None, :]
    rpos = ((total_r + r_cells).astype(jnp.float32) + 0.5) / total_r
    inside, rpos = (inside[:, :, None].astype(jnp.float32), rpos)
    z_end = extended.shape[1]
    r_end = extended.shape[2]
    potential = extended[0]
    for sweep in range(SWEEPS):
        rho_x = extended[1, sweep : z_end - sweep, sweep : r_end - sweep]
        eps_x = extended[2, sweep : z_end - sweep, sweep : r_end - sweep]
        potential = relax(
            potential,
            rho_x,
            eps_x,
            rpos[sweep : r_end - sweep],
            inside[sweep : z_end - sweep, sweep : r_end - sweep],
            half,
        )
    radial_ext = with_halo(potential, (("radius", 1),), 1)
    azimuth_ext = jnp.pad(potential, ((0, 0), (0, 0), (1, 1)))
    radial = (
        ((total_r + r_first + jnp.arange(band_r, dtype=jnp.int32)).astype(jnp.float32) + 0.5)
        / total_r
    )[:, None]
    field_r = -(radial_ext[:, 2:] - radial_ext[:, :-2]) * 0.5
    field_a = -(azimuth_ext[:, :, 2:] - azimuth_ext[:, :, :-2]) * 0.5 / radial
    scale = 1.0 / (8.0 * 1.09)
    ratios = jnp.stack([(field_r + 0.3 * field_a) * scale, (field_a - 0.3 * field_r) * scale])
    local = jnp.cumsum(ratios, axis=1)
    totals = local[:, -1]

    def combine(earlier, later):
        return earlier + later

    below = prefix(totals, "drift", combine, jnp.zeros_like(totals))
    distortion = local + below[:, None]
    return (charge, potential, distortion)


def solution(mesh):
    return jax.shard_map(
        body,
        mesh=mesh,
        in_specs=(
            P("drift", "radius", None),
            P("drift", "radius", None),
            P("drift", "radius", None),
            P("radius", None),
            P("radius", None),
            P("radius", None),
            P(),
        ),
        out_specs=(
            P("drift", "radius", None),
            P("drift", "radius", None),
            P(None, "drift", "radius", None),
        ),
        check_vma=False,
    )
```

profile of v0, /device:TPU:0, one launch (start us, length us, event | category | flops | bytes accessed | tf_op | source)
XLA Modules:
  0.0 174.3 jit_solution(2993553484541727007)
XLA Ops:
  7.2 2.5 %collective-permute-start = (f32[16,64,256]{2,1,0:T(8,128)}, f32[16,64,256]{2,1,0:T(8,128)S(1)}, u32[]{:S(2)}, u32[]{:S(2)}) collective-permute-start(f32[16,64,256]{2,1,0:T(8,128)} %param.9), channel_id=1, source_target_pairs={{0,2},{2,4},{4,6},{6,8},{8,10},{10,12},{12,14},{14,16},{16,18},{18... | collective-permute-start | bytes 3145736 | tf_op jit(solution)/shard_map/ppermute | solution.py:13
  9.7 1.2 select_reduce_fusion
  13.1 14.3 %collective-permute-start.1 = (f32[16,64,256]{2,1,0:T(8,128)S(1)}, f32[16,64,256]{2,1,0:T(8,128)S(1)}, u32[]{:S(2)}, u32[]{:S(2)}) collective-permute-start(f32[16,64,256]{2,1,0:T(8,128)S(1)} %divide_add_fusion.1), channel_id=1, source_target_pairs={{0,2},{2,4},{4,6},{6,8},{8,10},{10,12},{12,14},{14,16},{16,18},{18... | collective-permute-start | bytes 3145736 | tf_op jit(solution)/shard_map/ppermute | solution.py:13
  27.8 1.8 %collective-permute-done.1 = f32[16,64,256]{2,1,0:T(8,128)S(1)} collective-permute-done((f32[16,64,256]{2,1,0:T(8,128)S(1)}, f32[16,64,256]{2,1,0:T(8,128)S(1)}, u32[]{:S(2)}, u32[]{:S(2)}) %collective-permute-start.1) | collective-permute-done | bytes 1048608 | tf_op jit(solution)/shard_map/ppermute | solution.py:13
  30.9 1.3 collective-permute-start.3
  32.2 14.4 %collective-permute-start.2 = (f32[3,4,64,256]{3,2,1,0:T(8,128)S(1)}, f32[3,4,64,256]{3,2,1,0:T(8,128)S(1)}, u32[]{:S(2)}, u32[]{:S(2)}) collective-permute-start(f32[3,4,64,256]{3,2,1,0:T(8,128)S(1)} %get-tuple-element.117), channel_id=1, source_target_pairs={{0,2},{2,4},{4,6},{6,8},{8,10},{10,12},{12,14},{14,16},{16,18},{18... | collective-permute-start | bytes 2359304 | tf_op jit(solution)/shard_map/ppermute | solution.py:24
  46.9 1.5 collective-permute-done.2
  49.5 1.3 collective-permute-start.5
  50.8 6.0 %collective-permute-start.4 = (f32[3,24,4,256]{3,2,1,0:T(4,128)}, f32[3,24,4,256]{3,2,1,0:T(4,128)}, u32[]{:S(2)}, u32[]{:S(2)}) collective-permute-start(f32[3,24,4,256]{3,2,1,0:T(4,128)} %get-tuple-element.115), channel_id=1, source_target_pairs={{0,1},{2,3},{4,5},{6,7},{8,9},{10,11},{12,13},{14,15},{16,17},{18,... | collective-permute-start | bytes 884744 | tf_op jit(solution)/shard_map/ppermute | solution.py:24
  57.0 1.5 collective-permute-done.5
  58.5 2.2 %collective-permute-done.4 = f32[3,24,4,256]{3,2,1,0:T(4,128)} collective-permute-done((f32[3,24,4,256]{3,2,1,0:T(4,128)}, f32[3,24,4,256]{3,2,1,0:T(4,128)}, u32[]{:S(2)}, u32[]{:S(2)}) %collective-permute-start.4) | collective-permute-done | bytes 294944 | tf_op jit(solution)/shard_map/ppermute | solution.py:24
  60.6 2.2 %pad_maximum_fusion = f32[3,24,72,256]{3,2,1,0:T(8,128)S(1)} fusion(f32[3,24,4,256]{3,2,1,0:T(4,128)} %collective-permute-done.5, f32[3,4,64,256]{3,2,1,0:T(8,128)} %copy-done.5, f32[1,16,64,256]{3,2,1,0:T(8,128)S(1)} %bitcast.49, f32[1,16,64,256]{3,2,1,0:T(8,128)S(1)} %fusion.100, f32[1,16,64,256]{3,2,1,0:T(8,128)S(1)} %bitcast.52, ...), kind=kLoop, calls=%fused_computation.1 | loop fusion | flops 7962624 | bytes 10616832 | tf_op jit(solution)/shard_map/concatenate | solution.py:22
  64.0 4.7 %fusion.15 = f32[22,70,256]{2,1,0:T(8,128)S(1)} fusion(f32[24,72,256]{2,1,0:T(8,128)S(1)} %get-tuple-element.113, f32[24,72,256]{2,1,0:T(8,128)S(1)} %get-tuple-element.114, f32[24,72,256]{2,1,0:T(8,128)S(1)} %get-tuple-element.112, f32[22,70]{1,0:T(8,128)S(1)} %slice_bitcast_fusion.11, f32[70]{0:T(128)S(1)} %get-tuple-element.133, ...), kind=kLoop, calls=%fused_computation.38 | loop fusion | flops 13404160 | bytes 21352960 | tf_op jit(solution)/shard_map/mul | solution.py:62
  68.8 4.0 %fusion.35 = f32[20,68,256]{2,1,0:T(8,128)S(1)} fusion(f32[22,70,256]{2,1,0:T(8,128)S(1)} %fusion.15, f32[22,70,256]{2,1,0:T(8,128)S(1)} %get-tuple-element.111, f32[22,70,256]{2,1,0:T(8,128)S(1)} %get-tuple-element.110, f32[20,68]{1,0:T(8,128)S(1)} %slice_bitcast_fusion.10, f32[68]{0:T(128)S(1)} %get-tuple-element.130, f32[68]{0:T(128)S(1)} %get-tuple-element.131, ...), kind=kLoop, calls=%fused_computation.68 | loop fusion | flops 11837440 | bytes 19399168 | tf_op jit(solution)/shard_map/mul | solution.py:62
  72.8 3.8 %fusion.55 = f32[18,66,256]{2,1,0:T(8,128)S(1)} fusion(f32[20,68,256]{2,1,0:T(8,128)S(1)} %fusion.35, f32[20,68,256]{2,1,0:T(8,128)S(1)} %get-tuple-element.109, f32[20,68,256]{2,1,0:T(8,128)S(1)} %get-tuple-element.108, f32[18,66]{1,0:T(8,128)S(1)} %slice_bitcast_fusion.9, f32[66]{0:T(128)S(1)} %get-tuple-element.127, f32[66]{0:T(128)S(1)} %get-tuple-element.128, ...), kind=kLoop, calls=%fused_computation.98 | loop fusion | flops 10340352 | bytes 17453568 | tf_op jit(solution)/shard_map/mul | solution.py:62
  76.6 2.9 %fusion.89 = f32[16,64,256]{2,1,0:T(8,128)S(1)} fusion(f32[18,66,256]{2,1,0:T(8,128)S(1)} %fusion.55, f32[18,66,256]{2,1,0:T(8,128)S(1)} %get-tuple-element.107, f32[18,66,256]{2,1,0:T(8,128)S(1)} %get-tuple-element.106, f32[16,64]{1,0:T(8,128)S(1)} %slice_bitcast_fusion.12, f32[64]{0:T(128)S(1)} %get-tuple-element.124, f32[64]{0:T(128)S(1)} %get-tuple-element.125, ...), kind=kLoop, calls=%fused_computation.159 | loop fusion | flops 8912896 | bytes 14200320 | tf_op jit(solution)/shard_map/mul | solution.py:62
  79.5 4.4 %collective-permute-start.7 = (f32[16,1,256]{2,1,0:T(1,128)S(1)}, f32[16,1,256]{2,1,0:T(1,128)S(1)}, u32[]{:S(2)}, u32[]{:S(2)}) collective-permute-start(f32[16,1,256]{2,1,0:T(1,128)S(1)} %get-tuple-element.122), channel_id=1, source_target_pairs={{0,1},{2,3},{4,5},{6,7},{8,9},{10,11},{12,13},{14,15},{16,17},{18,... | collective-permute-start | bytes 49160 | tf_op jit(solution)/shard_map/ppermute | solution.py:24
  83.9 1.3 collective-permute-start.6
  85.4 4.2 %collective-permute-done.6 = f32[16,1,256]{2,1,0:T(1,128)S(1)} collective-permute-done((f32[16,1,256]{2,1,0:T(1,128)S(1)}, f32[16,1,256]{2,1,0:T(1,128)S(1)}, u32[]{:S(2)}, u32[]{:S(2)}) %collective-permute-start.6) | collective-permute-done | bytes 16416 | tf_op jit(solution)/shard_map/ppermute | solution.py:26
  89.6 1.2 multiply_bitcast_fusion.1
  92.0 1.2 divide_add_fusion
  93.2 58.1 %all-gather.3.cloned.1.call-done = f32[32,1,64,256]{3,2,1,0:T(8,128)} async-done(((f32[2,1,64,256]{3,2,1,0:T(8,128)}), f32[32,1,64,256]{3,2,1,0:T(8,128)}) %all-gather.3.cloned.1.call-update) | async-done | bytes 2097168 | tf_op jit(solution)/shard_map/all_gather | solution.py:35
  151.3 14.6 %while.14 = (s32[]{:T(128)}, f32[2,64,256]{2,1,0:T(8,128)S(1)}, s32[]{:T(128)}, f32[16,2,64,256]{3,2,1,0:T(8,128)}, s32[]{:T(128)}, /*index=5*/s32[]{:T(128)}) while((s32[]{:T(128)}, f32[2,64,256]{2,1,0:T(8,128)S(1)}, s32[]{:T(128)}, f32[16,2,64,256]{3,2,1,0:T(8,128)}, s32[]{:T(128)}, /*index=5*/s32[]{:T(128)}) %tuple.58), condition=%wide.region_3.4_spmd.clone, body=%wide.region_2.3_spmd.clone.sunk | while | flops 98308 | bytes 393317 | solution.py:42
  165.9 1.5 broadcast_add_fusion
  (66 shorter events, 22.1 us)
Async XLA Ops:
  7.2 23.4 %copy-start.7 = (f32[64,256]{1,0:T(8,128)S(1)}, f32[64,256]{1,0:T(8,128)}, u32[]{:S(2)}) copy-start(f32[64,256]{1,0:T(8,128)} %param.12) | copy-start | bytes 196612
  7.2 144.1 %all-gather.3.cloned.1.call-start = ((), (), s32[]{:S(2)}) async-start(), calls=%async_computation | async-start | bytes 2228224 | tf_op jit(solution)/shard_map/all_gather | solution.py:35
  7.2 4.9 %collective-permute-start = (f32[16,64,256]{2,1,0:T(8,128)}, f32[16,64,256]{2,1,0:T(8,128)S(1)}, u32[]{:S(2)}, u32[]{:S(2)}) collective-permute-start(f32[16,64,256]{2,1,0:T(8,128)} %param.9), channel_id=1, source_target_pairs={{0,2},{2,4},{4,6},{6,8},{8,10},{10,12},{12,14},{14,16},{16,18},{18... | collective-permute-start | bytes 3145736 | tf_op jit(solution)/shard_map/ppermute | solution.py:13
  13.1 17.6 %copy-start = (f32[16,64,256]{2,1,0:T(8,128)S(1)}, f32[16,64,256]{2,1,0:T(8,128)}, u32[]{:S(2)}) copy-start(f32[16,64,256]{2,1,0:T(8,128)} %param.11) | copy-start | bytes 3145732
  13.1 17.6 %copy-start.1 = (f32[16,64,256]{2,1,0:T(8,128)S(1)}, f32[16,64,256]{2,1,0:T(8,128)}, u32[]{:S(2)}) copy-start(f32[16,64,256]{2,1,0:T(8,128)} %param.10) | copy-start | bytes 3145732
  13.1 16.5 %collective-permute-start.1 = (f32[16,64,256]{2,1,0:T(8,128)S(1)}, f32[16,64,256]{2,1,0:T(8,128)S(1)}, u32[]{:S(2)}, u32[]{:S(2)}) collective-permute-start(f32[16,64,256]{2,1,0:T(8,128)S(1)} %divide_add_fusion.1), channel_id=1, source_target_pairs={{0,2},{2,4},{4,6},{6,8},{8,10},{10,12},{12,14},{14,16},{16,18},{18... | collective-permute-start | bytes 3145736 | tf_op jit(solution)/shard_map/ppermute | solution.py:13
  29.6 1.0 copy-start.3
  30.9 16.0 %collective-permute-start.3 = (f32[3,4,64,256]{3,2,1,0:T(8,128)S(1)}, f32[3,4,64,256]{3,2,1,0:T(8,128)S(1)}, u32[]{:S(2)}, u32[]{:S(2)}) collective-permute-start(f32[3,4,64,256]{3,2,1,0:T(8,128)S(1)} %get-tuple-element.118), channel_id=1, source_target_pairs={{2,0},{4,2},{6,4},{8,6},{10,8},{12,10},{14,12},{16,14},{18,16},{20... | collective-permute-start | bytes 2359304 | tf_op jit(solution)/shard_map/ppermute | solution.py:26
  32.2 16.3 %collective-permute-start.2 = (f32[3,4,64,256]{3,2,1,0:T(8,128)S(1)}, f32[3,4,64,256]{3,2,1,0:T(8,128)S(1)}, u32[]{:S(2)}, u32[]{:S(2)}) collective-permute-start(f32[3,4,64,256]{3,2,1,0:T(8,128)S(1)} %get-tuple-element.117), channel_id=1, source_target_pairs={{0,2},{2,4},{4,6},{6,8},{8,10},{10,12},{12,14},{14,16},{16,18},{18... | collective-permute-start | bytes 2359304 | tf_op jit(solution)/shard_map/ppermute | solution.py:24
  46.9 2.6 %copy-start.5 = (f32[3,4,64,256]{3,2,1,0:T(8,128)}, f32[3,4,64,256]{3,2,1,0:T(8,128)S(1)}, u32[]{:S(2)}) copy-start(f32[3,4,64,256]{3,2,1,0:T(8,128)S(1)} %collective-permute-done.3) | copy-start | bytes 2359300
  48.5 1.1 copy-start.6
  49.5 8.9 %collective-permute-start.5 = (f32[3,24,4,256]{3,2,1,0:T(4,128)}, f32[3,24,4,256]{3,2,1,0:T(4,128)}, u32[]{:S(2)}, u32[]{:S(2)}) collective-permute-start(f32[3,24,4,256]{3,2,1,0:T(4,128)} %get-tuple-element.116), channel_id=1, source_target_pairs={{1,0},{3,2},{5,4},{7,6},{9,8},{11,10},{13,12},{15,14},{17,16},{19,... | collective-permute-start | bytes 884744 | tf_op jit(solution)/shard_map/ppermute | solution.py:26
  50.8 9.8 %collective-permute-start.4 = (f32[3,24,4,256]{3,2,1,0:T(4,128)}, f32[3,24,4,256]{3,2,1,0:T(4,128)}, u32[]{:S(2)}, u32[]{:S(2)}) collective-permute-start(f32[3,24,4,256]{3,2,1,0:T(4,128)} %get-tuple-element.115), channel_id=1, source_target_pairs={{0,1},{2,3},{4,5},{6,7},{8,9},{10,11},{12,13},{14,15},{16,17},{18,... | collective-permute-start | bytes 884744 | tf_op jit(solution)/shard_map/ppermute | solution.py:24
  79.5 11.2 %copy-start.2 = (f32[16,64,256]{2,1,0:T(8,128)}, f32[16,64,256]{2,1,0:T(8,128)S(1)}, u32[]{:S(2)}) copy-start(f32[16,64,256]{2,1,0:T(8,128)S(1)} %fusion.89) | copy-start | bytes 3145732
  79.5 5.8 %collective-permute-start.7 = (f32[16,1,256]{2,1,0:T(1,128)S(1)}, f32[16,1,256]{2,1,0:T(1,128)S(1)}, u32[]{:S(2)}, u32[]{:S(2)}) collective-permute-start(f32[16,1,256]{2,1,0:T(1,128)S(1)} %get-tuple-element.122), channel_id=1, source_target_pairs={{0,1},{2,3},{4,5},{6,7},{8,9},{10,11},{12,13},{14,15},{16,17},{18,... | collective-permute-start | bytes 49160 | tf_op jit(solution)/shard_map/ppermute | solution.py:24
  83.9 5.6 %collective-permute-start.6 = (f32[16,1,256]{2,1,0:T(1,128)S(1)}, f32[16,1,256]{2,1,0:T(1,128)S(1)}, u32[]{:S(2)}, u32[]{:S(2)}) collective-permute-start(f32[16,1,256]{2,1,0:T(1,128)S(1)} %get-tuple-element.121), channel_id=1, source_target_pairs={{1,0},{3,2},{5,4},{7,6},{9,8},{11,10},{13,12},{15,14},{17,16},{19,... | collective-permute-start | bytes 49160 | tf_op jit(solution)/shard_map/ppermute | solution.py:26
  90.7 1.3 copy-start.4
Sparse Core Ops, SparseCore 0:
  91.8 59.4 all-gather.2
where the time goes:
time: 175 us; the launch traced here: 174 us
  waiting for transfers between devices  69.6 us (40%)
  starting transfers between devices  45.4 us (26%)
  other arithmetic  41.1 us (23%)
  between operations  14.3 us (8%)
  local copies, waits for them, and re-layouts  3.51 us (2%)
    all_gather x1, waiting for transfers between devices, prefix(): pieces = lax.all_gather(value, axis)  58.1 us
    ppermute x3, starting transfers between devices, with_halo(): lax.ppermute(tail, axis, [(i, (i + 1) % count) for i in range(ends)])  24.8 us
    ppermute x2, starting transfers between devices, passed_along(): return lax.ppermute(block, axis, route)  16.7 us
    mul x4, other arithmetic, relax(): return (rho_x[1:-1, 1:-1] + total) / safe * inner  15.4 us
    select_n x15, other arithmetic, lap(): return jnp.where(position < mine, longer, total)  14.3 us
    ppermute x3, waiting for transfers between devices, with_halo(): lax.ppermute(head, axis, [((i + 1) % count, i) for i in range(ends)])  5.71 us
    ppermute x3, starting transfers between devices, with_halo(): lax.ppermute(head, axis, [((i + 1) % count, i) for i in range(ends)])  3.86 us
    ppermute x3, waiting for transfers between devices, with_halo(): lax.ppermute(tail, axis, [(i, (i + 1) % count) for i in range(ends)])  3.82 us
  transfers between devices with their start and end apart: 9, of which 8 were waited for; matrix products, arithmetic and copies ran while one was open for 2% of the time, Pallas kernels for 0%

commit v1 on v0

v1 whole, which is shorter than its diff:
```python
import jax
import jax.numpy as jnp
from jax import lax
from jax.experimental import pallas as pl
from jax.experimental.pallas import tpu as pltpu
from jax.sharding import PartitionSpec as P

SWEEPS = 4
ROWS = 8
VMEM = pltpu.MemorySpace.VMEM


def shifted(block, axis, distance):
    count = lax.axis_size(axis)
    route = [(i, i + distance) for i in range(count) if 0 <= i + distance < count]
    return lax.ppermute(block, axis, route)


def edges(block):
    band = block.shape[-2]
    if lax.axis_size("radius") == 2:
        start = jnp.where(lax.axis_index("radius") == 0, band - ROWS, 0)
        return (lax.dynamic_slice_in_dim(block, start, ROWS, axis=block.ndim - 2),)
    tail = lax.slice_in_dim(block, band - ROWS, band, axis=block.ndim - 2)
    head = lax.slice_in_dim(block, 0, ROWS, axis=block.ndim - 2)
    return (tail, head)


def radial(blocks):
    if len(blocks) == 1:
        got = lax.ppermute(blocks[0], "radius", [(0, 1), (1, 0)])
        return got, got
    return shifted(blocks[0], "radius", 1), shifted(blocks[1], "radius", -1)


def transit(slab, rec, inj):
    return slab / (1.0 + rec * slab) + inj


def roll(x, amount, axis):
    return pltpu.roll(x, amount % x.shape[axis], axis)


def lane_pair(x, lane):
    return roll(x, -1, 1), roll(x, 1, 1)


def relax_kernel(
    phi, eps, moved, moved_lo, moved_hi, raw_lo, raw_hi, below, above, far, corner_lo, corner_hi, pads,
    charge_out, potential_out, window_out, sums_out,
    p0, p1, ex, bx, wzu, wzd, wru, wrd, wau, wad, geo,
):
    layers, band, sector = phi.shape
    depth = SWEEPS
    zs = layers + 2 * depth
    rows = band + 2 * ROWS
    d, drifts = lax.axis_index("drift"), lax.axis_size("drift")
    r, bands = lax.axis_index("radius"), lax.axis_size("radius")
    total_r = band * bands
    has_lo, has_hi = r > 0, r < bands - 1
    own = slice(ROWS, ROWS + band)
    top = slice(ROWS + band, rows)
    tiles = rows // ROWS

    def blank(cond, value):
        return jnp.where(cond, value, 0.0)

    n = layers
    for dst, src, base, at_lo, at_hi in ((p0, phi, 0, 0, 0), (ex, eps, n, depth, depth)):
        dst[0:depth, own] = below[at_lo : at_lo + depth]
        dst[depth : depth + n, own] = src[...]
        dst[depth + n : zs, own] = above[at_hi : at_hi + depth]
        for side, raw, corner, has in ((slice(0, ROWS), raw_lo, corner_lo, has_lo), (top, raw_hi, corner_hi, has_hi)):
            dst[0:depth, side] = blank(has, corner[at_lo : at_lo + depth])
            dst[depth : depth + n, side] = blank(has, raw[base : base + n])
            up = 3 * depth - 1 + at_hi
            dst[depth + n : zs, side] = blank(has, corner[up : up + depth])

    row = lax.broadcasted_iota(jnp.int32, (rows, sector), 0) - ROWS + r * band
    lane = lax.broadcasted_iota(jnp.int32, (rows, sector), 1)
    rpos = ((total_r + row).astype(jnp.float32) + 0.5) / total_r
    half = 0.5 / total_r
    inside = (row >= 0) & (row < total_r)
    geo[0] = (rpos + half) / rpos
    geo[1] = (rpos - half) / rpos
    geo[2] = 1.0 / (rpos * rpos)
    geo[3] = jnp.where(inside, 1.0, 0.0)
    geo[4] = jnp.where(lane == sector - 1, 0.0, 1.0)
    geo[5] = jnp.where(lane == 0, 0.0, 1.0)
    geo[6, own] = pads[0]
    geo[7, own] = pads[1]
    for side, raw, has in ((slice(0, ROWS), raw_lo, has_lo), (top, raw_hi, has_hi)):
        geo[6, side] = blank(has, raw[3 * n])
        geo[7, side] = blank(has, raw[3 * n + 1])

    def drift_charge(ions, at, slab):
        rec, inj = geo[6, at], geo[7, at]
        once = transit(ions, rec, inj)
        return transit(jnp.where(slab >= 1, once, 0.0), rec, inj)

    @pl.loop(0, n)
    def _(z):
        value = drift_charge(moved[z], own, d)
        charge_out[z] = value
        bx[depth + z, own] = value
        bx[depth + z, 0:ROWS] = drift_charge(blank(has_lo, moved_lo[z]), slice(0, ROWS), d)
        bx[depth + z, top] = drift_charge(blank(has_hi, moved_hi[z]), top, d)

    for k in range(depth - 1):
        for z, ions, slab, at in ((1 + k, far, d - 1, k), (depth + n + k, below, d + 1, 2 * depth + k)):
            bx[z, own] = drift_charge(ions[at], own, slab)
            spot = 5 * depth - 1 + k if ions is far else 2 * depth + k
            bx[z, 0:ROWS] = drift_charge(blank(has_lo, corner_lo[spot]), slice(0, ROWS), slab)
            bx[z, top] = drift_charge(blank(has_hi, corner_hi[spot]), top, slab)

    sub = lax.broadcasted_iota(jnp.int32, (ROWS, sector), 0)

    def row_pairs(ref, z):
        x = [ref[z, t * ROWS : (t + 1) * ROWS] for t in range(tiles)]
        up = [roll(v, -1, 0) for v in x]
        down = [roll(v, 1, 0) for v in x]
        for t in range(tiles):
            higher = jnp.where(sub == ROWS - 1, up[(t + 1) % tiles], up[t])
            lower = jnp.where(sub == 0, down[(t - 1) % tiles], down[t])
            yield t, slice(t * ROWS, (t + 1) * ROWS), x[t], higher, lower

    @pl.loop(1, zs - 1)
    def _(z):
        zg = d * n - depth + z
        alive = jnp.where((zg >= 0) & (zg < drifts * n), 1.0, 0.0)
        for t, at, e, e_up, e_down in row_pairs(ex, z):
            right, left = lane_pair(e, None)
            not_last, not_first = geo[4, at], geo[5, at]
            inv_r2 = geo[2, at]
            zu = e + ex[z + 1, at]
            zd = e + ex[z - 1, at]
            ru = (e + e_up) * geo[0, at]
            rd = (e + e_down) * geo[1, at]
            au = (e + right * not_last) * inv_r2
            ad = (e + left * not_first) * inv_r2
            diag = ((zu + zd) + (ru + rd)) + (au + ad)
            keep = geo[3, at] * alive
            inv = jnp.where(keep > 0, 1.0 / diag, 0.0)
            wzu[z, at] = zu * inv
            wzd[z, at] = zd * inv
            wru[z, at] = ru * inv
            wrd[z, at] = rd * inv
            wau[z, at] = au * inv * not_last
            wad[z, at] = ad * inv * not_first
            bx[z, at] = bx[z, at] * (inv + inv)

    sums_out[...] = jnp.zeros_like(sums_out)
    for sweep in range(1, SWEEPS + 1):
        src, dst = (p0, p1) if sweep % 2 else (p1, p0)
        last = sweep == SWEEPS

        @pl.loop(sweep, zs - sweep)
        def _(z, src=src, dst=dst, last=last):
            for t, at, p, p_up, p_down in row_pairs(src, z):
                right, left = lane_pair(p, None)
                total = bx[z, at] + (wzu[z, at] * src[z + 1, at] + wzd[z, at] * src[z - 1, at])
                total = total + (wru[z, at] * p_up + wrd[z, at] * p_down)
                total = total + (wau[z, at] * right + wad[z, at] * left)
                if last:
                    window_out[z - depth, at] = total
                    sums_out[at] += total
                    if 0 < t < tiles - 1:
                        potential_out[z - depth, (t - 1) * ROWS : t * ROWS] = total
                else:
                    dst[z, at] = total


def integrate_kernel(window, prefix, out, run):
    layers, rows, sector = window.shape
    band = rows - 2 * ROWS
    r, bands = lax.axis_index("radius"), lax.axis_size("radius")
    total_r = band * bands
    tiles = rows // ROWS
    run[...] = prefix[...]
    sub = lax.broadcasted_iota(jnp.int32, (ROWS, sector), 0)
    lane = lax.broadcasted_iota(jnp.int32, (ROWS, sector), 1)
    scale = 1.0 / (8.0 * 1.09)

    @pl.loop(0, layers)
    def _(z):
        x = []
        for t in range(tiles):
            at = slice(t * ROWS, (t + 1) * ROWS)
            value = run[at] + window[z, at]
            run[at] = value
            x.append(value)
        up = [roll(v, -1, 0) for v in x]
        down = [roll(v, 1, 0) for v in x]
        for t in range(1, tiles - 1):
            row = sub + ((t - 1) * ROWS + r * band)
            rpos = ((total_r + row).astype(jnp.float32) + 0.5) / total_r
            higher = jnp.where(sub == ROWS - 1, up[t + 1], up[t])
            lower = jnp.where(sub == 0, down[t - 1], down[t])
            right = jnp.where(lane == sector - 1, 0.0, roll(x[t], -1, 1))
            left = jnp.where(lane == 0, 0.0, roll(x[t], 1, 1))
            er = (lower - higher) * 0.5
            ea = (left - right) * (0.5 / rpos)
            at = slice((t - 1) * ROWS, t * ROWS)
            out[0, z, at] = (er + 0.3 * ea) * scale
            out[1, z, at] = (ea - 0.3 * er) * scale


def sums_below(sums):
    count, mine = lax.axis_size("drift"), lax.axis_index("drift")
    assert count & (count - 1) == 0
    total, below, step = sums, jnp.zeros_like(sums), 1
    while step < count:
        other = lax.ppermute(total, "drift", [(i, i ^ step) for i in range(count)])
        below = below + jnp.where((mine & step) > 0, other, 0.0)
        total = total + other
        step *= 2
    return below


def body(ions, potential_guess, permittivity, recombination, rate_index, gap_mask, rate_table):
    layers, band, sector = ions.shape
    rows = band + 2 * ROWS
    zs = layers + 2 * SWEEPS
    f32 = jnp.float32
    levels = jnp.arange(rate_table.shape[0], dtype=jnp.int32)
    picked = jnp.sum(jnp.where(rate_index[:, :, None] == levels, rate_table, 0.0), axis=2)
    inject = picked * (1 - gap_mask).astype(f32)
    pads = jnp.stack([recombination, inject])

    up_block = jnp.concatenate(
        [potential_guess[layers - SWEEPS :], permittivity[layers - SWEEPS :], ions[: SWEEPS - 1]]
    )
    down_block = jnp.concatenate([potential_guess[:SWEEPS], permittivity[:SWEEPS]])
    below = shifted(up_block, "drift", 1)
    above = shifted(down_block, "drift", -1)
    far = shifted(ions[layers - SWEEPS + 1 :], "drift", 3)
    raw_lo, raw_hi = radial(
        tuple(jnp.concatenate(parts) for parts in zip(edges(potential_guess), edges(permittivity), edges(ions), edges(pads)))
    )
    swapped = len(edges(pads)) == 1
    moved_lo = shifted(raw_lo[2 * layers : 3 * layers], "drift", 2)
    moved_hi = moved_lo if swapped else shifted(raw_hi[2 * layers : 3 * layers], "drift", 2)
    moved = shifted(ions, "drift", 2)
    corner_lo, corner_hi = radial(
        tuple(jnp.concatenate(parts) for parts in zip(edges(below), edges(above), edges(far)))
    )
    plane = lambda *shape: jax.ShapeDtypeStruct(shape, f32)
    box = pltpu.VMEM((zs, rows, sector), f32)
    charge, potential, window, sums = pl.pallas_call(
        relax_kernel,
        out_shape=(
            plane(layers, band, sector),
            plane(layers, band, sector),
            plane(layers, rows, sector),
            plane(rows, sector),
        ),
        in_specs=[pl.BlockSpec(memory_space=VMEM)] * 13,
        out_specs=[pl.BlockSpec(memory_space=VMEM)] * 4,
        scratch_shapes=[box] * 10 + [pltpu.VMEM((8, rows, sector), f32)],
        name="relax",
    )(
        potential_guess, permittivity, moved, moved_lo, moved_hi, raw_lo, raw_hi, below, above, far,
        corner_lo, corner_hi, pads,
    )
    below_sums = sums_below(sums)
    distortion = pl.pallas_call(
        integrate_kernel,
        out_shape=plane(2, layers, band, sector),
        in_specs=[pl.BlockSpec(memory_space=VMEM)] * 2,
        out_specs=pl.BlockSpec(memory_space=VMEM),
        scratch_shapes=[pltpu.VMEM((rows, sector), f32)],
        name="integrate",
    )(window, below_sums)
    return charge, potential, distortion


def solution(mesh):
    return jax.shard_map(
        body,
        mesh=mesh,
        in_specs=(
            P("drift", "radius", None),
            P("drift", "radius", None),
            P("drift", "radius", None),
            P("radius", None),
            P("radius", None),
            P("radius", None),
            P(),
        ),
        out_specs=(
            P("drift", "radius", None),
            P("drift", "radius", None),
            P(None, "drift", "radius", None),
        ),
        check_vma=False,
    )
```

time: 175 us -> 94.8 us (0.54)
  waiting for transfers between devices: 69.6 us -> 27.4 us
  other arithmetic: 41.1 us -> 3.6 us
  Pallas kernels: 0 us -> 21.9 us
  between operations: 14.3 us -> 0.85 us
  starting transfers between devices: 45.4 us -> 33.1 us
  local copies, waits for them, and re-layouts: 3.51 us -> 7.42 us
    all_gather x1 -> x0, waiting for transfers between devices: 58.1 us -> none  [prefix(): pieces = lax.all_gather(value, axis)]
    pallas_call x0 -> x2, Pallas kernels: none -> 21.9 us  [the longest x1 17.5 us: body(): pl.pallas_call(relax_kernel, out_shape=(plane(layers, band, sector), plan...]
    mul x9 -> x0, other arithmetic: 16.6 us -> none  [the longest x4 15.4 us: relax(): return (rho_x[1:-1, 1:-1] + total) / safe * inner]
    ppermute x8 -> x11, waiting for transfers between devices: 11.4 us -> 27.4 us  [the longest x5 18.3 us: shifted(): return lax.ppermute(block, axis, route)]
    select_n x15 -> x0, other arithmetic: 14.3 us -> none  [lap(): return jnp.where(position < mine, longer, total)]
    ppermute x8 -> x11, starting transfers between devices: 45.4 us -> 33.1 us  [the longest x5 22 us: shifted(): return lax.ppermute(block, axis, route)]
    dynamic_slice x0 -> x5, local copies, waits for them, and re-layouts: none -> 2.67 us  [edges(): return (lax.dynamic_slice_in_dim(block, start, ROWS, axis=block.ndim - 2),)]
    slice x2 -> x3, local copies, waits for them, and re-layouts: 0.69 us -> 3.05 us  [the longest x1 1.74 us: body(): far = shifted(ions[layers - SWEEPS + 1:], 'drift', 3)]
  transfers between devices with their start and end apart: 9 -> 11, of which waited for: 8 -> 6; matrix products, arithmetic and copies ran while one was open for 2% -> 8% of each run, Pallas kernels for 0% -> 0%
where the time goes in v1:
time: 94.8 us; the launch traced here: 94.3 us
  starting transfers between devices  33.1 us (35%)
  waiting for transfers between devices  27.4 us (29%)
  Pallas kernels  21.9 us (23%)
  local copies, waits for them, and re-layouts  7.42 us (8%)
  other arithmetic  3.6 us (4%)
    ppermute x5, starting transfers between devices, shifted(): return lax.ppermute(block, axis, route)  22 us
    ppermute x5, waiting for transfers between devices, shifted(): return lax.ppermute(block, axis, route)  18.3 us
    pallas_call x1, Pallas kernels, body(): pl.pallas_call(relax_kernel, out_shape=(plane(layers, band, sector), plan...  17.5 us
    ppermute x4, waiting for transfers between devices, sums_below(): other = lax.ppermute(total, 'drift', [(i, i ^ step) for i in range(count)])  9.09 us
    ppermute x4, starting transfers between devices, sums_below(): other = lax.ppermute(total, 'drift', [(i, i ^ step) for i in range(count)])  7.94 us
    pallas_call x1, Pallas kernels, body(): pl.pallas_call(integrate_kernel, out_shape=plane(2, layers, band, sector)...  4.4 us
    ppermute x2, starting transfers between devices, radial(): got = lax.ppermute(blocks[0], 'radius', [(0, 1), (1, 0)])  3.17 us
    dynamic_slice x5, local copies, waits for them, and re-layouts, edges(): return (lax.dynamic_slice_in_dim(block, start, ROWS, axis=block.ndim - 2),)  2.67 us
  transfers between devices with their start and end apart: 11, of which 6 were waited for; matrix products, arithmetic and copies ran while one was open for 8% of the time, Pallas kernels for 0%

profile of v1, /device:TPU:0, one launch (start us, length us, event | category | flops | bytes accessed | tf_op | source)
XLA Modules:
  0.0 94.3 jit_solution(15866267562616338974)
XLA Ops:
  0.6 4.9 %collective-permute-start = (f32[16,64,256]{2,1,0:T(8,128)}, f32[16,64,256]{2,1,0:T(8,128)S(1)}, u32[]{:S(2)}, u32[]{:S(2)}) collective-permute-start(f32[16,64,256]{2,1,0:T(8,128)} %param.7), channel_id=1, source_target_pairs={{0,4},{2,6},{4,8},{6,10},{8,12},{10,14},{12,16},{14,18},{16,20},{1... | collective-permute-start | bytes 3145736 | tf_op jit(solution)/shard_map/ppermute | solution.py:16
  5.6 1.7 %fusion.1 = (f32[3,64,256]{2,1,0:T(8,128)}, f32[3,64,256]{2,1,0:T(8,128)S(1)}) fusion(f32[16,64,256]{2,1,0:T(8,128)} %param.7), kind=kLoop, calls=%fused_computation.18 | loop fusion | bytes 786432 | tf_op jit(solution)/shard_map/slice | solution.py:236
  7.3 1.3 %fusion.2 = (f32[4,64,256]{2,1,0:T(8,128)S(1)}, f32[4,64,256]{2,1,0:T(8,128)S(1)}, f32[4,64,256]{2,1,0:T(8,128)S(1)}, f32[4,64,256]{2,1,0:T(8,128)S(1)}) fusion(f32[16,64,256]{2,1,0:T(8,128)} %phi.1, f32[16,64,256]{2,1,0:T(8,128)} %eps.1), kind=kLoop, calls=%fused_computation.19 | loop fusion | bytes 2097152 | tf_op jit(solution)/shard_map/slice | solution.py:233
  8.7 1.5 %collective-permute-start.3 = (f32[11,64,256]{2,1,0:T(8,128)S(1)}, f32[11,64,256]{2,1,0:T(8,128)S(1)}, u32[]{:S(2)}, u32[]{:S(2)}) collective-permute-start(f32[11,64,256]{2,1,0:T(8,128)S(1)} %pad_maximum_fusion), channel_id=1, source_target_pairs={{0,2},{2,4},{4,6},{6,8},{8,10},{10,12},{12,14},{14,16},{16,18},{18... | collective-permute-start | bytes 2162696 | tf_op jit(solution)/shard_map/ppermute | solution.py:16
  11.1 1.3 %collective-permute-start.4 = (f32[8,64,256]{2,1,0:T(8,128)}, f32[8,64,256]{2,1,0:T(8,128)S(1)}, u32[]{:S(2)}, u32[]{:S(2)}) collective-permute-start(f32[8,64,256]{2,1,0:T(8,128)} %pad_maximum_fusion.1), channel_id=1, source_target_pairs={{2,0},{4,2},{6,4},{8,6},{10,8},{12,10},{14,12},{16,14},{18,16},{20... | collective-permute-start | bytes 1572872 | tf_op jit(solution)/shard_map/ppermute | solution.py:16
  12.4 6.3 %collective-permute-start.5 = (f32[3,64,256]{2,1,0:T(8,128)}, f32[3,64,256]{2,1,0:T(8,128)}, u32[]{:S(2)}, u32[]{:S(2)}) collective-permute-start(f32[3,64,256]{2,1,0:T(8,128)} %get-tuple-element.11), channel_id=1, source_target_pairs={{0,6},{2,8},{4,10},{6,12},{8,14},{10,16},{12,18},{14,20},{16,22},{... | collective-permute-start | bytes 589832 | tf_op jit(solution)/shard_map/ppermute | solution.py:16
  18.7 1.0 %constant_dynamic-slice_fusion.4 = (f32[16,8,256]{2,1,0:T(8,128)S(1)}, f32[16,8,256]{2,1,0:T(8,128)S(1)}) fusion(f32[16,64,256]{2,1,0:T(8,128)} %eps.1, s32[]{:T(128)S(6)} %select_n.47, f32[16,64,256]{2,1,0:T(8,128)} %phi.1), kind=kLoop, calls=%fused_computation.16 | loop fusion | bytes 524292 | tf_op jit(solution)/shard_map/dynamic_slice | solution.py:23
  20.1 0.9 constant_dynamic-slice_fusion.3
  21.1 1.6 %collective-permute-start.1 = (f32[50,8,256]{2,1,0:T(8,128)S(1)}, f32[50,8,256]{2,1,0:T(8,128)S(1)}, u32[]{:S(2)}, u32[]{:S(2)}) collective-permute-start(f32[50,8,256]{2,1,0:T(8,128)S(1)} %pad_maximum_fusion.2), channel_id=1, source_target_pairs={{0,1},{1,0},{2,3},{3,2},{4,5},{5,4},{6,7},{7,6},{8,9},{9,8},{10,11... | collective-permute-start | bytes 1228808 | tf_op jit(solution)/shard_map/ppermute | solution.py:31
  22.7 16.5 %collective-permute-done.5.far = f32[3,64,256]{2,1,0:T(8,128)} collective-permute-done((f32[3,64,256]{2,1,0:T(8,128)}, f32[3,64,256]{2,1,0:T(8,128)}, u32[]{:S(2)}, u32[]{:S(2)}) %collective-permute-start.5) | collective-permute-done | bytes 196640 | tf_op jit(solution)/shard_map/ppermute | solution.py:16
  40.0 1.6 %collective-permute-start.6 = (f32[22,8,256]{2,1,0:T(8,128)S(1)}, f32[22,8,256]{2,1,0:T(8,128)S(1)}, u32[]{:S(2)}, u32[]{:S(2)}) collective-permute-start(f32[22,8,256]{2,1,0:T(8,128)S(1)} %pad_maximum_fusion.3), channel_id=1, source_target_pairs={{0,1},{1,0},{2,3},{3,2},{4,5},{5,4},{6,7},{7,6},{8,9},{9,8},{10,11... | collective-permute-start | bytes 540680 | tf_op jit(solution)/shard_map/ppermute | solution.py:31
  41.6 8.0 %collective-permute-start.2 = (f32[16,8,256]{2,1,0:T(8,128)S(1)}, f32[16,8,256]{2,1,0:T(8,128)S(1)}, u32[]{:S(2)}, u32[]{:S(2)}) collective-permute-start(f32[16,8,256]{2,1,0:T(8,128)S(1)} %slice.28), channel_id=1, source_target_pairs={{0,4},{2,6},{4,8},{6,10},{8,12},{10,14},{12,16},{14,18},{16,20},{1... | collective-permute-start | bytes 393224 | tf_op jit(solution)/shard_map/ppermute | solution.py:16
  50.3 1.8 %collective-permute-done.2.moved_lo.moved_hi = f32[16,8,256]{2,1,0:T(8,128)S(1)} collective-permute-done((f32[16,8,256]{2,1,0:T(8,128)S(1)}, f32[16,8,256]{2,1,0:T(8,128)S(1)}, u32[]{:S(2)}, u32[]{:S(2)}) %collective-permute-start.2) | collective-permute-done | bytes 131104 | tf_op jit(solution)/shard_map/ppermute | solution.py:16
  52.8 1.0 %copy-done.1 = f32[16,64,256]{2,1,0:T(8,128)} copy-done((f32[16,64,256]{2,1,0:T(8,128)}, f32[16,64,256]{2,1,0:T(8,128)S(1)}, u32[]{:S(2)}) %copy-start.1) | copy-done | bytes 1048600
  53.8 17.5 %relax.1 = (f32[16,64,256]{2,1,0:T(8,128)}, f32[16,64,256]{2,1,0:T(8,128)}, f32[16,80,256]{2,1,0:T(8,128)}, f32[80,256]{1,0:T(8,128)}) custom-call(f32[16,64,256]{2,1,0:T(8,128)} %phi.1, f32[16,64,256]{2,1,0:T(8,128)} %eps.1, f32[16,64,256]{2,1,0:T(8,128)} %copy-done.1, f32[16,8,256]{2,1,0:T(8,128)} %copy-done.5, f32[16,8,256]{2,1,0:T(8,128)} %copy-done.5, ...), custom_call_target="tpu_custom_call" | custom-call | tf_op jit(solution)/shard_map/relax/pallas_call | solution.py:249
  71.3 1.5 %collective-permute-done.7 = f32[80,256]{1,0:T(8,128)S(1)} collective-permute-done((f32[80,256]{1,0:T(8,128)}, f32[80,256]{1,0:T(8,128)S(1)}, u32[]{:S(2)}, u32[]{:S(2)}) %collective-permute-start.7) | collective-permute-done | bytes 81952 | tf_op jit(solution)/shard_map/ppermute | solution.py:213
  72.8 0.9 add.12
  73.7 2.5 %collective-permute-start.8 = (f32[80,256]{1,0:T(8,128)S(1)}, f32[80,256]{1,0:T(8,128)S(1)}, u32[]{:S(2)}, u32[]{:S(2)}) collective-permute-start(f32[80,256]{1,0:T(8,128)S(1)} %add.12), channel_id=1, source_target_pairs={{0,4},{2,6},{4,0},{6,2},{8,12},{10,14},{12,8},{14,10},{16,20},{18,... | collective-permute-start | bytes 245768 | tf_op jit(solution)/shard_map/ppermute | solution.py:213
  76.2 2.8 %collective-permute-done.8 = f32[80,256]{1,0:T(8,128)S(1)} collective-permute-done((f32[80,256]{1,0:T(8,128)S(1)}, f32[80,256]{1,0:T(8,128)S(1)}, u32[]{:S(2)}, u32[]{:S(2)}) %collective-permute-start.8) | collective-permute-done | bytes 81952 | tf_op jit(solution)/shard_map/ppermute | solution.py:213
  79.0 2.3 %collective-permute-start.9 = (f32[80,256]{1,0:T(8,128)S(1)}, f32[80,256]{1,0:T(8,128)S(1)}, u32[]{:S(2)}, u32[]{:S(2)}) collective-permute-start(f32[80,256]{1,0:T(8,128)S(1)} %add.27), channel_id=1, source_target_pairs={{0,8},{2,10},{4,12},{6,14},{8,0},{10,2},{12,4},{14,6},{16,24},{18,... | collective-permute-start | bytes 245768 | tf_op jit(solution)/shard_map/ppermute | solution.py:213
  81.3 2.4 %collective-permute-done.9 = f32[80,256]{1,0:T(8,128)S(1)} collective-permute-done((f32[80,256]{1,0:T(8,128)S(1)}, f32[80,256]{1,0:T(8,128)S(1)}, u32[]{:S(2)}, u32[]{:S(2)}) %collective-permute-start.9) | collective-permute-done | bytes 81952 | tf_op jit(solution)/shard_map/ppermute | solution.py:213
  83.7 3.1 %collective-permute-start.10 = (f32[80,256]{1,0:T(8,128)S(1)}, f32[80,256]{1,0:T(8,128)S(1)}, u32[]{:S(2)}, u32[]{:S(2)}) collective-permute-start(f32[80,256]{1,0:T(8,128)S(1)} %add.29), channel_id=1, source_target_pairs={{0,16},{2,18},{4,20},{6,22},{8,24},{10,26},{12,28},{14,30},{16,0},... | collective-permute-start | bytes 245768 | tf_op jit(solution)/shard_map/ppermute | solution.py:213
  86.8 2.4 %collective-permute-done.10 = f32[80,256]{1,0:T(8,128)S(1)} collective-permute-done((f32[80,256]{1,0:T(8,128)S(1)}, f32[80,256]{1,0:T(8,128)S(1)}, u32[]{:S(2)}, u32[]{:S(2)}) %collective-permute-start.10) | collective-permute-done | bytes 81952 | tf_op jit(solution)/shard_map/ppermute | solution.py:213
  89.9 4.4 %integrate.1 = f32[2,16,64,256]{3,2,1,0:T(8,128)} custom-call(f32[16,80,256]{2,1,0:T(8,128)} %get-tuple-element.9.window, f32[80,256]{1,0:T(8,128)} %select_add_fusion.prefix), custom_call_target="tpu_custom_call" | custom-call | tf_op jit(solution)/shard_map/integrate/pallas_call | solution.py:266
  (40 shorter events, 4.2 us)
Async XLA Ops:
  0.6 51.5 %collective-permute-start = (f32[16,64,256]{2,1,0:T(8,128)}, f32[16,64,256]{2,1,0:T(8,128)S(1)}, u32[]{:S(2)}, u32[]{:S(2)}) collective-permute-start(f32[16,64,256]{2,1,0:T(8,128)} %param.7), channel_id=1, source_target_pairs={{0,4},{2,6},{4,8},{6,10},{8,12},{10,14},{12,16},{14,18},{16,20},{1... | collective-permute-start | bytes 3145736 | tf_op jit(solution)/shard_map/ppermute | solution.py:16
  7.3 12.4 %copy-start.8 = (s32[64,256]{1,0:T(8,128)S(1)}, s32[64,256]{1,0:T(8,128)}, u32[]{:S(2)}) copy-start(s32[64,256]{1,0:T(8,128)} %param.11) | copy-start | bytes 196612
  7.3 12.4 %copy-start.9 = (f32[16]{0:T(128)S(1)}, f32[16]{0:T(128)}, u32[]{:S(2)}) copy-start(f32[16]{0:T(128)} %param.13) | copy-start | bytes 196
  8.6 12.4 %copy-start.7 = (s32[64,256]{1,0:T(8,128)S(1)}, s32[64,256]{1,0:T(8,128)}, u32[]{:S(2)}) copy-start(s32[64,256]{1,0:T(8,128)} %param.12) | copy-start | bytes 196612
  8.6 12.4 %copy-start.6 = (f32[64,256]{1,0:T(8,128)S(1)}, f32[64,256]{1,0:T(8,128)}, u32[]{:S(2)}) copy-start(f32[64,256]{1,0:T(8,128)} %param.10) | copy-start | bytes 196612
  8.7 31.2 %collective-permute-start.3 = (f32[11,64,256]{2,1,0:T(8,128)S(1)}, f32[11,64,256]{2,1,0:T(8,128)S(1)}, u32[]{:S(2)}, u32[]{:S(2)}) collective-permute-start(f32[11,64,256]{2,1,0:T(8,128)S(1)} %pad_maximum_fusion), channel_id=1, source_target_pairs={{0,2},{2,4},{4,6},{6,8},{8,10},{10,12},{12,14},{14,16},{16,18},{18... | collective-permute-start | bytes 2162696 | tf_op jit(solution)/shard_map/ppermute | solution.py:16
  11.1 28.8 %collective-permute-start.4 = (f32[8,64,256]{2,1,0:T(8,128)}, f32[8,64,256]{2,1,0:T(8,128)S(1)}, u32[]{:S(2)}, u32[]{:S(2)}) collective-permute-start(f32[8,64,256]{2,1,0:T(8,128)} %pad_maximum_fusion.1), channel_id=1, source_target_pairs={{2,0},{4,2},{6,4},{8,6},{10,8},{12,10},{14,12},{16,14},{18,16},{20... | collective-permute-start | bytes 1572872 | tf_op jit(solution)/shard_map/ppermute | solution.py:16
  12.4 26.8 %collective-permute-start.5 = (f32[3,64,256]{2,1,0:T(8,128)}, f32[3,64,256]{2,1,0:T(8,128)}, u32[]{:S(2)}, u32[]{:S(2)}) collective-permute-start(f32[3,64,256]{2,1,0:T(8,128)} %get-tuple-element.11), channel_id=1, source_target_pairs={{0,6},{2,8},{4,10},{6,12},{8,14},{10,16},{12,18},{14,20},{16,22},{... | collective-permute-start | bytes 589832 | tf_op jit(solution)/shard_map/ppermute | solution.py:16
  21.1 20.5 %collective-permute-start.1 = (f32[50,8,256]{2,1,0:T(8,128)S(1)}, f32[50,8,256]{2,1,0:T(8,128)S(1)}, u32[]{:S(2)}, u32[]{:S(2)}) collective-permute-start(f32[50,8,256]{2,1,0:T(8,128)S(1)} %pad_maximum_fusion.2), channel_id=1, source_target_pairs={{0,1},{1,0},{2,3},{3,2},{4,5},{5,4},{6,7},{7,6},{8,9},{9,8},{10,11... | collective-permute-start | bytes 1228808 | tf_op jit(solution)/shard_map/ppermute | solution.py:31
  39.9 12.2 %copy-start.4 = (f32[8,64,256]{2,1,0:T(8,128)}, f32[8,64,256]{2,1,0:T(8,128)S(1)}, u32[]{:S(2)}) copy-start(f32[8,64,256]{2,1,0:T(8,128)S(1)} %collective-permute-done.4.above) | copy-start | bytes 1572868
  40.0 12.2 %copy-start.2 = (f32[11,64,256]{2,1,0:T(8,128)}, f32[11,64,256]{2,1,0:T(8,128)S(1)}, u32[]{:S(2)}) copy-start(f32[11,64,256]{2,1,0:T(8,128)S(1)} %collective-permute-done.3.below) | copy-start | bytes 2162692
  40.0 12.1 %collective-permute-start.6 = (f32[22,8,256]{2,1,0:T(8,128)S(1)}, f32[22,8,256]{2,1,0:T(8,128)S(1)}, u32[]{:S(2)}, u32[]{:S(2)}) collective-permute-start(f32[22,8,256]{2,1,0:T(8,128)S(1)} %pad_maximum_fusion.3), channel_id=1, source_target_pairs={{0,1},{1,0},{2,3},{3,2},{4,5},{5,4},{6,7},{7,6},{8,9},{9,8},{10,11... | collective-permute-start | bytes 540680 | tf_op jit(solution)/shard_map/ppermute | solution.py:31
  41.6 10.5 %copy-start = (f32[50,8,256]{2,1,0:T(8,128)}, f32[50,8,256]{2,1,0:T(8,128)S(1)}, u32[]{:S(2)}) copy-start(f32[50,8,256]{2,1,0:T(8,128)S(1)} %collective-permute-done.1.raw_lo.raw_hi) | copy-start | bytes 1228804
  41.6 10.5 %collective-permute-start.2 = (f32[16,8,256]{2,1,0:T(8,128)S(1)}, f32[16,8,256]{2,1,0:T(8,128)S(1)}, u32[]{:S(2)}, u32[]{:S(2)}) collective-permute-start(f32[16,8,256]{2,1,0:T(8,128)S(1)} %slice.28), channel_id=1, source_target_pairs={{0,4},{2,6},{4,8},{6,10},{8,12},{10,14},{12,16},{14,18},{16,20},{1... | collective-permute-start | bytes 393224 | tf_op jit(solution)/shard_map/ppermute | solution.py:16
  52.1 0.7 copy-start.5
  52.1 0.7 copy-start.3
  52.8 1.0 %copy-start.1 = (f32[16,64,256]{2,1,0:T(8,128)}, f32[16,64,256]{2,1,0:T(8,128)S(1)}, u32[]{:S(2)}) copy-start(f32[16,64,256]{2,1,0:T(8,128)S(1)} %collective-permute-done.moved) | copy-start | bytes 3145732
  71.3 1.5 %collective-permute-start.7 = (f32[80,256]{1,0:T(8,128)}, f32[80,256]{1,0:T(8,128)S(1)}, u32[]{:S(2)}, u32[]{:S(2)}) collective-permute-start(f32[80,256]{1,0:T(8,128)} %get-tuple-element.10), channel_id=1, source_target_pairs={{0,2},{2,0},{4,6},{6,4},{8,10},{10,8},{12,14},{14,12},{16,18},{18,... | collective-permute-start | bytes 245768 | tf_op jit(solution)/shard_map/ppermute | solution.py:213
  73.7 5.3 %collective-permute-start.8 = (f32[80,256]{1,0:T(8,128)S(1)}, f32[80,256]{1,0:T(8,128)S(1)}, u32[]{:S(2)}, u32[]{:S(2)}) collective-permute-start(f32[80,256]{1,0:T(8,128)S(1)} %add.12), channel_id=1, source_target_pairs={{0,4},{2,6},{4,0},{6,2},{8,12},{10,14},{12,8},{14,10},{16,20},{18,... | collective-permute-start | bytes 245768 | tf_op jit(solution)/shard_map/ppermute | solution.py:213
  79.0 4.7 %collective-permute-start.9 = (f32[80,256]{1,0:T(8,128)S(1)}, f32[80,256]{1,0:T(8,128)S(1)}, u32[]{:S(2)}, u32[]{:S(2)}) collective-permute-start(f32[80,256]{1,0:T(8,128)S(1)} %add.27), channel_id=1, source_target_pairs={{0,8},{2,10},{4,12},{6,14},{8,0},{10,2},{12,4},{14,6},{16,24},{18,... | collective-permute-start | bytes 245768 | tf_op jit(solution)/shard_map/ppermute | solution.py:213
  83.7 5.5 %collective-permute-start.10 = (f32[80,256]{1,0:T(8,128)S(1)}, f32[80,256]{1,0:T(8,128)S(1)}, u32[]{:S(2)}, u32[]{:S(2)}) collective-permute-start(f32[80,256]{1,0:T(8,128)S(1)} %add.29), channel_id=1, source_target_pairs={{0,16},{2,18},{4,20},{6,22},{8,24},{10,26},{12,28},{14,30},{16,0},... | collective-permute-start | bytes 245768 | tf_op jit(solution)/shard_map/ppermute | solution.py:213

commit v2 on v0

v2 whole, which is shorter than its diff:
```python
import functools

import jax
import jax.numpy as jnp
from jax import lax
from jax.experimental import pallas as pl
from jax.experimental.pallas import tpu as pltpu
from jax.sharding import PartitionSpec as P

SWEEPS = 4
ROWS = 8
F32 = jnp.float32
IN_VMEM = pl.BlockSpec(memory_space=pltpu.VMEM)
ANYWHERE = pl.BlockSpec(memory_space=pl.ANY)


def plane(*shape):
    return jax.ShapeDtypeStruct(shape, F32)


def near(*shape):
    return pltpu.VMEM(shape, F32)


def fetched(x):
    return pltpu.with_memory_space_constraint(x, pltpu.VMEM)


def shifted(block, axis, distance):
    count = lax.axis_size(axis)
    route = [(i, i + distance) for i in range(count) if 0 <= i + distance < count]
    return lax.ppermute(block, axis, route)


def transit(slab, rec, inj):
    return slab / (1.0 + rec * slab) + inj


def drift_charge(ions, rec, inj, slab):
    once = transit(ions, rec, inj)
    return transit(jnp.where(slab >= 1, once, 0.0), rec, inj)


def roll(x, amount, axis):
    return pltpu.roll(x, amount % x.shape[axis], axis)


def row_tiles(load, tiles, sub):
    x = [load(slice(t * ROWS, (t + 1) * ROWS)) for t in range(tiles)]
    up = [roll(v, -1, 0) for v in x]
    down = [roll(v, 1, 0) for v in x]
    for t in range(tiles):
        higher = jnp.where(sub == ROWS - 1, up[(t + 1) % tiles], up[t])
        lower = jnp.where(sub == 0, down[(t - 1) % tiles], down[t])
        yield t, slice(t * ROWS, (t + 1) * ROWS), x[t], higher, lower


def run_all(copies, sems):
    running = [pltpu.make_async_copy(src, dst, sems.at[k]) for k, (src, dst) in enumerate(copies)]
    for copy in running:
        copy.start()
    return running


def sides_of(count, band):
    if count == 1:
        return [pl.multiple_of(jnp.where(lax.axis_index("radius") == 0, band - ROWS, 0), ROWS)]
    return [band - ROWS, 0]


def rows_kernel(phi, eps, ions, rec, index, gap, table, *rest):
    blocks, pads, sems = rest[:-2], rest[-2], rest[-1]
    layers, band, sector = phi.shape
    starts = sides_of(len(blocks), band)
    copies = []
    for start, block in zip(starts, blocks):
        for k, src in enumerate((phi, eps, ions)):
            copies.append((src.at[:, pl.ds(start, ROWS)], block.at[k * layers : (k + 1) * layers]))
    running = run_all(copies, sems)
    for t in range(band // ROWS):
        at = slice(t * ROWS, (t + 1) * ROWS)
        which = index[at]
        picked = jnp.zeros((ROWS, sector), F32)
        for k in range(table.shape[0]):
            picked = jnp.where(which == k, table[k], picked)
        pads[0, at] = rec[at]
        pads[1, at] = picked * (1 - gap[at]).astype(F32)
    for start, block in zip(starts, blocks):
        for k in range(2):
            block[3 * layers + k] = pads[k, pl.ds(start, ROWS)]
    for copy in running:
        copy.wait()


def halo_kernel(sides, phi, eps, ions, *refs):
    raws, (up, down, far, sems) = refs[:sides], refs[sides:]
    layers, band, _ = phi.shape
    depth = SWEEPS
    copies = []
    for dst, at, k, start, count in (
        (up, 0, 0, layers - depth, depth),
        (up, depth, 1, layers - depth, depth),
        (up, 2 * depth, 2, 0, depth - 1),
        (down, 0, 0, 0, depth),
        (down, depth, 1, 0, depth),
        (far, 0, 2, layers - depth + 1, depth - 1),
    ):
        src = (phi, eps, ions)[k]
        copies.append((src.at[start : start + count], dst.at[at : at + count, 0:band]))
        for side, raw in enumerate(raws):
            rows = slice(band + side * ROWS, band + (side + 1) * ROWS)
            first = k * layers + start
            copies.append((raw.at[first : first + count], dst.at[at : at + count, rows]))
    for copy in run_all(copies, sems):
        copy.wait()


class Window:
    def __init__(self, sides, band):
        r, bands = lax.axis_index("radius"), lax.axis_size("radius")
        self.band, self.rows = band, band + 2 * ROWS
        self.own = slice(ROWS, ROWS + band)
        self.ends = (
            (slice(0, ROWS), 0, r > 0),
            (slice(ROWS + band, self.rows), sides - 1, r < bands - 1),
        )

    def pieces(self, own, outer):
        yield self.own, own()
        for at, side, has in self.ends:
            yield at, jnp.where(has, outer(side), 0.0)

    def of_halo(self, ref, index):
        band = self.band
        return self.pieces(
            lambda: ref[index, 0:band],
            lambda side: ref[index, band + side * ROWS : band + (side + 1) * ROWS],
        )


def coupling_rows(z, ex, z_up, z_down, geo, alive, tiles, sub, put):
    for t, at, e, e_up, e_down in row_tiles(lambda s: ex(z, s), tiles, sub):
        not_last, not_first = geo[4, at], geo[5, at]
        right, left = roll(e, -1, 1), roll(e, 1, 1)
        inv_r2 = geo[2, at]
        zu = e + ex(z_up, at)
        zd = e + ex(z_down, at)
        ru = (e + e_up) * geo[0, at]
        rd = (e + e_down) * geo[1, at]
        au = (e + right * not_last) * inv_r2
        ad = (e + left * not_first) * inv_r2
        diag = ((zu + zd) + (ru + rd)) + (au + ad)
        inv = jnp.where(geo[3, at] * alive > 0, 1.0 / diag, 0.0)
        put(at, (zu * inv, zd * inv, ru * inv, rd * inv, au * inv * not_last, ad * inv * not_first), inv + inv)


def inner_coupling_kernel(sides, phi, eps, pads, *refs):
    raws, (p0, ex, w, inv2, geo) = refs[:sides], refs[sides:]
    layers, band, sector = phi.shape
    win = Window(sides, band)
    rows, tiles = win.rows, win.rows // ROWS
    r, bands = lax.axis_index("radius"), lax.axis_size("radius")
    total_r = band * bands
    sub = lax.broadcasted_iota(jnp.int32, (ROWS, sector), 0)

    row = lax.broadcasted_iota(jnp.int32, (rows, sector), 0) - ROWS + r * band
    lane = lax.broadcasted_iota(jnp.int32, (rows, sector), 1)
    rpos = ((total_r + row).astype(F32) + 0.5) / total_r
    half = 0.5 / total_r
    geo[0] = (rpos + half) / rpos
    geo[1] = (rpos - half) / rpos
    geo[2] = 1.0 / (rpos * rpos)
    geo[3] = jnp.where((row >= 0) & (row < total_r), 1.0, 0.0)
    geo[4] = jnp.where(lane == sector - 1, 0.0, 1.0)
    geo[5] = jnp.where(lane == 0, 0.0, 1.0)
    for k in range(2):
        for at, value in win.pieces(lambda k=k: pads[k], lambda side, k=k: raws[side][3 * layers + k]):
            geo[6 + k, at] = value

    @pl.loop(0, layers)
    def _(z):
        for dst, src, base in ((p0, phi, 0), (ex, eps, layers)):
            for at, value in win.pieces(lambda: src[z], lambda side: raws[side][base + z]):
                dst[z, at] = value

    @pl.loop(1, layers - 1)
    def _(z):
        def put(at, values, twice):
            for k, value in enumerate(values):
                w[k, z, at] = value
            inv2[z, at] = twice

        coupling_rows(z, lambda i, s: ex[i, s], z + 1, z - 1, geo, 1.0, tiles, sub, put)


def sweep_layer(src, src_up, src_down, w, b, tiles, sub, put):
    for t, at, p, p_up, p_down in row_tiles(src, tiles, sub):
        right, left = roll(p, -1, 1), roll(p, 1, 1)
        total = b(at) + (w(0, at) * src_up(at) + w(1, at) * src_down(at))
        total = total + (w(2, at) * p_up + w(3, at) * p_down)
        total = total + (w(4, at) * right + w(5, at) * left)
        put(at, total)


def inner_relax_kernel(sides, moved, p0, w, inv2, geo, *refs):
    rows_moved = refs[:sides]
    charge_out, window_out, sums_out, state, b_out, p1, p2, p3, b = refs[sides:]
    layers, band, sector = moved.shape
    depth = SWEEPS
    win = Window(sides, band)
    tiles = win.rows // ROWS
    d = lax.axis_index("drift")
    sub = lax.broadcasted_iota(jnp.int32, (ROWS, sector), 0)
    phis = (p0, p1, p2, p3)

    @pl.loop(0, layers)
    def _(z):
        inner = (z > 0) & (z < layers - 1)
        for at, ions in win.pieces(lambda: moved[z], lambda side: rows_moved[side][z]):
            value = drift_charge(ions, geo[6, at], geo[7, at], d)
            if at is win.own:
                charge_out[z] = value
            b[z, at] = jnp.where(inner, value * inv2[z, at], value)

    sums_out[...] = jnp.zeros_like(sums_out)
    for s in range(1, depth + 1):
        src = phis[s - 1]

        @pl.loop(s, layers - s)
        def _(z, s=s, src=src):
            def put(at, total):
                if s < depth:
                    phis[s][z, at] = total
                else:
                    window_out[z - depth, at] = total
                    sums_out[at] += total

            sweep_layer(
                lambda at: src[z, at],
                lambda at: src[z + 1, at],
                lambda at: src[z - 1, at],
                lambda k, at: w[k, z, at],
                lambda at: b[z, at],
                tiles,
                sub,
                put,
            )

    for s in range(1, depth):
        for k in range(2):
            state[0, s - 1, k] = phis[s][s + k]
            state[1, s - 1, k] = phis[s][layers - s - 2 + k]
    for k in range(depth):
        b_out[0, k] = b[k]
        b_out[1, k] = b[layers - depth + k]


def outer_relax_kernel(sides, below, above, far, p0, ex, w, geo, state, b_in, sums_in, *refs):
    low_out, high_out, sums_out, ph, eh, wb, bb, q = refs
    layers, rows, sector = p0.shape
    depth, n = SWEEPS, layers
    zs = n + 2 * depth
    band = rows - 2 * ROWS
    win = Window(sides, band)
    tiles = rows // ROWS
    d, drifts = lax.axis_index("drift"), lax.axis_size("drift")
    sub = lax.broadcasted_iota(jnp.int32, (ROWS, sector), 0)

    for k in range(depth):
        for ref, dst in ((below, 0), (above, 1)):
            for at, value in win.of_halo(ref, k):
                ph[dst, k, at] = value
            for at, value in win.of_halo(ref, depth + k):
                eh[dst, k if dst == 0 else 2 + k, at] = value
    for k in range(2):
        eh[0, depth + k] = ex[k]
        eh[1, k] = ex[n - 2 + k]

    for k in range(depth - 1):
        for side, at_layer, ref, index, slab in ((0, k, far, k, d - 1), (1, k + 1, below, 2 * depth + k, d + 1)):
            for at, ions in win.of_halo(ref, index):
                bb[side, at_layer, at] = drift_charge(ions, geo[6, at], geo[7, at], slab)
    bb[0, depth - 1] = b_in[0, 0]
    bb[1, 0] = b_in[1, depth - 1]
    for side in range(2):

        @pl.loop(0, depth)
        def _(k, side=side):
            zg = d * n - depth + (k + 1 if side == 0 else depth + n - 1 + k)
            alive = jnp.where((zg >= 0) & (zg < drifts * n), 1.0, 0.0)

            def put(at, values, twice):
                for j, value in enumerate(values):
                    wb[j, side, k, at] = value
                bb[side, k, at] = bb[side, k, at] * twice

            coupling_rows(k + 1, lambda i, s: eh[side, i, s], k + 2, k, geo, alive, tiles, sub, put)

    def phi_at(s, e):
        if s == 0:
            if e < depth:
                return lambda at: ph[0, e, at]
            if e >= depth + n:
                return lambda at: ph[1, e - depth - n, at]
            return lambda at: p0[e - depth, at]
        z = e - depth
        if s <= z < n - s:
            if z < n // 2:
                return lambda at: state[0, s - 1, z - s, at]
            return lambda at: state[1, s - 1, z - (n - s - 2), at]
        side = 0 if e < zs // 2 else 1
        return lambda at: q[s - 1, side, (e - s) if side == 0 else e - (zs - s - depth), at]

    sums_out[...] = sums_in[...]
    for s in range(1, depth + 1):
        for side in range(2):
            for k in range(depth):
                e = s + k if side == 0 else zs - s - depth + k
                z = e - depth
                if 0 < z < n - 1:
                    w_at = lambda j, at, z=z: w[j, z, at]
                    b_at = lambda at, z=z: b_in[0, z, at] if z < n // 2 else b_in[1, z - (n - depth), at]
                else:
                    at_layer = e - 1 if side == 0 else e - (zs - depth - 1)
                    w_at = lambda j, at, side=side, i=at_layer: wb[j, side, i, at]
                    b_at = lambda at, side=side, i=at_layer: bb[side, i, at]

                def put(at, total, s=s, side=side, k=k):
                    if s < depth:
                        q[s - 1, side, k, at] = total
                    else:
                        (low_out, high_out)[side][k, at] = total
                        sums_out[at] += total

                sweep_layer(phi_at(s - 1, e), phi_at(s - 1, e + 1), phi_at(s - 1, e - 1), w_at, b_at, tiles, sub, put)


def local_kernel(low, inner, high, potential, out, run):
    _, band, _ = potential.shape
    rows = band + 2 * ROWS
    tiles = rows // ROWS
    run[...] = jnp.zeros_like(run)
    base = 0
    for window in (low, inner, high):

        @pl.loop(0, window.shape[0])
        def _(k, window=window, base=base):
            for t in range(tiles):
                at = slice(t * ROWS, (t + 1) * ROWS)
                value = window[k, at]
                run[at] += value
                if 0 < t < tiles - 1:
                    potential[base + k, (t - 1) * ROWS : t * ROWS] = value

            def put(at, first, second):
                out[0, base + k, at] = first
                out[1, base + k, at] = second

            ratios_of(run, put)

        base += window.shape[0]


def ratios_of(field, put):
    rows, sector = field.shape
    band = rows - 2 * ROWS
    r, bands = lax.axis_index("radius"), lax.axis_size("radius")
    total_r = band * bands
    tiles = rows // ROWS
    sub = lax.broadcasted_iota(jnp.int32, (ROWS, sector), 0)
    lane = lax.broadcasted_iota(jnp.int32, (ROWS, sector), 1)
    scale = 1.0 / (8.0 * 1.09)
    for t, at, x, higher, lower in row_tiles(lambda s: field[s], tiles, sub):
        if 0 < t < tiles - 1:
            row = sub + ((t - 1) * ROWS + r * band)
            rpos = ((total_r + row).astype(F32) + 0.5) / total_r
            right = jnp.where(lane == sector - 1, 0.0, roll(x, -1, 1))
            left = jnp.where(lane == 0, 0.0, roll(x, 1, 1))
            er = (lower - higher) * (0.5 * scale)
            ea = (left - right) * (0.5 * scale / rpos)
            put(slice((t - 1) * ROWS, t * ROWS), er + 0.3 * ea, ea - 0.3 * er)


def offset_kernel(local, prefix, out, shift, stage, sems):
    layers = local.shape[1]
    copies = []

    def put(at, first, second):
        shift[0, at] = first
        shift[1, at] = second

    ratios_of(prefix, put)
    parts = sems.shape[0]
    each = layers // parts
    for k in range(parts):
        for c in range(2):
            stage[c, k * each : (k + 1) * each] = local[c, k * each : (k + 1) * each] + shift[c]
        copy = pltpu.make_async_copy(
            stage.at[:, k * each : (k + 1) * each], out.at[:, k * each : (k + 1) * each], sems.at[k]
        )
        copy.start()
        copies.append(copy)
    for copy in copies:
        copy.wait()


def sums_below(sums):
    count, mine = lax.axis_size("drift"), lax.axis_index("drift")
    assert count & (count - 1) == 0
    total, below, step = sums, jnp.zeros_like(sums), 1
    while step < count:
        other = lax.ppermute(total, "drift", [(i, i ^ step) for i in range(count)])
        below = below + jnp.where((mine & step) > 0, other, 0.0)
        total = total + other
        step *= 2
    return below


def kernel(function, out_shape, in_specs, out_specs=None, scratch=(), mb=16):
    return pl.pallas_call(
        function,
        out_shape=out_shape,
        in_specs=in_specs,
        out_specs=out_specs if out_specs is not None else [IN_VMEM] * len(out_shape),
        scratch_shapes=list(scratch),
        compiler_params=pltpu.CompilerParams(vmem_limit_bytes=mb << 20),
    )


def body(ions, potential_guess, permittivity, recombination, rate_index, gap_mask, rate_table):
    layers, band, sector = ions.shape
    rows = band + 2 * ROWS
    depth = SWEEPS
    sides = 1 if lax.axis_size("radius") == 2 else 2
    sent = band + sides * ROWS
    dma = pltpu.SemaphoreType.DMA
    phi, eps, ions_far = [
        pltpu.with_memory_space_constraint(x, pltpu.HBM) for x in (potential_guess, permittivity, ions)
    ]

    moved = shifted(ions, "drift", 2)
    *blocks, pads = kernel(
        rows_kernel,
        [plane(3 * layers + 2, ROWS, sector)] * sides + [plane(2, band, sector)],
        [ANYWHERE] * 3 + [IN_VMEM] * 3 + [pl.BlockSpec(memory_space=pltpu.SMEM)],
        scratch=[dma((3 * sides,))],
        mb=4,
    )(phi, eps, ions_far, recombination, rate_index, gap_mask, rate_table)
    if sides == 1:
        raws = [lax.ppermute(blocks[0], "radius", [(0, 1), (1, 0)])]
    else:
        raws = [shifted(blocks[0], "radius", 1), shifted(blocks[1], "radius", -1)]
    up, down, beyond = kernel(
        functools.partial(halo_kernel, sides),
        [plane(3 * depth - 1, sent, sector), plane(2 * depth, sent, sector), plane(depth - 1, sent, sector)],
        [ANYWHERE] * 3 + [IN_VMEM] * sides,
        scratch=[dma((6 * (1 + sides),))],
        mb=6,
    )(phi, eps, ions_far, *raws)
    rows_moved = [shifted(raw[2 * layers : 3 * layers], "drift", 2) for raw in raws]
    below = shifted(up, "drift", 1)
    above = shifted(down, "drift", -1)
    far = shifted(beyond, "drift", 3)

    box = plane(layers, rows, sector)
    p0, ex, w, inv2, geo = kernel(
        functools.partial(inner_coupling_kernel, sides),
        [box, box, plane(6, layers, rows, sector), box, plane(8, rows, sector)],
        [IN_VMEM] * (3 + sides),
        mb=20,
    )(potential_guess, permittivity, pads, *raws)
    p0, ex, w, inv2, geo = [fetched(x) for x in (p0, ex, w, inv2, geo)]
    charge, inner, sums, state, b = kernel(
        functools.partial(inner_relax_kernel, sides),
        [
            plane(layers, band, sector),
            plane(layers - 2 * depth, rows, sector),
            plane(rows, sector),
            plane(2, depth - 1, 2, rows, sector),
            plane(2, depth, rows, sector),
        ],
        [IN_VMEM] * (5 + sides),
        scratch=[near(layers, rows, sector)] * 4,
        mb=16,
    )(moved, p0, w, inv2, geo, *rows_moved)
    low, high, sums = kernel(
        functools.partial(outer_relax_kernel, sides),
        [plane(depth, rows, sector), plane(depth, rows, sector), plane(rows, sector)],
        [IN_VMEM] * 10,
        scratch=[
            near(2, depth, rows, sector),
            near(2, depth + 2, rows, sector),
            near(6, 2, depth, rows, sector),
            near(2, depth, rows, sector),
            near(depth - 1, 2, depth, rows, sector),
        ],
        mb=16,
    )(below, above, far, p0, ex, w, geo, fetched(state), fetched(b), fetched(sums))
    potential, local = kernel(
        local_kernel,
        [plane(layers, band, sector), plane(2, layers, band, sector)],
        [IN_VMEM] * 3,
        scratch=[near(rows, sector)],
        mb=16,
    )(low, inner, high)
    below_sums = sums_below(sums)
    distortion = kernel(
        offset_kernel,
        plane(2, layers, band, sector),
        [IN_VMEM] * 2,
        ANYWHERE,
        [near(2, band, sector), near(2, layers, band, sector), dma((4,))],
        mb=12,
    )(fetched(local), below_sums)
    return charge, potential, distortion


def solution(mesh):
    return jax.shard_map(
        body,
        mesh=mesh,
        in_specs=(
            P("drift", "radius", None),
            P("drift", "radius", None),
            P("drift", "radius", None),
            P("radius", None),
            P("radius", None),
            P("radius", None),
            P(),
        ),
        out_specs=(
            P("drift", "radius", None),
            P("drift", "radius", None),
            P(None, "drift", "radius", None),
        ),
        check_vma=False,
    )
```

time: 175 us -> 82.6 us (0.47)
  waiting for transfers between devices: 69.6 us -> 28.3 us
  other arithmetic: 41.1 us -> 0.06 us
  Pallas kernels: 0 us -> 19.5 us
  starting transfers between devices: 45.4 us -> 30.3 us
  between operations: 14.3 us -> 0.78 us
    all_gather x1 -> x0, waiting for transfers between devices: 58.1 us -> none  [prefix(): pieces = lax.all_gather(value, axis)]
    pallas_call x0 -> x7, Pallas kernels: none -> 19.5 us  [the longest x1 6.72 us: body(): kernel(functools.partial(inner_relax_kernel, sides), [plane(layers, band,...]
    ppermute x8 -> x10, waiting for transfers between devices: 11.4 us -> 28.3 us  [the longest x5 15.4 us: shifted(): return lax.ppermute(block, axis, route)]
    mul x9 -> x0, other arithmetic: 16.6 us -> none  [the longest x4 15.4 us: relax(): return (rho_x[1:-1, 1:-1] + total) / safe * inner]
    ppermute x8 -> x10, starting transfers between devices: 45.4 us -> 30.3 us  [the longest x5 15.6 us: shifted(): return lax.ppermute(block, axis, route)]
    select_n x15 -> x0, other arithmetic: 14.3 us -> none  [lap(): return jnp.where(position < mine, longer, total)]
    add x3 -> x4, other arithmetic: 3.73 us -> 0.06 us  [the longest x3 0.04 us: sums_below(): total = total + other]
    concatenate x1 -> x0, other arithmetic: 2.23 us -> none  [with_halo(): jnp.concatenate([lax.ppermute(tail, axis, [(i, (i + 1) % count) for i in...]
  transfers between devices with their start and end apart: 9 -> 10, of which waited for: 8 -> 6; matrix products, arithmetic and copies ran while one was open for 2% -> 0% of each run, Pallas kernels for 0% -> 16%
where the time goes in v2:
time: 82.6 us; the launch traced here: 82.1 us
  starting transfers between devices  30.3 us (37%)
  waiting for transfers between devices  28.3 us (34%)
  Pallas kernels  19.5 us (24%)
  local copies, waits for them, and re-layouts  3.19 us (4%)
    ppermute x5, starting transfers between devices, shifted(): return lax.ppermute(block, axis, route)  15.6 us
    ppermute x5, waiting for transfers between devices, shifted(): return lax.ppermute(block, axis, route)  15.4 us
    ppermute x4, starting transfers between devices, sums_below(): other = lax.ppermute(total, 'drift', [(i, i ^ step) for i in range(count)])  11.6 us
    ppermute x4, waiting for transfers between devices, sums_below(): other = lax.ppermute(total, 'drift', [(i, i ^ step) for i in range(count)])  6.88 us
    pallas_call x1, Pallas kernels, body(): kernel(functools.partial(inner_relax_kernel, sides), [plane(layers, band,...  6.72 us
    ppermute x1, waiting for transfers between devices, body(): raws = [lax.ppermute(blocks[0], 'radius', [(0, 1), (1, 0)])]  6 us
    pallas_call x1, Pallas kernels, body(): kernel(functools.partial(outer_relax_kernel, sides), [plane(depth, rows,...  3.31 us
    unnamed x14, local copies, waits for them, and re-layouts  3.18 us
  transfers between devices with their start and end apart: 10, of which 6 were waited for; matrix products, arithmetic and copies ran while one was open for 0% of the time, Pallas kernels for 16%

profile of v2, /device:TPU:0, one launch (start us, length us, event | category | flops | bytes accessed | tf_op | source)
XLA Modules:
  0.0 82.1 jit_solution(17981438721651733655)
XLA Ops:
  1.5 0.8 %copy-done.3 = s32[64,256]{1,0:T(8,128)S(1)} copy-done((s32[64,256]{1,0:T(8,128)S(1)}, s32[64,256]{1,0:T(8,128)}, u32[]{:S(2)}) %copy-start.3) | copy-done | bytes 65560
  2.3 0.8 %copy-done.4 = s32[64,256]{1,0:T(8,128)S(1)} copy-done((s32[64,256]{1,0:T(8,128)S(1)}, s32[64,256]{1,0:T(8,128)}, u32[]{:S(2)}) %copy-start.4) | copy-done | bytes 65560
  3.8 1.6 %shard_map.94 = (f32[50,8,256]{2,1,0:T(8,128)S(1)}, f32[2,64,256]{2,1,0:T(8,128)S(1)}) custom-call(f32[16,64,256]{2,1,0:T(8,128)} %phi.5, f32[16,64,256]{2,1,0:T(8,128)} %eps.5, f32[16,64,256]{2,1,0:T(8,128)} %ions.3, f32[64,256]{1,0:T(8,128)S(1)} %copy-done.2, s32[64,256]{1,0:T(8,128)S(1)} %copy-done.3, s32[64,256]{1,0:T(8,128)S(1)} %copy-done.4, ...), custom_call_target="tpu_custom_call" | custom-call | tf_op jit(solution)/shard_map/pallas_call | solution.py:442
  5.4 3.1 %collective-permute-start.1 = (f32[50,8,256]{2,1,0:T(8,128)S(1)}, f32[50,8,256]{2,1,0:T(8,128)S(1)}, u32[]{:S(2)}, u32[]{:S(2)}) collective-permute-start(f32[50,8,256]{2,1,0:T(8,128)S(1)} %get-tuple-element.24), channel_id=1, source_target_pairs={{0,1},{1,0},{2,3},{3,2},{4,5},{5,4},{6,7},{7,6},{8,9},{9,8},{10,11... | collective-permute-start | bytes 1228808 | tf_op jit(solution)/shard_map/ppermute | solution.py:450
  8.5 3.5 %collective-permute-start = (f32[16,64,256]{2,1,0:T(8,128)S(1)}, f32[16,64,256]{2,1,0:T(8,128)S(1)}, u32[]{:S(2)}, u32[]{:S(2)}) collective-permute-start(f32[16,64,256]{2,1,0:T(8,128)S(1)} %copy-done.6), channel_id=1, source_target_pairs={{0,4},{2,6},{4,8},{6,10},{8,12},{10,14},{12,16},{14,18},{16,20},{1... | collective-permute-start | bytes 3145736 | tf_op jit(solution)/shard_map/ppermute | solution.py:32
  12.0 6.0 %collective-permute-done.1.refs_0_ = f32[50,8,256]{2,1,0:T(8,128)S(1)} collective-permute-done((f32[50,8,256]{2,1,0:T(8,128)S(1)}, f32[50,8,256]{2,1,0:T(8,128)S(1)}, u32[]{:S(2)}, u32[]{:S(2)}) %collective-permute-start.1) | collective-permute-done | bytes 409632 | tf_op jit(solution)/shard_map/ppermute | solution.py:450
  18.0 1.4 %shard_map.97 = (f32[11,72,256]{2,1,0:T(8,128)S(1)}, f32[8,72,256]{2,1,0:T(8,128)S(1)}, f32[3,72,256]{2,1,0:T(8,128)S(1)}) custom-call(f32[16,64,256]{2,1,0:T(8,128)} %phi.5, f32[16,64,256]{2,1,0:T(8,128)} %eps.5, f32[16,64,256]{2,1,0:T(8,128)} %ions.3, f32[50,8,256]{2,1,0:T(8,128)S(1)} %collective-permute-done.1.refs_0_), custom_call_target="tpu_custom_call" | custom-call | tf_op jit(solution)/shard_map/pallas_call | solution.py:453
  19.4 1.3 %collective-permute-start.3 = (f32[11,72,256]{2,1,0:T(8,128)S(1)}, f32[11,72,256]{2,1,0:T(8,128)S(1)}, u32[]{:S(2)}, u32[]{:S(2)}) collective-permute-start(f32[11,72,256]{2,1,0:T(8,128)S(1)} %get-tuple-element.30), channel_id=1, source_target_pairs={{0,2},{2,4},{4,6},{6,8},{8,10},{10,12},{12,14},{14,16},{16,18},{18... | collective-permute-start | bytes 2433032 | tf_op jit(solution)/shard_map/ppermute | solution.py:32
  20.7 1.3 %collective-permute-start.4 = (f32[8,72,256]{2,1,0:T(8,128)S(1)}, f32[8,72,256]{2,1,0:T(8,128)S(1)}, u32[]{:S(2)}, u32[]{:S(2)}) collective-permute-start(f32[8,72,256]{2,1,0:T(8,128)S(1)} %get-tuple-element.31), channel_id=1, source_target_pairs={{2,0},{4,2},{6,4},{8,6},{10,8},{12,10},{14,12},{16,14},{18,16},{20... | collective-permute-start | bytes 1769480 | tf_op jit(solution)/shard_map/ppermute | solution.py:32
  22.0 6.1 %collective-permute-start.5 = (f32[3,72,256]{2,1,0:T(8,128)S(1)}, f32[3,72,256]{2,1,0:T(8,128)S(1)}, u32[]{:S(2)}, u32[]{:S(2)}) collective-permute-start(f32[3,72,256]{2,1,0:T(8,128)S(1)} %get-tuple-element.32), channel_id=1, source_target_pairs={{0,6},{2,8},{4,10},{6,12},{8,14},{10,16},{12,18},{14,20},{16,22},{... | collective-permute-start | bytes 663560 | tf_op jit(solution)/shard_map/ppermute | solution.py:32
  28.2 3.4 %collective-permute-start.2 = (f32[16,8,256]{2,1,0:T(8,128)S(1)}, f32[16,8,256]{2,1,0:T(8,128)S(1)}, u32[]{:S(2)}, u32[]{:S(2)}) collective-permute-start(f32[16,8,256]{2,1,0:T(8,128)S(1)} %slice.4), channel_id=1, source_target_pairs={{0,4},{2,6},{4,8},{6,10},{8,12},{10,14},{12,16},{14,18},{16,20},{1... | collective-permute-start | bytes 393224 | tf_op jit(solution)/shard_map/ppermute | solution.py:32
  31.6 2.3 %shard_map.95 = (f32[16,80,256]{2,1,0:T(8,128)S(1)}, f32[16,80,256]{2,1,0:T(8,128)S(1)}, f32[6,16,80,256]{3,2,1,0:T(8,128)S(1)}, f32[16,80,256]{2,1,0:T(8,128)S(1)}, f32[8,80,256]{2,1,0:T(8,128)S(1)}) custom-call(f32[16,64,256]{2,1,0:T(8,128)S(1)} %copy-done, f32[16,64,256]{2,1,0:T(8,128)S(1)} %copy-done.1, f32[2,64,256]{2,1,0:T(8,128)S(1)} %get-tuple-element.23.pads, ...), custom_call_target="tpu_custom_call" | custom-call | tf_op jit(solution)/shard_map/pallas_call | solution.py:466
  33.9 15.4 %collective-permute-done.2.refs_0_ = f32[16,8,256]{2,1,0:T(8,128)S(1)} collective-permute-done((f32[16,8,256]{2,1,0:T(8,128)S(1)}, f32[16,8,256]{2,1,0:T(8,128)S(1)}, u32[]{:S(2)}, u32[]{:S(2)}) %collective-permute-start.2) | collective-permute-done | bytes 131104 | tf_op jit(solution)/shard_map/ppermute | solution.py:32
  49.3 6.7 %shard_map.96 = (f32[16,64,256]{2,1,0:T(8,128)}, f32[8,80,256]{2,1,0:T(8,128)S(1)}, f32[80,256]{1,0:T(8,128)S(1)}, f32[2,3,2,80,256]{4,3,2,1,0:T(8,128)S(1)}, f32[2,4,80,256]{3,2,1,0:T(8,128)S(1)}) custom-call(f32[16,64,256]{2,1,0:T(8,128)S(1)} %collective-permute-done.moved, f32[16,80,256]{2,1,0:T(8,128)S(1)} %get-tuple-element.25.p0, ...), custom_call_target="tpu_custom_call" | custom-call | tf_op jit(solution)/shard_map/pallas_call | solution.py:473
  56.0 3.3 %shard_map.98 = (f32[4,80,256]{2,1,0:T(8,128)S(1)}, f32[4,80,256]{2,1,0:T(8,128)S(1)}, f32[80,256]{1,0:T(8,128)S(1)}) custom-call(f32[11,72,256]{2,1,0:T(8,128)S(1)} %collective-permute-done.3.below, f32[8,72,256]{2,1,0:T(8,128)S(1)} %collective-permute-done.4.above, f32[3,72,256]{2,1,0:T(8,128)S(1)} %collective-permute-done.5.far, ...), custom_call_target="tpu_custom_call" | custom-call | tf_op jit(solution)/shard_map/pallas_call | solution.py:486
  59.4 5.1 %collective-permute-start.6 = (f32[80,256]{1,0:T(8,128)S(1)}, f32[80,256]{1,0:T(8,128)S(1)}, u32[]{:S(2)}, u32[]{:S(2)}) collective-permute-start(f32[80,256]{1,0:T(8,128)S(1)} %get-tuple-element.42), channel_id=1, source_target_pairs={{0,2},{2,0},{4,6},{6,4},{8,10},{10,8},{12,14},{14,12},{16,18},{18,... | collective-permute-start | bytes 245768 | tf_op jit(solution)/shard_map/ppermute | solution.py:412
  64.4 0.9 %collective-permute-done.6 = f32[80,256]{1,0:T(8,128)S(1)} collective-permute-done((f32[80,256]{1,0:T(8,128)S(1)}, f32[80,256]{1,0:T(8,128)S(1)}, u32[]{:S(2)}, u32[]{:S(2)}) %collective-permute-start.6) | collective-permute-done | bytes 81952 | tf_op jit(solution)/shard_map/ppermute | solution.py:412
  65.4 2.3 %collective-permute-start.7 = (f32[80,256]{1,0:T(8,128)S(1)}, f32[80,256]{1,0:T(8,128)S(1)}, u32[]{:S(2)}, u32[]{:S(2)}) collective-permute-start(f32[80,256]{1,0:T(8,128)S(1)} %add.18), channel_id=1, source_target_pairs={{0,4},{2,6},{4,0},{6,2},{8,12},{10,14},{12,8},{14,10},{16,20},{18,... | collective-permute-start | bytes 245768 | tf_op jit(solution)/shard_map/ppermute | solution.py:412
  67.6 3.0 %collective-permute-done.7 = f32[80,256]{1,0:T(8,128)S(1)} collective-permute-done((f32[80,256]{1,0:T(8,128)S(1)}, f32[80,256]{1,0:T(8,128)S(1)}, u32[]{:S(2)}, u32[]{:S(2)}) %collective-permute-start.7) | collective-permute-done | bytes 81952 | tf_op jit(solution)/shard_map/ppermute | solution.py:412
  70.6 1.6 %collective-permute-start.8 = (f32[80,256]{1,0:T(8,128)S(1)}, f32[80,256]{1,0:T(8,128)S(1)}, u32[]{:S(2)}, u32[]{:S(2)}) collective-permute-start(f32[80,256]{1,0:T(8,128)S(1)} %add.20), channel_id=1, source_target_pairs={{0,8},{2,10},{4,12},{6,14},{8,0},{10,2},{12,4},{14,6},{16,24},{18,... | collective-permute-start | bytes 245768 | tf_op jit(solution)/shard_map/ppermute | solution.py:412
  72.3 2.9 %collective-permute-done.8 = f32[80,256]{1,0:T(8,128)S(1)} collective-permute-done((f32[80,256]{1,0:T(8,128)S(1)}, f32[80,256]{1,0:T(8,128)S(1)}, u32[]{:S(2)}, u32[]{:S(2)}) %collective-permute-start.8) | collective-permute-done | bytes 81952 | tf_op jit(solution)/shard_map/ppermute | solution.py:412
  75.1 2.7 %collective-permute-start.9 = (f32[80,256]{1,0:T(8,128)S(1)}, f32[80,256]{1,0:T(8,128)S(1)}, u32[]{:S(2)}, u32[]{:S(2)}) collective-permute-start(f32[80,256]{1,0:T(8,128)S(1)} %add.22), channel_id=1, source_target_pairs={{0,16},{2,18},{4,20},{6,22},{8,24},{10,26},{12,28},{14,30},{16,0},... | collective-permute-start | bytes 245768 | tf_op jit(solution)/shard_map/ppermute | solution.py:412
  77.8 2.6 %shard_map.99 = (f32[16,64,256]{2,1,0:T(8,128)}, f32[2,16,64,256]{3,2,1,0:T(8,128)S(1)}) custom-call(f32[4,80,256]{2,1,0:T(8,128)S(1)} %get-tuple-element.37.low, f32[8,80,256]{2,1,0:T(8,128)S(1)} %get-tuple-element.38.inner, f32[4,80,256]{2,1,0:T(8,128)S(1)} %get-tuple-element.39.high), custom_call_target="tpu_custom_call" | custom-call | tf_op jit(solution)/shard_map/pallas_call | solution.py:499
  80.6 1.6 %shard_map.100 = f32[2,16,64,256]{3,2,1,0:T(8,128)} custom-call(f32[2,16,64,256]{3,2,1,0:T(8,128)S(1)} %get-tuple-element.41.local, f32[80,256]{1,0:T(8,128)S(1)} %select_add_fusion.prefix), custom_call_target="tpu_custom_call" | custom-call | tf_op jit(solution)/shard_map/pallas_call | solution.py:507
  (22 shorter events, 1.7 us)
Async XLA Ops:
  0.6 0.8 %copy-start.2 = (f32[64,256]{1,0:T(8,128)S(1)}, f32[64,256]{1,0:T(8,128)}, u32[]{:S(2)}) copy-start(f32[64,256]{1,0:T(8,128)} %rec.1) | copy-start | bytes 196612
  1.5 0.8 %copy-start.3 = (s32[64,256]{1,0:T(8,128)S(1)}, s32[64,256]{1,0:T(8,128)}, u32[]{:S(2)}) copy-start(s32[64,256]{1,0:T(8,128)} %index.1) | copy-start | bytes 196612
  2.3 0.8 %copy-start.4 = (s32[64,256]{1,0:T(8,128)S(1)}, s32[64,256]{1,0:T(8,128)}, u32[]{:S(2)}) copy-start(s32[64,256]{1,0:T(8,128)} %gap.1) | copy-start | bytes 196612
  3.2 0.7 copy-start.5
  3.8 4.7 %copy-start.6 = (f32[16,64,256]{2,1,0:T(8,128)S(1)}, f32[16,64,256]{2,1,0:T(8,128)}, u32[]{:S(2)}) copy-start(f32[16,64,256]{2,1,0:T(8,128)} %ions.3) | copy-start | bytes 3145732
  5.4 26.2 %copy-start = (f32[16,64,256]{2,1,0:T(8,128)S(1)}, f32[16,64,256]{2,1,0:T(8,128)}, u32[]{:S(2)}) copy-start(f32[16,64,256]{2,1,0:T(8,128)} %phi.5) | copy-start | bytes 3145732
  5.4 26.2 %copy-start.1 = (f32[16,64,256]{2,1,0:T(8,128)S(1)}, f32[16,64,256]{2,1,0:T(8,128)}, u32[]{:S(2)}) copy-start(f32[16,64,256]{2,1,0:T(8,128)} %eps.5) | copy-start | bytes 3145732
  5.4 12.5 %collective-permute-start.1 = (f32[50,8,256]{2,1,0:T(8,128)S(1)}, f32[50,8,256]{2,1,0:T(8,128)S(1)}, u32[]{:S(2)}, u32[]{:S(2)}) collective-permute-start(f32[50,8,256]{2,1,0:T(8,128)S(1)} %get-tuple-element.24), channel_id=1, source_target_pairs={{0,1},{1,0},{2,3},{3,2},{4,5},{5,4},{6,7},{7,6},{8,9},{9,8},{10,11... | collective-permute-start | bytes 1228808 | tf_op jit(solution)/shard_map/ppermute | solution.py:450
  8.5 40.8 %collective-permute-start = (f32[16,64,256]{2,1,0:T(8,128)S(1)}, f32[16,64,256]{2,1,0:T(8,128)S(1)}, u32[]{:S(2)}, u32[]{:S(2)}) collective-permute-start(f32[16,64,256]{2,1,0:T(8,128)S(1)} %copy-done.6), channel_id=1, source_target_pairs={{0,4},{2,6},{4,8},{6,10},{8,12},{10,14},{12,16},{14,18},{16,20},{1... | collective-permute-start | bytes 3145736 | tf_op jit(solution)/shard_map/ppermute | solution.py:32
  19.4 36.6 %collective-permute-start.3 = (f32[11,72,256]{2,1,0:T(8,128)S(1)}, f32[11,72,256]{2,1,0:T(8,128)S(1)}, u32[]{:S(2)}, u32[]{:S(2)}) collective-permute-start(f32[11,72,256]{2,1,0:T(8,128)S(1)} %get-tuple-element.30), channel_id=1, source_target_pairs={{0,2},{2,4},{4,6},{6,8},{8,10},{10,12},{12,14},{14,16},{16,18},{18... | collective-permute-start | bytes 2433032 | tf_op jit(solution)/shard_map/ppermute | solution.py:32
  20.7 35.3 %collective-permute-start.4 = (f32[8,72,256]{2,1,0:T(8,128)S(1)}, f32[8,72,256]{2,1,0:T(8,128)S(1)}, u32[]{:S(2)}, u32[]{:S(2)}) collective-permute-start(f32[8,72,256]{2,1,0:T(8,128)S(1)} %get-tuple-element.31), channel_id=1, source_target_pairs={{2,0},{4,2},{6,4},{8,6},{10,8},{12,10},{14,12},{16,14},{18,16},{20... | collective-permute-start | bytes 1769480 | tf_op jit(solution)/shard_map/ppermute | solution.py:32
  22.0 34.0 %collective-permute-start.5 = (f32[3,72,256]{2,1,0:T(8,128)S(1)}, f32[3,72,256]{2,1,0:T(8,128)S(1)}, u32[]{:S(2)}, u32[]{:S(2)}) collective-permute-start(f32[3,72,256]{2,1,0:T(8,128)S(1)} %get-tuple-element.32), channel_id=1, source_target_pairs={{0,6},{2,8},{4,10},{6,12},{8,14},{10,16},{12,18},{14,20},{16,22},{... | collective-permute-start | bytes 663560 | tf_op jit(solution)/shard_map/ppermute | solution.py:32
  28.2 21.1 %collective-permute-start.2 = (f32[16,8,256]{2,1,0:T(8,128)S(1)}, f32[16,8,256]{2,1,0:T(8,128)S(1)}, u32[]{:S(2)}, u32[]{:S(2)}) collective-permute-start(f32[16,8,256]{2,1,0:T(8,128)S(1)} %slice.4), channel_id=1, source_target_pairs={{0,4},{2,6},{4,8},{6,10},{8,12},{10,14},{12,16},{14,18},{16,20},{1... | collective-permute-start | bytes 393224 | tf_op jit(solution)/shard_map/ppermute | solution.py:32
  59.4 6.0 %collective-permute-start.6 = (f32[80,256]{1,0:T(8,128)S(1)}, f32[80,256]{1,0:T(8,128)S(1)}, u32[]{:S(2)}, u32[]{:S(2)}) collective-permute-start(f32[80,256]{1,0:T(8,128)S(1)} %get-tuple-element.42), channel_id=1, source_target_pairs={{0,2},{2,0},{4,6},{6,4},{8,10},{10,8},{12,14},{14,12},{16,18},{18,... | collective-permute-start | bytes 245768 | tf_op jit(solution)/shard_map/ppermute | solution.py:412
  65.4 5.2 %collective-permute-start.7 = (f32[80,256]{1,0:T(8,128)S(1)}, f32[80,256]{1,0:T(8,128)S(1)}, u32[]{:S(2)}, u32[]{:S(2)}) collective-permute-start(f32[80,256]{1,0:T(8,128)S(1)} %add.18), channel_id=1, source_target_pairs={{0,4},{2,6},{4,0},{6,2},{8,12},{10,14},{12,8},{14,10},{16,20},{18,... | collective-permute-start | bytes 245768 | tf_op jit(solution)/shard_map/ppermute | solution.py:412
  70.6 4.5 %collective-permute-start.8 = (f32[80,256]{1,0:T(8,128)S(1)}, f32[80,256]{1,0:T(8,128)S(1)}, u32[]{:S(2)}, u32[]{:S(2)}) collective-permute-start(f32[80,256]{1,0:T(8,128)S(1)} %add.20), channel_id=1, source_target_pairs={{0,8},{2,10},{4,12},{6,14},{8,0},{10,2},{12,4},{14,6},{16,24},{18,... | collective-permute-start | bytes 245768 | tf_op jit(solution)/shard_map/ppermute | solution.py:412
  75.1 5.4 %collective-permute-start.9 = (f32[80,256]{1,0:T(8,128)S(1)}, f32[80,256]{1,0:T(8,128)S(1)}, u32[]{:S(2)}, u32[]{:S(2)}) collective-permute-start(f32[80,256]{1,0:T(8,128)S(1)} %add.22), channel_id=1, source_target_pairs={{0,16},{2,18},{4,20},{6,22},{8,24},{10,26},{12,28},{14,30},{16,0},... | collective-permute-start | bytes 245768 | tf_op jit(solution)/shard_map/ppermute | solution.py:412

commit v3 on v2

--- a/solution.py
+++ b/solution.py
@@ -69,48 +69,73 @@
 
 
 def rows_kernel(phi, eps, ions, rec, index, gap, table, *rest):
-    blocks, pads, sems = rest[:-2], rest[-2], rest[-1]
+    sides = (len(rest) - 7) // 2
+    blocks, pads, stages = rest[:sides], rest[sides], rest[sides + 1 : 2 * sides + 1]
+    rec_v, index_v, gap_v, table_s, sems, pad_sems = rest[2 * sides + 1 :]
     layers, band, sector = phi.shape
-    starts = sides_of(len(blocks), band)
+    ends = SWEEPS - 1
+    starts = sides_of(sides, band)
     copies = []
-    for start, block in zip(starts, blocks):
-        for k, src in enumerate((phi, eps, ions)):
-            copies.append((src.at[:, pl.ds(start, ROWS)], block.at[k * layers : (k + 1) * layers]))
+    for start, block, stage in zip(starts, blocks, stages):
+        rows = pl.ds(start, ROWS)
+        copies.append((phi.at[:, rows], block.at[0:layers]))
+        copies.append((eps.at[:, rows], block.at[layers : 2 * layers]))
+        copies.append((ions.at[:, rows], stage))
     running = run_all(copies, sems)
+    pad_copies = run_all([(rec, rec_v), (index, index_v), (gap, gap_v), (table, table_s)], pad_sems)
+    for copy in pad_copies:
+        copy.wait()
     for t in range(band // ROWS):
         at = slice(t * ROWS, (t + 1) * ROWS)
-        which = index[at]
+        which = index_v[at]
         picked = jnp.zeros((ROWS, sector), F32)
-        for k in range(table.shape[0]):
-            picked = jnp.where(which == k, table[k], picked)
-        pads[0, at] = rec[at]
-        pads[1, at] = picked * (1 - gap[at]).astype(F32)
-    for start, block in zip(starts, blocks):
-        for k in range(2):
-            block[3 * layers + k] = pads[k, pl.ds(start, ROWS)]
+        for k in range(table_s.shape[0]):
+            picked = jnp.where(which == k, table_s[k], picked)
+        pads[0, at] = rec_v[at]
+        pads[1, at] = picked * (1 - gap_v[at]).astype(F32)
     for copy in running:
         copy.wait()
+    sub = lax.broadcasted_iota(jnp.int32, (ROWS, sector), 0)
+    first_half = sub < ROWS // 2
+    for side, (start, block, stage) in enumerate(zip(starts, blocks, stages)):
+        tail = (lax.axis_index("radius") == 0) if sides == 1 else side == 0
+        base = 2 * layers
+        for j in range(layers // 2):
+            one, two = stage[2 * j], stage[2 * j + 1]
+            from_tail = jnp.where(first_half, roll(one, ROWS // 2, 0), two)
+            from_head = jnp.where(first_half, one, roll(two, ROWS // 2, 0))
+            block[base + j] = jnp.where(tail, from_tail, from_head)
+        base += layers // 2
+        for k in range(ends):
+            block[base + k] = stage[k]
+            block[base + ends + k] = stage[layers - ends + k]
+        base += 2 * ends
+        for k in range(2):
+            block[base + k] = pads[k, pl.ds(start, ROWS)]
 
 
 def halo_kernel(sides, phi, eps, ions, *refs):
-    raws, (up, down, far, sems) = refs[:sides], refs[sides:]
+    raws, (inner, outer, far, sems) = refs[:sides], refs[sides:]
     layers, band, _ = phi.shape
     depth = SWEEPS
+    odd = lax.rem(lax.axis_index("drift"), 2) == 1
+    low, high = 0, layers - depth
+    near_at, far_at = jnp.where(odd, low, high), jnp.where(odd, high, low)
+    ends = 2 * layers + layers // 2
     copies = []
-    for dst, at, k, start, count in (
-        (up, 0, 0, layers - depth, depth),
-        (up, depth, 1, layers - depth, depth),
-        (up, 2 * depth, 2, 0, depth - 1),
-        (down, 0, 0, 0, depth),
-        (down, depth, 1, 0, depth),
-        (far, 0, 2, layers - depth + 1, depth - 1),
+    for dst, at, k, start, raw_at, count in (
+        (inner, 0, 0, near_at, near_at, depth),
+        (inner, depth, 1, near_at, layers + near_at, depth),
+        (inner, 2 * depth, 2, 0, ends, depth - 1),
+        (outer, 0, 0, far_at, far_at, depth),
+        (outer, depth, 1, far_at, layers + far_at, depth),
+        (far, 0, 2, layers - depth + 1, ends + depth - 1, depth - 1),
     ):
         src = (phi, eps, ions)[k]
-        copies.append((src.at[start : start + count], dst.at[at : at + count, 0:band]))
+        copies.append((src.at[pl.ds(start, count)], dst.at[at : at + count, 0:band]))
         for side, raw in enumerate(raws):
             rows = slice(band + side * ROWS, band + (side + 1) * ROWS)
-            first = k * layers + start
-            copies.append((raw.at[first : first + count], dst.at[at : at + count, rows]))
+            copies.append((raw.at[pl.ds(raw_at, count)], dst.at[at : at + count, rows]))
     for copy in run_all(copies, sems):
         copy.wait()
 
@@ -174,7 +199,7 @@
     geo[4] = jnp.where(lane == sector - 1, 0.0, 1.0)
     geo[5] = jnp.where(lane == 0, 0.0, 1.0)
     for k in range(2):
-        for at, value in win.pieces(lambda k=k: pads[k], lambda side, k=k: raws[side][3 * layers + k]):
+        for at, value in win.pieces(lambda k=k: pads[k], lambda side, k=k: raws[side][2 * layers + layers // 2 + 2 * (SWEEPS - 1) + k]):
             geo[6 + k, at] = value
 
     @pl.loop(0, layers)
@@ -204,7 +229,7 @@
 
 def inner_relax_kernel(sides, moved, p0, w, inv2, geo, *refs):
     rows_moved = refs[:sides]
-    charge_out, window_out, sums_out, state, b_out, p1, p2, p3, b = refs[sides:]
+    charge_out, swap, window_out, sums_out, state, b_out, p1, p2, p3, b, raw = refs[sides:]
     layers, band, sector = moved.shape
     depth = SWEEPS
     win = Window(sides, band)
@@ -213,38 +238,53 @@
     sub = lax.broadcasted_iota(jnp.int32, (ROWS, sector), 0)
     phis = (p0, p1, p2, p3)
 
-    @pl.loop(0, layers)
-    def _(z):
-        inner = (z > 0) & (z < layers - 1)
-        for at, ions in win.pieces(lambda: moved[z], lambda side: rows_moved[side][z]):
-            value = drift_charge(ions, geo[6, at], geo[7, at], d)
-            if at is win.own:
-                charge_out[z] = value
-            b[z, at] = jnp.where(inner, value * inv2[z, at], value)
-
+    @pl.loop(0, layers // 2)
+    def _(j):
+        for half in range(2):
+            z = 2 * j + half
+            inner = (z > 0) & (z < layers - 1)
+            for at, side, has in ((win.own, None, None), *win.ends):
+                if side is None:
+                    ions = moved[z]
+                else:
+                    ions = rows_moved[side][j]
+                    if half == (0 if at is win.ends[0][0] else 1):
+                        ions = roll(ions, ROWS // 2, 0)
+                    ions = jnp.where(has, ions, 0.0)
+                value = drift_charge(ions, geo[6, at], geo[7, at], d)
+                if side is None:
+                    charge_out[z] = value
+                raw[z, at] = value
+                b[z, at] = jnp.where(inner, value * inv2[z, at], value)
+
+    odd = lax.rem(d, 2) == 1
+    for k in range(depth - 1):
+        swap[k] = raw[jnp.where(odd, k, layers - depth + 1 + k)]
     sums_out[...] = jnp.zeros_like(sums_out)
     for s in range(1, depth + 1):
         src = phis[s - 1]
 
-        @pl.loop(s, layers - s)
-        def _(z, s=s, src=src):
-            def put(at, total):
-                if s < depth:
-                    phis[s][z, at] = total
-                else:
-                    window_out[z - depth, at] = total
-                    sums_out[at] += total
-
-            sweep_layer(
-                lambda at: src[z, at],
-                lambda at: src[z + 1, at],
-                lambda at: src[z - 1, at],
-                lambda k, at: w[k, z, at],
-                lambda at: b[z, at],
-                tiles,
-                sub,
-                put,
-            )
+        @pl.loop(s, layers - s, step=2)
+        def _(first, s=s, src=src):
+            for z in (first, first + 1):
+
+                def put(at, total, z=z):
+                    if s < depth:
+                        phis[s][z, at] = total
+                    else:
+                        window_out[z - depth, at] = total
+                        sums_out[at] += total
+
+                sweep_layer(
+                    lambda at, z=z: src[z, at],
+                    lambda at, z=z: src[z + 1, at],
+                    lambda at, z=z: src[z - 1, at],
+                    lambda k, at, z=z: w[k, z, at],
+                    lambda at, z=z: b[z, at],
+                    tiles,
+                    sub,
+                    put,
+                )
 
     for s in range(1, depth):
         for k in range(2):
@@ -255,7 +295,7 @@
         b_out[1, k] = b[layers - depth + k]
 
 
-def outer_relax_kernel(sides, below, above, far, p0, ex, w, geo, state, b_in, sums_in, *refs):
+def outer_relax_kernel(sides, inner, outer, far, swapped, p0, ex, w, geo, state, b_in, sums_in, *refs):
     low_out, high_out, sums_out, ph, eh, wb, bb, q = refs
     layers, rows, sector = p0.shape
     depth, n = SWEEPS, layers
@@ -266,20 +306,22 @@
     d, drifts = lax.axis_index("drift"), lax.axis_size("drift")
     sub = lax.broadcasted_iota(jnp.int32, (ROWS, sector), 0)
 
+    odd = lax.rem(d, 2) == 1
     for k in range(depth):
-        for ref, dst in ((below, 0), (above, 1)):
-            for at, value in win.of_halo(ref, k):
-                ph[dst, k, at] = value
-            for at, value in win.of_halo(ref, depth + k):
-                eh[dst, k if dst == 0 else 2 + k, at] = value
+        for ref, half, to in ((ph, 0, (k, k)), (eh, depth, (k, 2 + k))):
+            for (at, one), (_, two) in zip(win.of_halo(inner, half + k), win.of_halo(outer, half + k)):
+                ref[0, to[0], at] = jnp.where(odd, one, two)
+                ref[1, to[1], at] = jnp.where(odd, two, one)
     for k in range(2):
         eh[0, depth + k] = ex[k]
         eh[1, k] = ex[n - 2 + k]
 
     for k in range(depth - 1):
-        for side, at_layer, ref, index, slab in ((0, k, far, k, d - 1), (1, k + 1, below, 2 * depth + k, d + 1)):
-            for at, ions in win.of_halo(ref, index):
-                bb[side, at_layer, at] = drift_charge(ions, geo[6, at], geo[7, at], slab)
+        for (at, near_ions), (_, far_ions) in zip(win.of_halo(inner, 2 * depth + k), win.of_halo(far, k)):
+            rec, inj = geo[6, at], geo[7, at]
+            ready = swapped[k, at]
+            bb[0, k, at] = jnp.where(odd, ready, drift_charge(far_ions, rec, inj, d - 1))
+            bb[1, k + 1, at] = jnp.where(odd, drift_charge(near_ions, rec, inj, d + 1), ready)
     bb[0, depth - 1] = b_in[0, 0]
     bb[1, 0] = b_in[1, depth - 1]
     for side in range(2):
@@ -434,33 +476,46 @@
     sides = 1 if lax.axis_size("radius") == 2 else 2
     sent = band + sides * ROWS
     dma = pltpu.SemaphoreType.DMA
-    phi, eps, ions_far = [
-        pltpu.with_memory_space_constraint(x, pltpu.HBM) for x in (potential_guess, permittivity, ions)
-    ]
+    ends = depth - 1
+    row_block = 2 * layers + layers // 2 + 2 * ends + 2
+    far_args = (potential_guess, permittivity, ions, recombination, rate_index, gap_mask, rate_table)
+    phi, eps, ions_far, *pad_args = [pltpu.with_memory_space_constraint(x, pltpu.HBM) for x in far_args]
 
     moved = shifted(ions, "drift", 2)
     *blocks, pads = kernel(
         rows_kernel,
-        [plane(3 * layers + 2, ROWS, sector)] * sides + [plane(2, band, sector)],
-        [ANYWHERE] * 3 + [IN_VMEM] * 3 + [pl.BlockSpec(memory_space=pltpu.SMEM)],
-        scratch=[dma((3 * sides,))],
-        mb=4,
-    )(phi, eps, ions_far, recombination, rate_index, gap_mask, rate_table)
+        [plane(row_block, ROWS, sector)] * sides + [plane(2, band, sector)],
+        [ANYWHERE] * 7,
+        scratch=[near(layers, ROWS, sector)] * sides
+        + [
+            near(band, sector),
+            pltpu.VMEM((band, sector), jnp.int32),
+            pltpu.VMEM((band, sector), jnp.int32),
+            pltpu.SMEM(rate_table.shape, F32),
+            dma((3 * sides,)),
+            dma((4,)),
+        ],
+        mb=5,
+    )(phi, eps, ions_far, *pad_args)
     if sides == 1:
         raws = [lax.ppermute(blocks[0], "radius", [(0, 1), (1, 0)])]
     else:
         raws = [shifted(blocks[0], "radius", 1), shifted(blocks[1], "radius", -1)]
-    up, down, beyond = kernel(
+    to_core, to_chip, beyond = kernel(
         functools.partial(halo_kernel, sides),
         [plane(3 * depth - 1, sent, sector), plane(2 * depth, sent, sector), plane(depth - 1, sent, sector)],
         [ANYWHERE] * 3 + [IN_VMEM] * sides,
         scratch=[dma((6 * (1 + sides),))],
         mb=6,
     )(phi, eps, ions_far, *raws)
-    rows_moved = [shifted(raw[2 * layers : 3 * layers], "drift", 2) for raw in raws]
-    below = shifted(up, "drift", 1)
-    above = shifted(down, "drift", -1)
-    far = shifted(beyond, "drift", 3)
+    count = lax.axis_size("drift")
+    assert count % 2 == 0
+    partners = [(i, i ^ 1) for i in range(count)]
+    chips = [(i, i + 1 if i % 2 else i - 1) for i in range(1, count - 1)]
+    rows_moved = [shifted(raw[2 * layers : 2 * layers + layers // 2], "drift", 2) for raw in raws]
+    outer = lax.ppermute(to_chip, "drift", chips)
+    far = lax.ppermute(beyond, "drift", [(i - 3, i) for i in range(4, count, 2)])
+    inner = lax.ppermute(to_core, "drift", partners)
 
     box = plane(layers, rows, sector)
     p0, ex, w, inv2, geo = kernel(
@@ -470,23 +525,25 @@
         mb=20,
     )(potential_guess, permittivity, pads, *raws)
     p0, ex, w, inv2, geo = [fetched(x) for x in (p0, ex, w, inv2, geo)]
-    charge, inner, sums, state, b = kernel(
+    charge, swap, middle, sums, state, b = kernel(
         functools.partial(inner_relax_kernel, sides),
         [
             plane(layers, band, sector),
+            plane(depth - 1, rows, sector),
             plane(layers - 2 * depth, rows, sector),
             plane(rows, sector),
             plane(2, depth - 1, 2, rows, sector),
             plane(2, depth, rows, sector),
         ],
         [IN_VMEM] * (5 + sides),
-        scratch=[near(layers, rows, sector)] * 4,
+        scratch=[near(layers, rows, sector)] * 5,
         mb=16,
     )(moved, p0, w, inv2, geo, *rows_moved)
+    swapped = lax.ppermute(swap, "drift", partners)
     low, high, sums = kernel(
         functools.partial(outer_relax_kernel, sides),
         [plane(depth, rows, sector), plane(depth, rows, sector), plane(rows, sector)],
-        [IN_VMEM] * 10,
+        [IN_VMEM] * 11,
         scratch=[
             near(2, depth, rows, sector),
             near(2, depth + 2, rows, sector),
@@ -495,14 +552,14 @@
             near(depth - 1, 2, depth, rows, sector),
         ],
         mb=16,
-    )(below, above, far, p0, ex, w, geo, fetched(state), fetched(b), fetched(sums))
+    )(inner, outer, far, swapped, p0, ex, w, geo, fetched(state), fetched(b), fetched(sums))
     potential, local = kernel(
         local_kernel,
         [plane(layers, band, sector), plane(2, layers, band, sector)],
         [IN_VMEM] * 3,
         scratch=[near(rows, sector)],
         mb=16,
-    )(low, inner, high)
+    )(low, middle, high)
     below_sums = sums_below(sums)
     distortion = kernel(
         offset_kernel,

time: 82.6 us -> 76 us (0.920)
  local copies, waits for them, and re-layouts: 3.19 us -> 0.02 us
  waiting for transfers between devices: 28.3 us -> 25.6 us
  Pallas kernels: 19.5 us -> 17.5 us
  starting transfers between devices: 30.3 us -> 31.8 us
    ppermute x0 -> x4, starting transfers between devices: none -> 6.74 us  [the longest x1 5.31 us: body(): swapped = lax.ppermute(swap, 'drift', partners)]
    ppermute x5 -> x2, waiting for transfers between devices: 15.4 us -> 9.76 us  [shifted(): return lax.ppermute(block, axis, route)]
    ppermute x5 -> x2, starting transfers between devices: 15.6 us -> 10.2 us  [shifted(): return lax.ppermute(block, axis, route)]
    unnamed x14 -> x4, local copies, waits for them, and re-layouts: 3.18 us -> 0.01 us
    ppermute x1, waiting for transfers between devices: 6 us -> 9.05 us  [body(): raws = [lax.ppermute(blocks[0], 'radius', [(0, 1), (1, 0)])]]
    ppermute x4, starting transfers between devices: 11.6 us -> 13.3 us  [sums_below(): other = lax.ppermute(total, 'drift', [(i, i ^ step) for i in range(count)])]
    pallas_call x1, Pallas kernels: 6.72 us -> 5.14 us  [body(): kernel(functools.partial(inner_relax_kernel, sides), [plane(layers, band,...]
    ppermute x1, starting transfers between devices: 3.06 us -> 1.58 us  [body(): raws = [lax.ppermute(blocks[0], 'radius', [(0, 1), (1, 0)])]]
  transfers between devices with their start and end apart: 10 -> 11, of which waited for: 6 -> 6; matrix products, arithmetic and copies ran while one was open for 0% -> 0% of each run, Pallas kernels for 16% -> 17%
where the time goes in v3:
time: 76 us; the launch traced here: 75.8 us
  starting transfers between devices  31.8 us (42%)
  waiting for transfers between devices  25.6 us (34%)
  Pallas kernels  17.5 us (23%)
  between operations  0.78 us (1%)
    ppermute x4, starting transfers between devices, sums_below(): other = lax.ppermute(total, 'drift', [(i, i ^ step) for i in range(count)])  13.3 us
    ppermute x2, starting transfers between devices, shifted(): return lax.ppermute(block, axis, route)  10.2 us
    ppermute x2, waiting for transfers between devices, shifted(): return lax.ppermute(block, axis, route)  9.76 us
    ppermute x1, waiting for transfers between devices, body(): raws = [lax.ppermute(blocks[0], 'radius', [(0, 1), (1, 0)])]  9.05 us
    ppermute x4, waiting for transfers between devices, sums_below(): other = lax.ppermute(total, 'drift', [(i, i ^ step) for i in range(count)])  6.31 us
    ppermute x1, starting transfers between devices, body(): swapped = lax.ppermute(swap, 'drift', partners)  5.31 us
    pallas_call x1, Pallas kernels, body(): kernel(functools.partial(inner_relax_kernel, sides), [plane(layers, band,...  5.14 us
    pallas_call x1, Pallas kernels, body(): kernel(functools.partial(outer_relax_kernel, sides), [plane(depth, rows,...  3.32 us
  transfers between devices with their start and end apart: 11, of which 6 were waited for; matrix products, arithmetic and copies ran while one was open for 0% of the time, Pallas kernels for 17%

profile of v3, /device:TPU:0, one launch (start us, length us, event | category | flops | bytes accessed | tf_op | source)
XLA Modules:
  0.0 75.8 jit_solution(519445273163899233)
XLA Ops:
  0.6 4.9 %collective-permute-start = (f32[16,64,256]{2,1,0:T(8,128)}, f32[16,64,256]{2,1,0:T(8,128)S(1)}, u32[]{:S(2)}, u32[]{:S(2)}) collective-permute-start(f32[16,64,256]{2,1,0:T(8,128)} %ions.3), channel_id=1, source_target_pairs={{0,4},{2,6},{4,8},{6,10},{8,12},{10,14},{12,16},{14,18},{16,20},{1... | collective-permute-start | bytes 3145736 | tf_op jit(solution)/shard_map/ppermute | solution.py:32
  5.6 1.2 %shard_map.94 = (f32[48,8,256]{2,1,0:T(8,128)S(1)}, f32[2,64,256]{2,1,0:T(8,128)S(1)}) custom-call(f32[16,64,256]{2,1,0:T(8,128)} %phi.5, f32[16,64,256]{2,1,0:T(8,128)} %eps.5, f32[16,64,256]{2,1,0:T(8,128)} %ions.3, f32[64,256]{1,0:T(8,128)} %rec.1, s32[64,256]{1,0:T(8,128)} %index.1, s32[64,256]{1,0:T(8,128)} %gap.1, f32[16]{0:T(128)} %table.1), custom_call_target="tpu_custom_call" | custom-call | tf_op jit(solution)/shard_map/pallas_call | solution.py:485
  6.8 1.6 %collective-permute-start.1 = (f32[48,8,256]{2,1,0:T(8,128)S(1)}, f32[48,8,256]{2,1,0:T(8,128)S(1)}, u32[]{:S(2)}, u32[]{:S(2)}) collective-permute-start(f32[48,8,256]{2,1,0:T(8,128)S(1)} %get-tuple-element.25), channel_id=1, source_target_pairs={{0,1},{1,0},{2,3},{3,2},{4,5},{5,4},{6,7},{7,6},{8,9},{9,8},{10,11... | collective-permute-start | bytes 1179656 | tf_op jit(solution)/shard_map/ppermute | solution.py:501
  8.4 9.1 %collective-permute-done.1.refs_0_ = f32[48,8,256]{2,1,0:T(8,128)S(1)} collective-permute-done((f32[48,8,256]{2,1,0:T(8,128)S(1)}, f32[48,8,256]{2,1,0:T(8,128)S(1)}, u32[]{:S(2)}, u32[]{:S(2)}) %collective-permute-start.1) | collective-permute-done | bytes 393248 | tf_op jit(solution)/shard_map/ppermute | solution.py:501
  17.5 1.4 %shard_map.97 = (f32[11,72,256]{2,1,0:T(8,128)S(1)}, f32[8,72,256]{2,1,0:T(8,128)S(1)}, f32[3,72,256]{2,1,0:T(8,128)S(1)}) custom-call(f32[16,64,256]{2,1,0:T(8,128)} %phi.5, f32[16,64,256]{2,1,0:T(8,128)} %eps.5, f32[16,64,256]{2,1,0:T(8,128)} %ions.3, f32[48,8,256]{2,1,0:T(8,128)S(1)} %collective-permute-done.1.refs_0_), custom_call_target="tpu_custom_call" | custom-call | tf_op jit(solution)/shard_map/pallas_call | solution.py:504
  18.9 0.1 collective-permute-start.3
  19.0 0.7 collective-permute-start.4
  19.7 5.2 %collective-permute-start.2 = (f32[8,8,256]{2,1,0:T(8,128)S(1)}, f32[8,8,256]{2,1,0:T(8,128)S(1)}, u32[]{:S(2)}, u32[]{:S(2)}) collective-permute-start(f32[8,8,256]{2,1,0:T(8,128)S(1)} %slice.4), channel_id=1, source_target_pairs={{0,4},{2,6},{4,8},{6,10},{8,12},{10,14},{12,16},{14,18},{16,20},{1... | collective-permute-start | bytes 196616 | tf_op jit(solution)/shard_map/ppermute | solution.py:32
  25.0 2.3 %shard_map.95 = (f32[16,80,256]{2,1,0:T(8,128)S(1)}, f32[16,80,256]{2,1,0:T(8,128)S(1)}, f32[6,16,80,256]{3,2,1,0:T(8,128)S(1)}, f32[16,80,256]{2,1,0:T(8,128)S(1)}, f32[8,80,256]{2,1,0:T(8,128)S(1)}) custom-call(f32[16,64,256]{2,1,0:T(8,128)S(1)} %copy-done, f32[16,64,256]{2,1,0:T(8,128)S(1)} %copy-done.1, f32[2,64,256]{2,1,0:T(8,128)S(1)} %get-tuple-element.24.pads, ...), custom_call_target="tpu_custom_call" | custom-call | tf_op jit(solution)/shard_map/pallas_call | solution.py:521
  27.2 9.8 %collective-permute-done.2.refs_0_ = f32[8,8,256]{2,1,0:T(8,128)S(1)} collective-permute-done((f32[8,8,256]{2,1,0:T(8,128)S(1)}, f32[8,8,256]{2,1,0:T(8,128)S(1)}, u32[]{:S(2)}, u32[]{:S(2)}) %collective-permute-start.2) | collective-permute-done | bytes 65568 | tf_op jit(solution)/shard_map/ppermute | solution.py:32
  37.0 5.1 %shard_map.96 = (f32[16,64,256]{2,1,0:T(8,128)}, f32[3,80,256]{2,1,0:T(8,128)S(1)}, f32[8,80,256]{2,1,0:T(8,128)S(1)}, f32[80,256]{1,0:T(8,128)S(1)}, f32[2,3,2,...) custom-call(f32[16,64,256]{2,1,0:T(8,128)S(1)} %collective-permute-done.moved, ...), custom_call_target="tpu_custom_call" | custom-call | tf_op jit(solution)/shard_map/pallas_call | solution.py:528
  42.1 5.3 %collective-permute-start.6 = (f32[3,80,256]{2,1,0:T(8,128)S(1)}, f32[3,80,256]{2,1,0:T(8,128)S(1)}, u32[]{:S(2)}, u32[]{:S(2)}) collective-permute-start(f32[3,80,256]{2,1,0:T(8,128)S(1)} %get-tuple-element.34), channel_id=1, source_target_pairs={{0,2},{2,0},{4,6},{6,4},{8,10},{10,8},{12,14},{14,12},{16,18},{18,... | collective-permute-start | bytes 737288 | tf_op jit(solution)/shard_map/ppermute | solution.py:542
  47.4 0.7 collective-permute-start.5
  48.1 0.4 collective-permute-done.6.swapped
  48.6 3.3 %shard_map.98 = (f32[4,80,256]{2,1,0:T(8,128)S(1)}, f32[4,80,256]{2,1,0:T(8,128)S(1)}, f32[80,256]{1,0:T(8,128)S(1)}) custom-call(f32[11,72,256]{2,1,0:T(8,128)S(1)} %collective-permute-done.3.inner, f32[8,72,256]{2,1,0:T(8,128)S(1)} %collective-permute-done.4.outer, f32[3,72,256]{2,1,0:T(8,128)S(1)} %collective-permute-done.5.far, ...), custom_call_target="tpu_custom_call" | custom-call | tf_op jit(solution)/shard_map/pallas_call | solution.py:543
  51.9 5.4 %collective-permute-start.7 = (f32[80,256]{1,0:T(8,128)S(1)}, f32[80,256]{1,0:T(8,128)S(1)}, u32[]{:S(2)}, u32[]{:S(2)}) collective-permute-start(f32[80,256]{1,0:T(8,128)S(1)} %get-tuple-element.44), channel_id=1, source_target_pairs={{0,2},{2,0},{4,6},{6,4},{8,10},{10,8},{12,14},{14,12},{16,18},{18,... | collective-permute-start | bytes 245768 | tf_op jit(solution)/shard_map/ppermute | solution.py:454
  57.3 0.9 %collective-permute-done.7 = f32[80,256]{1,0:T(8,128)S(1)} collective-permute-done((f32[80,256]{1,0:T(8,128)S(1)}, f32[80,256]{1,0:T(8,128)S(1)}, u32[]{:S(2)}, u32[]{:S(2)}) %collective-permute-start.7) | collective-permute-done | bytes 81952 | tf_op jit(solution)/shard_map/ppermute | solution.py:454
  58.2 2.3 %collective-permute-start.8 = (f32[80,256]{1,0:T(8,128)S(1)}, f32[80,256]{1,0:T(8,128)S(1)}, u32[]{:S(2)}, u32[]{:S(2)}) collective-permute-start(f32[80,256]{1,0:T(8,128)S(1)} %add.18), channel_id=1, source_target_pairs={{0,4},{2,6},{4,0},{6,2},{8,12},{10,14},{12,8},{14,10},{16,20},{18,... | collective-permute-start | bytes 245768 | tf_op jit(solution)/shard_map/ppermute | solution.py:454
  60.5 3.0 %collective-permute-done.8 = f32[80,256]{1,0:T(8,128)S(1)} collective-permute-done((f32[80,256]{1,0:T(8,128)S(1)}, f32[80,256]{1,0:T(8,128)S(1)}, u32[]{:S(2)}, u32[]{:S(2)}) %collective-permute-start.8) | collective-permute-done | bytes 81952 | tf_op jit(solution)/shard_map/ppermute | solution.py:454
  63.5 2.6 %collective-permute-start.9 = (f32[80,256]{1,0:T(8,128)S(1)}, f32[80,256]{1,0:T(8,128)S(1)}, u32[]{:S(2)}, u32[]{:S(2)}) collective-permute-start(f32[80,256]{1,0:T(8,128)S(1)} %add.20), channel_id=1, source_target_pairs={{0,8},{2,10},{4,12},{6,14},{8,0},{10,2},{12,4},{14,6},{16,24},{18,... | collective-permute-start | bytes 245768 | tf_op jit(solution)/shard_map/ppermute | solution.py:454
  66.0 2.4 %collective-permute-done.9 = f32[80,256]{1,0:T(8,128)S(1)} collective-permute-done((f32[80,256]{1,0:T(8,128)S(1)}, f32[80,256]{1,0:T(8,128)S(1)}, u32[]{:S(2)}, u32[]{:S(2)}) %collective-permute-start.9) | collective-permute-done | bytes 81952 | tf_op jit(solution)/shard_map/ppermute | solution.py:454
  68.5 3.1 %collective-permute-start.10 = (f32[80,256]{1,0:T(8,128)S(1)}, f32[80,256]{1,0:T(8,128)S(1)}, u32[]{:S(2)}, u32[]{:S(2)}) collective-permute-start(f32[80,256]{1,0:T(8,128)S(1)} %add.22), channel_id=1, source_target_pairs={{0,16},{2,18},{4,20},{6,22},{8,24},{10,26},{12,28},{14,30},{16,0},... | collective-permute-start | bytes 245768 | tf_op jit(solution)/shard_map/ppermute | solution.py:454
  71.6 2.6 %shard_map.99 = (f32[16,64,256]{2,1,0:T(8,128)}, f32[2,16,64,256]{3,2,1,0:T(8,128)S(1)}) custom-call(f32[4,80,256]{2,1,0:T(8,128)S(1)} %get-tuple-element.39.low, f32[8,80,256]{2,1,0:T(8,128)S(1)} %get-tuple-element.40.inner, f32[4,80,256]{2,1,0:T(8,128)S(1)} %get-tuple-element.41.high), custom_call_target="tpu_custom_call" | custom-call | tf_op jit(solution)/shard_map/pallas_call | solution.py:556
  74.2 1.6 %shard_map.100 = f32[2,16,64,256]{3,2,1,0:T(8,128)} custom-call(f32[2,16,64,256]{3,2,1,0:T(8,128)S(1)} %get-tuple-element.43.local, f32[80,256]{1,0:T(8,128)S(1)} %select_add_fusion.prefix), custom_call_target="tpu_custom_call" | custom-call | tf_op jit(solution)/shard_map/pallas_call | solution.py:564
  (14 shorter events, 0.1 us)
Async XLA Ops:
  0.6 36.3 %collective-permute-start = (f32[16,64,256]{2,1,0:T(8,128)}, f32[16,64,256]{2,1,0:T(8,128)S(1)}, u32[]{:S(2)}, u32[]{:S(2)}) collective-permute-start(f32[16,64,256]{2,1,0:T(8,128)} %ions.3), channel_id=1, source_target_pairs={{0,4},{2,6},{4,8},{6,10},{8,12},{10,14},{12,16},{14,18},{16,20},{1... | collective-permute-start | bytes 3145736 | tf_op jit(solution)/shard_map/ppermute | solution.py:32
  6.8 18.1 %copy-start = (f32[16,64,256]{2,1,0:T(8,128)S(1)}, f32[16,64,256]{2,1,0:T(8,128)}, u32[]{:S(2)}) copy-start(f32[16,64,256]{2,1,0:T(8,128)} %phi.5) | copy-start | bytes 3145732
  6.8 18.1 %copy-start.1 = (f32[16,64,256]{2,1,0:T(8,128)S(1)}, f32[16,64,256]{2,1,0:T(8,128)}, u32[]{:S(2)}) copy-start(f32[16,64,256]{2,1,0:T(8,128)} %eps.5) | copy-start | bytes 3145732
  6.8 10.6 %collective-permute-start.1 = (f32[48,8,256]{2,1,0:T(8,128)S(1)}, f32[48,8,256]{2,1,0:T(8,128)S(1)}, u32[]{:S(2)}, u32[]{:S(2)}) collective-permute-start(f32[48,8,256]{2,1,0:T(8,128)S(1)} %get-tuple-element.25), channel_id=1, source_target_pairs={{0,1},{1,0},{2,3},{3,2},{4,5},{5,4},{6,7},{7,6},{8,9},{9,8},{10,11... | collective-permute-start | bytes 1179656 | tf_op jit(solution)/shard_map/ppermute | solution.py:501
  18.9 29.2 %collective-permute-start.3 = (f32[11,72,256]{2,1,0:T(8,128)S(1)}, f32[11,72,256]{2,1,0:T(8,128)S(1)}, u32[]{:S(2)}, u32[]{:S(2)}) collective-permute-start(f32[11,72,256]{2,1,0:T(8,128)S(1)} %get-tuple-element.31), channel_id=1, source_target_pairs={{0,2},{2,0},{4,6},{6,4},{8,10},{10,8},{12,14},{14,12},{16,18},{18,... | collective-permute-start | bytes 2433032 | tf_op jit(solution)/shard_map/ppermute | solution.py:518
  19.0 29.1 %collective-permute-start.4 = (f32[8,72,256]{2,1,0:T(8,128)S(1)}, f32[8,72,256]{2,1,0:T(8,128)S(1)}, u32[]{:S(2)}, u32[]{:S(2)}) collective-permute-start(f32[8,72,256]{2,1,0:T(8,128)S(1)} %get-tuple-element.32), channel_id=1, source_target_pairs={{2,4},{4,2},{6,8},{8,6},{10,12},{12,10},{14,16},{16,14},{18,20},{2... | collective-permute-start | bytes 1769480 | tf_op jit(solution)/shard_map/ppermute | solution.py:516
  19.7 17.3 %collective-permute-start.2 = (f32[8,8,256]{2,1,0:T(8,128)S(1)}, f32[8,8,256]{2,1,0:T(8,128)S(1)}, u32[]{:S(2)}, u32[]{:S(2)}) collective-permute-start(f32[8,8,256]{2,1,0:T(8,128)S(1)} %slice.4), channel_id=1, source_target_pairs={{0,4},{2,6},{4,8},{6,10},{8,12},{10,14},{12,16},{14,18},{16,20},{1... | collective-permute-start | bytes 196616 | tf_op jit(solution)/shard_map/ppermute | solution.py:32
  42.1 6.4 %collective-permute-start.6 = (f32[3,80,256]{2,1,0:T(8,128)S(1)}, f32[3,80,256]{2,1,0:T(8,128)S(1)}, u32[]{:S(2)}, u32[]{:S(2)}) collective-permute-start(f32[3,80,256]{2,1,0:T(8,128)S(1)} %get-tuple-element.34), channel_id=1, source_target_pairs={{0,2},{2,0},{4,6},{6,4},{8,10},{10,8},{12,14},{14,12},{16,18},{18,... | collective-permute-start | bytes 737288 | tf_op jit(solution)/shard_map/ppermute | solution.py:542
  47.4 0.7 collective-permute-start.5
  51.9 6.3 %collective-permute-start.7 = (f32[80,256]{1,0:T(8,128)S(1)}, f32[80,256]{1,0:T(8,128)S(1)}, u32[]{:S(2)}, u32[]{:S(2)}) collective-permute-start(f32[80,256]{1,0:T(8,128)S(1)} %get-tuple-element.44), channel_id=1, source_target_pairs={{0,2},{2,0},{4,6},{6,4},{8,10},{10,8},{12,14},{14,12},{16,18},{18,... | collective-permute-start | bytes 245768 | tf_op jit(solution)/shard_map/ppermute | solution.py:454
  58.2 5.2 %collective-permute-start.8 = (f32[80,256]{1,0:T(8,128)S(1)}, f32[80,256]{1,0:T(8,128)S(1)}, u32[]{:S(2)}, u32[]{:S(2)}) collective-permute-start(f32[80,256]{1,0:T(8,128)S(1)} %add.18), channel_id=1, source_target_pairs={{0,4},{2,6},{4,0},{6,2},{8,12},{10,14},{12,8},{14,10},{16,20},{18,... | collective-permute-start | bytes 245768 | tf_op jit(solution)/shard_map/ppermute | solution.py:454
  63.5 5.0 %collective-permute-start.9 = (f32[80,256]{1,0:T(8,128)S(1)}, f32[80,256]{1,0:T(8,128)S(1)}, u32[]{:S(2)}, u32[]{:S(2)}) collective-permute-start(f32[80,256]{1,0:T(8,128)S(1)} %add.20), channel_id=1, source_target_pairs={{0,8},{2,10},{4,12},{6,14},{8,0},{10,2},{12,4},{14,6},{16,24},{18,... | collective-permute-start | bytes 245768 | tf_op jit(solution)/shard_map/ppermute | solution.py:454
  68.5 5.7 %collective-permute-start.10 = (f32[80,256]{1,0:T(8,128)S(1)}, f32[80,256]{1,0:T(8,128)S(1)}, u32[]{:S(2)}, u32[]{:S(2)}) collective-permute-start(f32[80,256]{1,0:T(8,128)S(1)} %add.22), channel_id=1, source_target_pairs={{0,16},{2,18},{4,20},{6,22},{8,24},{10,26},{12,28},{14,30},{16,0},... | collective-permute-start | bytes 245768 | tf_op jit(solution)/shard_map/ppermute | solution.py:454

commit v4 on v3

--- a/solution.py
+++ b/solution.py
@@ -65,7 +65,14 @@
 def sides_of(count, band):
     if count == 1:
         return [pl.multiple_of(jnp.where(lax.axis_index("radius") == 0, band - ROWS, 0), ROWS)]
-    return [band - ROWS, 0]
+    return [0, band - ROWS]
+
+
+def window_rows(sides, band):
+    own = [t * ROWS for t in range(band // ROWS)]
+    if sides == 1:
+        return [*own, jnp.where(lax.axis_index("radius") == 0, band, -ROWS)]
+    return [*own, band, -ROWS]
 
 
 def rows_kernel(phi, eps, ions, rec, index, gap, table, *rest):
@@ -98,7 +105,7 @@
     sub = lax.broadcasted_iota(jnp.int32, (ROWS, sector), 0)
     first_half = sub < ROWS // 2
     for side, (start, block, stage) in enumerate(zip(starts, blocks, stages)):
-        tail = (lax.axis_index("radius") == 0) if sides == 1 else side == 0
+        tail = (lax.axis_index("radius") == 0) if sides == 1 else side == 1
         base = 2 * layers
         for j in range(layers // 2):
             one, two = stage[2 * j], stage[2 * j + 1]
@@ -140,29 +147,6 @@
         copy.wait()
 
 
-class Window:
-    def __init__(self, sides, band):
-        r, bands = lax.axis_index("radius"), lax.axis_size("radius")
-        self.band, self.rows = band, band + 2 * ROWS
-        self.own = slice(ROWS, ROWS + band)
-        self.ends = (
-            (slice(0, ROWS), 0, r > 0),
-            (slice(ROWS + band, self.rows), sides - 1, r < bands - 1),
-        )
-
-    def pieces(self, own, outer):
-        yield self.own, own()
-        for at, side, has in self.ends:
-            yield at, jnp.where(has, outer(side), 0.0)
-
-    def of_halo(self, ref, index):
-        band = self.band
-        return self.pieces(
-            lambda: ref[index, 0:band],
-            lambda side: ref[index, band + side * ROWS : band + (side + 1) * ROWS],
-        )
-
-
 def coupling_rows(z, ex, z_up, z_down, geo, alive, tiles, sub, put):
     for t, at, e, e_up, e_down in row_tiles(lambda s: ex(z, s), tiles, sub):
         not_last, not_first = geo[4, at], geo[5, at]
@@ -170,43 +154,51 @@
         inv_r2 = geo[2, at]
         zu = e + ex(z_up, at)
         zd = e + ex(z_down, at)
-        ru = (e + e_up) * geo[0, at]
-        rd = (e + e_down) * geo[1, at]
+        has_up, has_down = geo[8, at], geo[9, at]
+        ru = (e + e_up * has_up) * geo[0, at]
+        rd = (e + e_down * has_down) * geo[1, at]
         au = (e + right * not_last) * inv_r2
         ad = (e + left * not_first) * inv_r2
         diag = ((zu + zd) + (ru + rd)) + (au + ad)
         inv = jnp.where(geo[3, at] * alive > 0, 1.0 / diag, 0.0)
-        put(at, (zu * inv, zd * inv, ru * inv, rd * inv, au * inv * not_last, ad * inv * not_first), inv + inv)
+        radials = (ru * inv * has_up, rd * inv * has_down)
+        put(at, (zu * inv, zd * inv, *radials, au * inv * not_last, ad * inv * not_first), inv + inv)
 
 
 def inner_coupling_kernel(sides, phi, eps, pads, *refs):
     raws, (p0, ex, w, inv2, geo) = refs[:sides], refs[sides:]
     layers, band, sector = phi.shape
-    win = Window(sides, band)
-    rows, tiles = win.rows, win.rows // ROWS
+    tiles = p0.shape[1] // ROWS
     r, bands = lax.axis_index("radius"), lax.axis_size("radius")
     total_r = band * bands
     sub = lax.broadcasted_iota(jnp.int32, (ROWS, sector), 0)
-
-    row = lax.broadcasted_iota(jnp.int32, (rows, sector), 0) - ROWS + r * band
-    lane = lax.broadcasted_iota(jnp.int32, (rows, sector), 1)
-    rpos = ((total_r + row).astype(F32) + 0.5) / total_r
+    lane = lax.broadcasted_iota(jnp.int32, (ROWS, sector), 1)
     half = 0.5 / total_r
-    geo[0] = (rpos + half) / rpos
-    geo[1] = (rpos - half) / rpos
-    geo[2] = 1.0 / (rpos * rpos)
-    geo[3] = jnp.where((row >= 0) & (row < total_r), 1.0, 0.0)
-    geo[4] = jnp.where(lane == sector - 1, 0.0, 1.0)
-    geo[5] = jnp.where(lane == 0, 0.0, 1.0)
+
+    for t, first in enumerate(window_rows(sides, band)):
+        at = slice(t * ROWS, (t + 1) * ROWS)
+        row = sub + (r * band + first)
+        rpos = ((total_r + row).astype(F32) + 0.5) / total_r
+        geo[0, at] = (rpos + half) / rpos
+        geo[1, at] = (rpos - half) / rpos
+        geo[2, at] = 1.0 / (rpos * rpos)
+        geo[3, at] = jnp.where((row >= 0) & (row < total_r), 1.0, 0.0)
+        geo[4, at] = jnp.where(lane == sector - 1, 0.0, 1.0)
+        geo[5, at] = jnp.where(lane == 0, 0.0, 1.0)
+        geo[8, at] = jnp.where(row == total_r - 1, 0.0, 1.0)
+        geo[9, at] = jnp.where(row == 0, 0.0, 1.0)
+    first_pads = 2 * layers + layers // 2 + 2 * (SWEEPS - 1)
     for k in range(2):
-        for at, value in win.pieces(lambda k=k: pads[k], lambda side, k=k: raws[side][2 * layers + layers // 2 + 2 * (SWEEPS - 1) + k]):
-            geo[6 + k, at] = value
+        geo[6 + k, 0:band] = pads[k]
+        for side, raw in enumerate(raws):
+            geo[6 + k, band + side * ROWS : band + (side + 1) * ROWS] = raw[first_pads + k]
 
     @pl.loop(0, layers)
     def _(z):
         for dst, src, base in ((p0, phi, 0), (ex, eps, layers)):
-            for at, value in win.pieces(lambda: src[z], lambda side: raws[side][base + z]):
-                dst[z, at] = value
+            dst[z, 0:band] = src[z]
+            for side, raw in enumerate(raws):
+                dst[z, band + side * ROWS : band + (side + 1) * ROWS] = raw[base + z]
 
     @pl.loop(1, layers - 1)
     def _(z):
@@ -232,8 +224,7 @@
     charge_out, swap, window_out, sums_out, state, b_out, p1, p2, p3, b, raw = refs[sides:]
     layers, band, sector = moved.shape
     depth = SWEEPS
-    win = Window(sides, band)
-    tiles = win.rows // ROWS
+    tiles = p0.shape[1] // ROWS
     d = lax.axis_index("drift")
     sub = lax.broadcasted_iota(jnp.int32, (ROWS, sector), 0)
     phis = (p0, p1, p2, p3)
@@ -242,20 +233,22 @@
     def _(j):
         for half in range(2):
             z = 2 * j + half
-            inner = (z > 0) & (z < layers - 1)
-            for at, side, has in ((win.own, None, None), *win.ends):
-                if side is None:
-                    ions = moved[z]
-                else:
-                    ions = rows_moved[side][j]
-                    if half == (0 if at is win.ends[0][0] else 1):
-                        ions = roll(ions, ROWS // 2, 0)
-                    ions = jnp.where(has, ions, 0.0)
+            inside = (z > 0) & (z < layers - 1)
+
+            def put(at, ions, z=z, inside=inside):
                 value = drift_charge(ions, geo[6, at], geo[7, at], d)
-                if side is None:
-                    charge_out[z] = value
                 raw[z, at] = value
-                b[z, at] = jnp.where(inner, value * inv2[z, at], value)
+                b[z, at] = jnp.where(inside, value * inv2[z, at], value)
+
+            own = slice(0, band)
+            put(own, moved[z])
+            charge_out[z] = raw[z, own]
+            for side, packed in enumerate(rows_moved):
+                above = (lax.axis_index("radius") == 0) if sides == 1 else side == 0
+                two = packed[j]
+                turned = roll(two, ROWS // 2, 0)
+                ions = jnp.where(above, two, turned) if half == 0 else jnp.where(above, turned, two)
+                put(slice(band + side * ROWS, band + (side + 1) * ROWS), ions)
 
     odd = lax.rem(d, 2) == 1
     for k in range(depth - 1):
@@ -295,13 +288,11 @@
         b_out[1, k] = b[layers - depth + k]
 
 
-def outer_relax_kernel(sides, inner, outer, far, swapped, p0, ex, w, geo, state, b_in, sums_in, *refs):
+def outer_relax_kernel(inner, outer, far, swapped, p0, ex, w, geo, state, b_in, sums_in, *refs):
     low_out, high_out, sums_out, ph, eh, wb, bb, q = refs
     layers, rows, sector = p0.shape
     depth, n = SWEEPS, layers
     zs = n + 2 * depth
-    band = rows - 2 * ROWS
-    win = Window(sides, band)
     tiles = rows // ROWS
     d, drifts = lax.axis_index("drift"), lax.axis_size("drift")
     sub = lax.broadcasted_iota(jnp.int32, (ROWS, sector), 0)
@@ -309,19 +300,17 @@
     odd = lax.rem(d, 2) == 1
     for k in range(depth):
         for ref, half, to in ((ph, 0, (k, k)), (eh, depth, (k, 2 + k))):
-            for (at, one), (_, two) in zip(win.of_halo(inner, half + k), win.of_halo(outer, half + k)):
-                ref[0, to[0], at] = jnp.where(odd, one, two)
-                ref[1, to[1], at] = jnp.where(odd, two, one)
+            one, two = inner[half + k], outer[half + k]
+            ref[0, to[0]] = jnp.where(odd, one, two)
+            ref[1, to[1]] = jnp.where(odd, two, one)
     for k in range(2):
         eh[0, depth + k] = ex[k]
         eh[1, k] = ex[n - 2 + k]
 
     for k in range(depth - 1):
-        for (at, near_ions), (_, far_ions) in zip(win.of_halo(inner, 2 * depth + k), win.of_halo(far, k)):
-            rec, inj = geo[6, at], geo[7, at]
-            ready = swapped[k, at]
-            bb[0, k, at] = jnp.where(odd, ready, drift_charge(far_ions, rec, inj, d - 1))
-            bb[1, k + 1, at] = jnp.where(odd, drift_charge(near_ions, rec, inj, d + 1), ready)
+        rec, inj, ready = geo[6], geo[7], swapped[k]
+        bb[0, k] = jnp.where(odd, ready, drift_charge(far[k], rec, inj, d - 1))
+        bb[1, k + 1] = jnp.where(odd, drift_charge(inner[2 * depth + k], rec, inj, d + 1), ready)
     bb[0, depth - 1] = b_in[0, 0]
     bb[1, 0] = b_in[1, depth - 1]
     for side in range(2):
@@ -379,8 +368,7 @@
 
 def local_kernel(low, inner, high, potential, out, run):
     _, band, _ = potential.shape
-    rows = band + 2 * ROWS
-    tiles = rows // ROWS
+    tiles = run.shape[0] // ROWS
     run[...] = jnp.zeros_like(run)
     base = 0
     for window in (low, inner, high):
@@ -391,36 +379,36 @@
                 at = slice(t * ROWS, (t + 1) * ROWS)
                 value = window[k, at]
                 run[at] += value
-                if 0 < t < tiles - 1:
-                    potential[base + k, (t - 1) * ROWS : t * ROWS] = value
+                if t < band // ROWS:
+                    potential[base + k, at] = value
 
             def put(at, first, second):
                 out[0, base + k, at] = first
                 out[1, base + k, at] = second
 
-            ratios_of(run, put)
+            ratios_of(run, band, put)
 
         base += window.shape[0]
 
 
-def ratios_of(field, put):
+def ratios_of(field, band, put):
     rows, sector = field.shape
-    band = rows - 2 * ROWS
     r, bands = lax.axis_index("radius"), lax.axis_size("radius")
     total_r = band * bands
-    tiles = rows // ROWS
     sub = lax.broadcasted_iota(jnp.int32, (ROWS, sector), 0)
     lane = lax.broadcasted_iota(jnp.int32, (ROWS, sector), 1)
     scale = 1.0 / (8.0 * 1.09)
-    for t, at, x, higher, lower in row_tiles(lambda s: field[s], tiles, sub):
-        if 0 < t < tiles - 1:
-            row = sub + ((t - 1) * ROWS + r * band)
+    for t, at, x, higher, lower in row_tiles(lambda s: field[s], rows // ROWS, sub):
+        if t < band // ROWS:
+            row = sub + (t * ROWS + r * band)
             rpos = ((total_r + row).astype(F32) + 0.5) / total_r
             right = jnp.where(lane == sector - 1, 0.0, roll(x, -1, 1))
             left = jnp.where(lane == 0, 0.0, roll(x, 1, 1))
+            higher = jnp.where(row == total_r - 1, 0.0, higher)
+            lower = jnp.where(row == 0, 0.0, lower)
             er = (lower - higher) * (0.5 * scale)
             ea = (left - right) * (0.5 * scale / rpos)
-            put(slice((t - 1) * ROWS, t * ROWS), er + 0.3 * ea, ea - 0.3 * er)
+            put(at, er + 0.3 * ea, ea - 0.3 * er)
 
 
 def offset_kernel(local, prefix, out, shift, stage, sems):
@@ -431,7 +419,7 @@
         shift[0, at] = first
         shift[1, at] = second
 
-    ratios_of(prefix, put)
+    ratios_of(prefix, local.shape[2], put)
     parts = sems.shape[0]
     each = layers // parts
     for k in range(parts):
@@ -471,10 +459,9 @@
 
 def body(ions, potential_guess, permittivity, recombination, rate_index, gap_mask, rate_table):
     layers, band, sector = ions.shape
-    rows = band + 2 * ROWS
     depth = SWEEPS
     sides = 1 if lax.axis_size("radius") == 2 else 2
-    sent = band + sides * ROWS
+    rows = band + sides * ROWS
     dma = pltpu.SemaphoreType.DMA
     ends = depth - 1
     row_block = 2 * layers + layers // 2 + 2 * ends + 2
@@ -500,10 +487,10 @@
     if sides == 1:
         raws = [lax.ppermute(blocks[0], "radius", [(0, 1), (1, 0)])]
     else:
-        raws = [shifted(blocks[0], "radius", 1), shifted(blocks[1], "radius", -1)]
+        raws = [shifted(blocks[0], "radius", -1), shifted(blocks[1], "radius", 1)]
     to_core, to_chip, beyond = kernel(
         functools.partial(halo_kernel, sides),
-        [plane(3 * depth - 1, sent, sector), plane(2 * depth, sent, sector), plane(depth - 1, sent, sector)],
+        [plane(3 * depth - 1, rows, sector), plane(2 * depth, rows, sector), plane(depth - 1, rows, sector)],
         [ANYWHERE] * 3 + [IN_VMEM] * sides,
         scratch=[dma((6 * (1 + sides),))],
         mb=6,
@@ -520,7 +507,7 @@
     box = plane(layers, rows, sector)
     p0, ex, w, inv2, geo = kernel(
         functools.partial(inner_coupling_kernel, sides),
-        [box, box, plane(6, layers, rows, sector), box, plane(8, rows, sector)],
+        [box, box, plane(6, layers, rows, sector), box, plane(10, rows, sector)],
         [IN_VMEM] * (3 + sides),
         mb=20,
     )(potential_guess, permittivity, pads, *raws)
@@ -541,7 +528,7 @@
     )(moved, p0, w, inv2, geo, *rows_moved)
     swapped = lax.ppermute(swap, "drift", partners)
     low, high, sums = kernel(
-        functools.partial(outer_relax_kernel, sides),
+        outer_relax_kernel,
         [plane(depth, rows, sector), plane(depth, rows, sector), plane(rows, sector)],
         [IN_VMEM] * 11,
         scratch=[

time: 76 us -> 69.3 us (0.912)
  starting transfers between devices: 31.8 us -> 25.5 us
    ppermute x4, starting transfers between devices: 13.3 us -> 6.99 us  [sums_below(): other = lax.ppermute(total, 'drift', [(i, i ^ step) for i in range(count)])]
  transfers between devices with their start and end apart: 11 -> 11, of which waited for: 6 -> 6; matrix products, arithmetic and copies ran while one was open for 0% -> 0% of each run, Pallas kernels for 17% -> 18%
where the time goes in v4:
time: 69.3 us; the launch traced here: 69.1 us
  waiting for transfers between devices  25.8 us (37%)
  starting transfers between devices  25.5 us (37%)
  Pallas kernels  17 us (25%)
  between operations  0.76 us (1%)
    ppermute x2, starting transfers between devices, shifted(): return lax.ppermute(block, axis, route)  10.2 us
    ppermute x2, waiting for transfers between devices, shifted(): return lax.ppermute(block, axis, route)  9.09 us
    ppermute x1, waiting for transfers between devices, body(): raws = [lax.ppermute(blocks[0], 'radius', [(0, 1), (1, 0)])]  9.05 us
    ppermute x4, starting transfers between devices, sums_below(): other = lax.ppermute(total, 'drift', [(i, i ^ step) for i in range(count)])  6.99 us
    ppermute x4, waiting for transfers between devices, sums_below(): other = lax.ppermute(total, 'drift', [(i, i ^ step) for i in range(count)])  6.52 us
    ppermute x1, starting transfers between devices, body(): swapped = lax.ppermute(swap, 'drift', partners)  5.31 us
    pallas_call x1, Pallas kernels, body(): kernel(functools.partial(inner_relax_kernel, sides), [plane(layers, band,...  4.78 us
    pallas_call x1, Pallas kernels, body(): kernel(outer_relax_kernel, [plane(depth, rows, sector), plane(depth, rows...  3.14 us
  transfers between devices with their start and end apart: 11, of which 6 were waited for; matrix products, arithmetic and copies ran while one was open for 0% of the time, Pallas kernels for 18%

profile of v4, /device:TPU:0, one launch (start us, length us, event | category | flops | bytes accessed | tf_op | source)
XLA Modules:
  0.0 69.1 jit_solution(7722118948614920985)
XLA Ops:
  0.6 4.9 %collective-permute-start = (f32[16,64,256]{2,1,0:T(8,128)}, f32[16,64,256]{2,1,0:T(8,128)S(1)}, u32[]{:S(2)}, u32[]{:S(2)}) collective-permute-start(f32[16,64,256]{2,1,0:T(8,128)} %ions.3), channel_id=1, source_target_pairs={{0,4},{2,6},{4,8},{6,10},{8,12},{10,14},{12,16},{14,18},{16,20},{1... | collective-permute-start | bytes 3145736 | tf_op jit(solution)/shard_map/ppermute | solution.py:32
  5.6 1.2 %shard_map.94 = (f32[48,8,256]{2,1,0:T(8,128)S(1)}, f32[2,64,256]{2,1,0:T(8,128)S(1)}) custom-call(f32[16,64,256]{2,1,0:T(8,128)} %phi.5, f32[16,64,256]{2,1,0:T(8,128)} %eps.5, f32[16,64,256]{2,1,0:T(8,128)} %ions.3, f32[64,256]{1,0:T(8,128)} %rec.1, s32[64,256]{1,0:T(8,128)} %index.1, s32[64,256]{1,0:T(8,128)} %gap.1, f32[16]{0:T(128)} %table.1), custom_call_target="tpu_custom_call" | custom-call | tf_op jit(solution)/shard_map/pallas_call | solution.py:472
  6.8 1.6 %collective-permute-start.1 = (f32[48,8,256]{2,1,0:T(8,128)S(1)}, f32[48,8,256]{2,1,0:T(8,128)S(1)}, u32[]{:S(2)}, u32[]{:S(2)}) collective-permute-start(f32[48,8,256]{2,1,0:T(8,128)S(1)} %get-tuple-element.25), channel_id=1, source_target_pairs={{0,1},{1,0},{2,3},{3,2},{4,5},{5,4},{6,7},{7,6},{8,9},{9,8},{10,11... | collective-permute-start | bytes 1179656 | tf_op jit(solution)/shard_map/ppermute | solution.py:488
  8.4 9.1 %collective-permute-done.1.refs_0_ = f32[48,8,256]{2,1,0:T(8,128)S(1)} collective-permute-done((f32[48,8,256]{2,1,0:T(8,128)S(1)}, f32[48,8,256]{2,1,0:T(8,128)S(1)}, u32[]{:S(2)}, u32[]{:S(2)}) %collective-permute-start.1) | collective-permute-done | bytes 393248 | tf_op jit(solution)/shard_map/ppermute | solution.py:488
  17.5 1.4 %shard_map.97 = (f32[11,72,256]{2,1,0:T(8,128)S(1)}, f32[8,72,256]{2,1,0:T(8,128)S(1)}, f32[3,72,256]{2,1,0:T(8,128)S(1)}) custom-call(f32[16,64,256]{2,1,0:T(8,128)} %phi.5, f32[16,64,256]{2,1,0:T(8,128)} %eps.5, f32[16,64,256]{2,1,0:T(8,128)} %ions.3, f32[48,8,256]{2,1,0:T(8,128)S(1)} %collective-permute-done.1.refs_0_), custom_call_target="tpu_custom_call" | custom-call | tf_op jit(solution)/shard_map/pallas_call | solution.py:491
  18.9 0.1 collective-permute-start.3
  19.0 0.7 %collective-permute-start.4 = (f32[8,72,256]{2,1,0:T(8,128)S(1)}, f32[8,72,256]{2,1,0:T(8,128)S(1)}, u32[]{:S(2)}, u32[]{:S(2)}) collective-permute-start(f32[8,72,256]{2,1,0:T(8,128)S(1)} %get-tuple-element.32), channel_id=1, source_target_pairs={{2,4},{4,2},{6,8},{8,6},{10,12},{12,10},{14,16},{16,14},{18,20},{2... | collective-permute-start | bytes 1769480 | tf_op jit(solution)/shard_map/ppermute | solution.py:503
  19.7 5.2 %collective-permute-start.2 = (f32[8,8,256]{2,1,0:T(8,128)S(1)}, f32[8,8,256]{2,1,0:T(8,128)S(1)}, u32[]{:S(2)}, u32[]{:S(2)}) collective-permute-start(f32[8,8,256]{2,1,0:T(8,128)S(1)} %slice.4), channel_id=1, source_target_pairs={{0,4},{2,6},{4,8},{6,10},{8,12},{10,14},{12,16},{14,18},{16,20},{1... | collective-permute-start | bytes 196616 | tf_op jit(solution)/shard_map/ppermute | solution.py:32
  24.9 0.7 collective-permute-start.5
  25.6 2.2 %shard_map.95 = (f32[16,72,256]{2,1,0:T(8,128)S(1)}, f32[16,72,256]{2,1,0:T(8,128)S(1)}, f32[6,16,72,256]{3,2,1,0:T(8,128)S(1)}, f32[16,72,256]{2,1,0:T(8,128)S(1)}, f32[10,72,256]{2,1,0:T(8,128)S(1)}) custom-call(f32[16,64,256]{2,1,0:T(8,128)S(1)} %copy-done, f32[16,64,256]{2,1,0:T(8,128)S(1)} %copy-done.1, f32[2,64,256]{2,1,0:T(8,128)S(1)} %get-tuple-element.24.pads, ...), custom_call_target="tpu_custom_call" | custom-call | tf_op jit(solution)/shard_map/pallas_call | solution.py:508
  27.9 9.1 %collective-permute-done.2.refs_0_ = f32[8,8,256]{2,1,0:T(8,128)S(1)} collective-permute-done((f32[8,8,256]{2,1,0:T(8,128)S(1)}, f32[8,8,256]{2,1,0:T(8,128)S(1)}, u32[]{:S(2)}, u32[]{:S(2)}) %collective-permute-start.2) | collective-permute-done | bytes 65568 | tf_op jit(solution)/shard_map/ppermute | solution.py:32
  37.0 4.8 %shard_map.96 = (f32[16,64,256]{2,1,0:T(8,128)}, f32[3,72,256]{2,1,0:T(8,128)S(1)}, f32[8,72,256]{2,1,0:T(8,128)S(1)}, f32[72,256]{1,0:T(8,128)S(1)}, f32[2,3,2,...) custom-call(f32[16,64,256]{2,1,0:T(8,128)S(1)} %collective-permute-done.moved, ...), custom_call_target="tpu_custom_call" | custom-call | tf_op jit(solution)/shard_map/pallas_call | solution.py:515
  41.8 5.3 %collective-permute-start.6 = (f32[3,72,256]{2,1,0:T(8,128)S(1)}, f32[3,72,256]{2,1,0:T(8,128)S(1)}, u32[]{:S(2)}, u32[]{:S(2)}) collective-permute-start(f32[3,72,256]{2,1,0:T(8,128)S(1)} %get-tuple-element.34), channel_id=1, source_target_pairs={{0,2},{2,0},{4,6},{6,4},{8,10},{10,8},{12,14},{14,12},{16,18},{18,... | collective-permute-start | bytes 663560 | tf_op jit(solution)/shard_map/ppermute | solution.py:529
  47.1 1.1 %collective-permute-done.6.swapped = f32[3,72,256]{2,1,0:T(8,128)S(1)} collective-permute-done((f32[3,72,256]{2,1,0:T(8,128)S(1)}, f32[3,72,256]{2,1,0:T(8,128)S(1)}, u32[]{:S(2)}, u32[]{:S(2)}) %collective-permute-start.6) | collective-permute-done | bytes 221216 | tf_op jit(solution)/shard_map/ppermute | solution.py:529
  48.2 3.1 %shard_map.98 = (f32[4,72,256]{2,1,0:T(8,128)S(1)}, f32[4,72,256]{2,1,0:T(8,128)S(1)}, f32[72,256]{1,0:T(8,128)S(1)}) custom-call(f32[11,72,256]{2,1,0:T(8,128)S(1)} %collective-permute-done.3.inner, f32[8,72,256]{2,1,0:T(8,128)S(1)} %collective-permute-done.4.outer, f32[3,72,256]{2,1,0:T(8,128)S(1)} %collective-permute-done.5.far, ...), custom_call_target="tpu_custom_call" | custom-call | tf_op jit(solution)/shard_map/pallas_call | solution.py:530
  51.3 0.4 collective-permute-start.7
  51.8 0.9 %collective-permute-done.7 = f32[72,256]{1,0:T(8,128)S(1)} collective-permute-done((f32[72,256]{1,0:T(8,128)S(1)}, f32[72,256]{1,0:T(8,128)S(1)}, u32[]{:S(2)}, u32[]{:S(2)}) %collective-permute-start.7) | collective-permute-done | bytes 73760 | tf_op jit(solution)/shard_map/ppermute | solution.py:442
  52.7 2.3 %collective-permute-start.8 = (f32[72,256]{1,0:T(8,128)S(1)}, f32[72,256]{1,0:T(8,128)S(1)}, u32[]{:S(2)}, u32[]{:S(2)}) collective-permute-start(f32[72,256]{1,0:T(8,128)S(1)} %add.18), channel_id=1, source_target_pairs={{0,4},{2,6},{4,0},{6,2},{8,12},{10,14},{12,8},{14,10},{16,20},{18,... | collective-permute-start | bytes 221192 | tf_op jit(solution)/shard_map/ppermute | solution.py:442
  54.9 2.8 %collective-permute-done.8 = f32[72,256]{1,0:T(8,128)S(1)} collective-permute-done((f32[72,256]{1,0:T(8,128)S(1)}, f32[72,256]{1,0:T(8,128)S(1)}, u32[]{:S(2)}, u32[]{:S(2)}) %collective-permute-start.8) | collective-permute-done | bytes 73760 | tf_op jit(solution)/shard_map/ppermute | solution.py:442
  57.7 1.6 %collective-permute-start.9 = (f32[72,256]{1,0:T(8,128)S(1)}, f32[72,256]{1,0:T(8,128)S(1)}, u32[]{:S(2)}, u32[]{:S(2)}) collective-permute-start(f32[72,256]{1,0:T(8,128)S(1)} %add.20), channel_id=1, source_target_pairs={{0,8},{2,10},{4,12},{6,14},{8,0},{10,2},{12,4},{14,6},{16,24},{18,... | collective-permute-start | bytes 221192 | tf_op jit(solution)/shard_map/ppermute | solution.py:442
  59.4 2.8 %collective-permute-done.9 = f32[72,256]{1,0:T(8,128)S(1)} collective-permute-done((f32[72,256]{1,0:T(8,128)S(1)}, f32[72,256]{1,0:T(8,128)S(1)}, u32[]{:S(2)}, u32[]{:S(2)}) %collective-permute-start.9) | collective-permute-done | bytes 73760 | tf_op jit(solution)/shard_map/ppermute | solution.py:442
  62.2 2.7 %collective-permute-start.10 = (f32[72,256]{1,0:T(8,128)S(1)}, f32[72,256]{1,0:T(8,128)S(1)}, u32[]{:S(2)}, u32[]{:S(2)}) collective-permute-start(f32[72,256]{1,0:T(8,128)S(1)} %add.22), channel_id=1, source_target_pairs={{0,16},{2,18},{4,20},{6,22},{8,24},{10,26},{12,28},{14,30},{16,0},... | collective-permute-start | bytes 221192 | tf_op jit(solution)/shard_map/ppermute | solution.py:442
  64.8 2.6 %shard_map.99 = (f32[16,64,256]{2,1,0:T(8,128)}, f32[2,16,64,256]{3,2,1,0:T(8,128)S(1)}) custom-call(f32[4,72,256]{2,1,0:T(8,128)S(1)} %get-tuple-element.39.low, f32[8,72,256]{2,1,0:T(8,128)S(1)} %get-tuple-element.40.inner, f32[4,72,256]{2,1,0:T(8,128)S(1)} %get-tuple-element.41.high), custom_call_target="tpu_custom_call" | custom-call | tf_op jit(solution)/shard_map/pallas_call | solution.py:543
  67.5 1.6 %shard_map.100 = f32[2,16,64,256]{3,2,1,0:T(8,128)} custom-call(f32[2,16,64,256]{3,2,1,0:T(8,128)S(1)} %get-tuple-element.43.local, f32[72,256]{1,0:T(8,128)S(1)} %select_add_fusion.prefix), custom_call_target="tpu_custom_call" | custom-call | tf_op jit(solution)/shard_map/pallas_call | solution.py:551
  (14 shorter events, 0.1 us)
Async XLA Ops:
  0.6 36.3 %collective-permute-start = (f32[16,64,256]{2,1,0:T(8,128)}, f32[16,64,256]{2,1,0:T(8,128)S(1)}, u32[]{:S(2)}, u32[]{:S(2)}) collective-permute-start(f32[16,64,256]{2,1,0:T(8,128)} %ions.3), channel_id=1, source_target_pairs={{0,4},{2,6},{4,8},{6,10},{8,12},{10,14},{12,16},{14,18},{16,20},{1... | collective-permute-start | bytes 3145736 | tf_op jit(solution)/shard_map/ppermute | solution.py:32
  6.8 18.8 %copy-start = (f32[16,64,256]{2,1,0:T(8,128)S(1)}, f32[16,64,256]{2,1,0:T(8,128)}, u32[]{:S(2)}) copy-start(f32[16,64,256]{2,1,0:T(8,128)} %phi.5) | copy-start | bytes 3145732
  6.8 18.8 %copy-start.1 = (f32[16,64,256]{2,1,0:T(8,128)S(1)}, f32[16,64,256]{2,1,0:T(8,128)}, u32[]{:S(2)}) copy-start(f32[16,64,256]{2,1,0:T(8,128)} %eps.5) | copy-start | bytes 3145732
  6.8 10.6 %collective-permute-start.1 = (f32[48,8,256]{2,1,0:T(8,128)S(1)}, f32[48,8,256]{2,1,0:T(8,128)S(1)}, u32[]{:S(2)}, u32[]{:S(2)}) collective-permute-start(f32[48,8,256]{2,1,0:T(8,128)S(1)} %get-tuple-element.25), channel_id=1, source_target_pairs={{0,1},{1,0},{2,3},{3,2},{4,5},{5,4},{6,7},{7,6},{8,9},{9,8},{10,11... | collective-permute-start | bytes 1179656 | tf_op jit(solution)/shard_map/ppermute | solution.py:488
  18.9 28.2 %collective-permute-start.3 = (f32[11,72,256]{2,1,0:T(8,128)S(1)}, f32[11,72,256]{2,1,0:T(8,128)S(1)}, u32[]{:S(2)}, u32[]{:S(2)}) collective-permute-start(f32[11,72,256]{2,1,0:T(8,128)S(1)} %get-tuple-element.31), channel_id=1, source_target_pairs={{0,2},{2,0},{4,6},{6,4},{8,10},{10,8},{12,14},{14,12},{16,18},{18,... | collective-permute-start | bytes 2433032 | tf_op jit(solution)/shard_map/ppermute | solution.py:505
  19.0 28.1 %collective-permute-start.4 = (f32[8,72,256]{2,1,0:T(8,128)S(1)}, f32[8,72,256]{2,1,0:T(8,128)S(1)}, u32[]{:S(2)}, u32[]{:S(2)}) collective-permute-start(f32[8,72,256]{2,1,0:T(8,128)S(1)} %get-tuple-element.32), channel_id=1, source_target_pairs={{2,4},{4,2},{6,8},{8,6},{10,12},{12,10},{14,16},{16,14},{18,20},{2... | collective-permute-start | bytes 1769480 | tf_op jit(solution)/shard_map/ppermute | solution.py:503
  19.7 17.3 %collective-permute-start.2 = (f32[8,8,256]{2,1,0:T(8,128)S(1)}, f32[8,8,256]{2,1,0:T(8,128)S(1)}, u32[]{:S(2)}, u32[]{:S(2)}) collective-permute-start(f32[8,8,256]{2,1,0:T(8,128)S(1)} %slice.4), channel_id=1, source_target_pairs={{0,4},{2,6},{4,8},{6,10},{8,12},{10,14},{12,16},{14,18},{16,20},{1... | collective-permute-start | bytes 196616 | tf_op jit(solution)/shard_map/ppermute | solution.py:32
  24.9 22.1 %collective-permute-start.5 = (f32[3,72,256]{2,1,0:T(8,128)S(1)}, f32[3,72,256]{2,1,0:T(8,128)S(1)}, u32[]{:S(2)}, u32[]{:S(2)}) collective-permute-start(f32[3,72,256]{2,1,0:T(8,128)S(1)} %get-tuple-element.33), channel_id=1, source_target_pairs={{2,8},{6,12},{10,16},{14,20},{18,24},{22,28},{3,9},{7,13},{11,17},... | collective-permute-start | bytes 663560 | tf_op jit(solution)/shard_map/ppermute | solution.py:504
  41.8 6.4 %collective-permute-start.6 = (f32[3,72,256]{2,1,0:T(8,128)S(1)}, f32[3,72,256]{2,1,0:T(8,128)S(1)}, u32[]{:S(2)}, u32[]{:S(2)}) collective-permute-start(f32[3,72,256]{2,1,0:T(8,128)S(1)} %get-tuple-element.34), channel_id=1, source_target_pairs={{0,2},{2,0},{4,6},{6,4},{8,10},{10,8},{12,14},{14,12},{16,18},{18,... | collective-permute-start | bytes 663560 | tf_op jit(solution)/shard_map/ppermute | solution.py:529
  51.3 1.4 %collective-permute-start.7 = (f32[72,256]{1,0:T(8,128)S(1)}, f32[72,256]{1,0:T(8,128)S(1)}, u32[]{:S(2)}, u32[]{:S(2)}) collective-permute-start(f32[72,256]{1,0:T(8,128)S(1)} %get-tuple-element.44), channel_id=1, source_target_pairs={{0,2},{2,0},{4,6},{6,4},{8,10},{10,8},{12,14},{14,12},{16,18},{18,... | collective-permute-start | bytes 221192 | tf_op jit(solution)/shard_map/ppermute | solution.py:442
  52.7 5.0 %collective-permute-start.8 = (f32[72,256]{1,0:T(8,128)S(1)}, f32[72,256]{1,0:T(8,128)S(1)}, u32[]{:S(2)}, u32[]{:S(2)}) collective-permute-start(f32[72,256]{1,0:T(8,128)S(1)} %add.18), channel_id=1, source_target_pairs={{0,4},{2,6},{4,0},{6,2},{8,12},{10,14},{12,8},{14,10},{16,20},{18,... | collective-permute-start | bytes 221192 | tf_op jit(solution)/shard_map/ppermute | solution.py:442
  57.7 4.4 %collective-permute-start.9 = (f32[72,256]{1,0:T(8,128)S(1)}, f32[72,256]{1,0:T(8,128)S(1)}, u32[]{:S(2)}, u32[]{:S(2)}) collective-permute-start(f32[72,256]{1,0:T(8,128)S(1)} %add.20), channel_id=1, source_target_pairs={{0,8},{2,10},{4,12},{6,14},{8,0},{10,2},{12,4},{14,6},{16,24},{18,... | collective-permute-start | bytes 221192 | tf_op jit(solution)/shard_map/ppermute | solution.py:442
  62.2 5.3 %collective-permute-start.10 = (f32[72,256]{1,0:T(8,128)S(1)}, f32[72,256]{1,0:T(8,128)S(1)}, u32[]{:S(2)}, u32[]{:S(2)}) collective-permute-start(f32[72,256]{1,0:T(8,128)S(1)} %add.22), channel_id=1, source_target_pairs={{0,16},{2,18},{4,20},{6,22},{8,24},{10,26},{12,28},{14,30},{16,0},... | collective-permute-start | bytes 221192 | tf_op jit(solution)/shard_map/ppermute | solution.py:442

commit v5 on v4

--- a/solution.py
+++ b/solution.py
@@ -32,13 +32,10 @@
     return lax.ppermute(block, axis, route)
 
 
-def transit(slab, rec, inj):
-    return slab / (1.0 + rec * slab) + inj
-
-
 def drift_charge(ions, rec, inj, slab):
-    once = transit(ions, rec, inj)
-    return transit(jnp.where(slab >= 1, once, 0.0), rec, inj)
+    below = 1.0 + rec * ions
+    above = jnp.where(slab >= 1, ions + inj * below, 0.0)
+    return above / (below + rec * above) + inj
 
 
 def roll(x, amount, axis):
@@ -75,19 +72,37 @@
     return [*own, band, -ROWS]
 
 
+def ion_rows_kernel(ions, *rest):
+    sides = (len(rest) - 1) // 2
+    blocks, stages, sems = rest[:sides], rest[sides : 2 * sides], rest[-1]
+    layers, band, sector = ions.shape
+    starts = sides_of(sides, band)
+    for copy in run_all([(ions.at[:, pl.ds(start, ROWS)], stage) for start, stage in zip(starts, stages)], sems):
+        copy.wait()
+    first_half = lax.broadcasted_iota(jnp.int32, (ROWS, sector), 0) < ROWS // 2
+    for side, (block, stage) in enumerate(zip(blocks, stages)):
+        tail = (lax.axis_index("radius") == 0) if sides == 1 else side == 1
+        for j in range(layers // 2):
+            one, two = stage[2 * j], stage[2 * j + 1]
+            from_tail = jnp.where(first_half, roll(one, ROWS // 2, 0), two)
+            from_head = jnp.where(first_half, one, roll(two, ROWS // 2, 0))
+            block[j] = jnp.where(tail, from_tail, from_head)
+
+
 def rows_kernel(phi, eps, ions, rec, index, gap, table, *rest):
-    sides = (len(rest) - 7) // 2
-    blocks, pads, stages = rest[:sides], rest[sides], rest[sides + 1 : 2 * sides + 1]
-    rec_v, index_v, gap_v, table_s, sems, pad_sems = rest[2 * sides + 1 :]
+    sides = len(rest) - 7
+    blocks, pads = rest[:sides], rest[sides]
+    rec_v, index_v, gap_v, table_s, sems, pad_sems = rest[sides + 1 :]
     layers, band, sector = phi.shape
     ends = SWEEPS - 1
     starts = sides_of(sides, band)
     copies = []
-    for start, block, stage in zip(starts, blocks, stages):
+    for start, block in zip(starts, blocks):
         rows = pl.ds(start, ROWS)
         copies.append((phi.at[:, rows], block.at[0:layers]))
         copies.append((eps.at[:, rows], block.at[layers : 2 * layers]))
-        copies.append((ions.at[:, rows], stage))
+        copies.append((ions.at[0:ends, rows], block.at[2 * layers : 2 * layers + ends]))
+        copies.append((ions.at[layers - ends :, rows], block.at[2 * layers + ends : 2 * layers + 2 * ends]))
     running = run_all(copies, sems)
     pad_copies = run_all([(rec, rec_v), (index, index_v), (gap, gap_v), (table, table_s)], pad_sems)
     for copy in pad_copies:
@@ -100,42 +115,28 @@
             picked = jnp.where(which == k, table_s[k], picked)
         pads[0, at] = rec_v[at]
         pads[1, at] = picked * (1 - gap_v[at]).astype(F32)
+    for start, block in zip(starts, blocks):
+        for k in range(2):
+            block[2 * layers + 2 * ends + k] = pads[k, pl.ds(start, ROWS)]
     for copy in running:
         copy.wait()
-    sub = lax.broadcasted_iota(jnp.int32, (ROWS, sector), 0)
-    first_half = sub < ROWS // 2
-    for side, (start, block, stage) in enumerate(zip(starts, blocks, stages)):
-        tail = (lax.axis_index("radius") == 0) if sides == 1 else side == 1
-        base = 2 * layers
-        for j in range(layers // 2):
-            one, two = stage[2 * j], stage[2 * j + 1]
-            from_tail = jnp.where(first_half, roll(one, ROWS // 2, 0), two)
-            from_head = jnp.where(first_half, one, roll(two, ROWS // 2, 0))
-            block[base + j] = jnp.where(tail, from_tail, from_head)
-        base += layers // 2
-        for k in range(ends):
-            block[base + k] = stage[k]
-            block[base + ends + k] = stage[layers - ends + k]
-        base += 2 * ends
-        for k in range(2):
-            block[base + k] = pads[k, pl.ds(start, ROWS)]
 
 
 def halo_kernel(sides, phi, eps, ions, *refs):
-    raws, (inner, outer, far, sems) = refs[:sides], refs[sides:]
+    raws, (inner, outer_eps, outer_phi, far, sems) = refs[:sides], refs[sides:]
     layers, band, _ = phi.shape
     depth = SWEEPS
     odd = lax.rem(lax.axis_index("drift"), 2) == 1
     low, high = 0, layers - depth
     near_at, far_at = jnp.where(odd, low, high), jnp.where(odd, high, low)
-    ends = 2 * layers + layers // 2
+    ends = 2 * layers
     copies = []
     for dst, at, k, start, raw_at, count in (
         (inner, 0, 0, near_at, near_at, depth),
         (inner, depth, 1, near_at, layers + near_at, depth),
         (inner, 2 * depth, 2, 0, ends, depth - 1),
-        (outer, 0, 0, far_at, far_at, depth),
-        (outer, depth, 1, far_at, layers + far_at, depth),
+        (outer_eps, 0, 1, far_at, layers + far_at, depth),
+        (outer_phi, 0, 0, far_at, far_at, depth),
         (far, 0, 2, layers - depth + 1, ends + depth - 1, depth - 1),
     ):
         src = (phi, eps, ions)[k]
@@ -187,7 +188,7 @@
         geo[5, at] = jnp.where(lane == 0, 0.0, 1.0)
         geo[8, at] = jnp.where(row == total_r - 1, 0.0, 1.0)
         geo[9, at] = jnp.where(row == 0, 0.0, 1.0)
-    first_pads = 2 * layers + layers // 2 + 2 * (SWEEPS - 1)
+    first_pads = 2 * layers + 2 * (SWEEPS - 1)
     for k in range(2):
         geo[6 + k, 0:band] = pads[k]
         for side, raw in enumerate(raws):
@@ -219,15 +220,12 @@
         put(at, total)
 
 
-def inner_relax_kernel(sides, moved, p0, w, inv2, geo, *refs):
+def charge_kernel(sides, moved, inv2, geo, *refs):
     rows_moved = refs[:sides]
-    charge_out, swap, window_out, sums_out, state, b_out, p1, p2, p3, b, raw = refs[sides:]
-    layers, band, sector = moved.shape
-    depth = SWEEPS
-    tiles = p0.shape[1] // ROWS
+    raw, swap, b = refs[sides:]
+    layers, band, _ = moved.shape
+    ends = SWEEPS - 1
     d = lax.axis_index("drift")
-    sub = lax.broadcasted_iota(jnp.int32, (ROWS, sector), 0)
-    phis = (p0, p1, p2, p3)
 
     @pl.loop(0, layers // 2)
     def _(j):
@@ -240,9 +238,7 @@
                 raw[z, at] = value
                 b[z, at] = jnp.where(inside, value * inv2[z, at], value)
 
-            own = slice(0, band)
-            put(own, moved[z])
-            charge_out[z] = raw[z, own]
+            put(slice(0, band), moved[z])
             for side, packed in enumerate(rows_moved):
                 above = (lax.axis_index("radius") == 0) if sides == 1 else side == 0
                 two = packed[j]
@@ -251,81 +247,103 @@
                 put(slice(band + side * ROWS, band + (side + 1) * ROWS), ions)
 
     odd = lax.rem(d, 2) == 1
-    for k in range(depth - 1):
-        swap[k] = raw[jnp.where(odd, k, layers - depth + 1 + k)]
+    for k in range(ends):
+        swap[k] = raw[jnp.where(odd, k, layers - ends + k)]
+
+
+def inner_relax_kernel(p0, w, b, raw, charge_out, window_out, sums_out, state, p1, p2, p3, sem):
+    layers, rows, sector = p0.shape
+    charge_copy = pltpu.make_async_copy(raw.at[:, 0 : charge_out.shape[1]], charge_out, sem)
+    charge_copy.start()
+    depth = SWEEPS
+    tiles = rows // ROWS
+    sub = lax.broadcasted_iota(jnp.int32, (ROWS, sector), 0)
+    phis = (p0, p1, p2, p3)
     sums_out[...] = jnp.zeros_like(sums_out)
     for s in range(1, depth + 1):
         src = phis[s - 1]
-
-        @pl.loop(s, layers - s, step=2)
-        def _(first, s=s, src=src):
-            for z in (first, first + 1):
-
-                def put(at, total, z=z):
-                    if s < depth:
-                        phis[s][z, at] = total
-                    else:
-                        window_out[z - depth, at] = total
-                        sums_out[at] += total
-
-                sweep_layer(
-                    lambda at, z=z: src[z, at],
-                    lambda at, z=z: src[z + 1, at],
-                    lambda at, z=z: src[z - 1, at],
-                    lambda k, at, z=z: w[k, z, at],
-                    lambda at, z=z: b[z, at],
-                    tiles,
-                    sub,
-                    put,
-                )
-
-    for s in range(1, depth):
-        for k in range(2):
-            state[0, s - 1, k] = phis[s][s + k]
-            state[1, s - 1, k] = phis[s][layers - s - 2 + k]
+        for z in range(s, layers - s):
+
+            def put(at, total, s=s, z=z):
+                if s < depth:
+                    phis[s][z, at] = total
+                    if z - s < 2:
+                        state[0, s - 1, z - s, at] = total
+                    if z - (layers - s - 2) >= 0:
+                        state[1, s - 1, z - (layers - s - 2), at] = total
+                else:
+                    window_out[z - depth, at] = total
+                    sums_out[at] += total
+
+            sweep_layer(
+                lambda at, z=z, src=src: src[z, at],
+                lambda at, z=z, src=src: src[z + 1, at],
+                lambda at, z=z, src=src: src[z - 1, at],
+                lambda k, at, z=z: w[k, z, at],
+                lambda at, z=z: b[z, at],
+                tiles,
+                sub,
+                put,
+            )
+    charge_copy.wait()
+
+
+def outer_coupling_kernel(inner, outer_eps, far, ex, geo, wb, bb, eh):
+    layers, rows, sector = ex.shape
+    depth, n = SWEEPS, layers
+    tiles = rows // ROWS
+    d, drifts = lax.axis_index("drift"), lax.axis_size("drift")
+    odd = lax.rem(d, 2) == 1
+    sub = lax.broadcasted_iota(jnp.int32, (ROWS, sector), 0)
+
     for k in range(depth):
-        b_out[0, k] = b[k]
-        b_out[1, k] = b[layers - depth + k]
-
-
-def outer_relax_kernel(inner, outer, far, swapped, p0, ex, w, geo, state, b_in, sums_in, *refs):
-    low_out, high_out, sums_out, ph, eh, wb, bb, q = refs
+        one, two = inner[depth + k], outer_eps[k]
+        eh[0, k] = jnp.where(odd, one, two)
+        eh[1, 2 + k] = jnp.where(odd, two, one)
+    for k in range(2):
+        eh[0, depth + k] = ex[k]
+        eh[1, k] = ex[n - 2 + k]
+
+    for k in range(depth - 1):
+        rec, inj = geo[6], geo[7]
+        bb[0, k] = jnp.where(odd, 1.0, drift_charge(far[k], rec, inj, d - 1))
+        bb[1, k + 1] = jnp.where(odd, drift_charge(inner[2 * depth + k], rec, inj, d + 1), 1.0)
+    bb[0, depth - 1] = jnp.ones_like(bb[0, 0])
+    bb[1, 0] = jnp.ones_like(bb[1, 0])
+    for side in range(2):
+
+        @pl.loop(0, depth)
+        def _(k, side=side):
+            zg = d * n - depth + (k + 1 if side == 0 else depth + n - 1 + k)
+            alive = jnp.where((zg >= 0) & (zg < drifts * n), 1.0, 0.0)
+
+            def put(at, values, twice):
+                for j, value in enumerate(values):
+                    wb[j, side, k, at] = value
+                bb[side, k, at] = bb[side, k, at] * twice
+
+            coupling_rows(k + 1, lambda i, s: eh[side, i, s], k + 2, k, geo, alive, tiles, sub, put)
+
+
+def outer_relax_kernel(
+    inner, outer_phi, swapped, p0, w, wb, bb_in, state, b_in, sums_in, low_out, high_out, sums_out, ph, bb, q
+):
     layers, rows, sector = p0.shape
     depth, n = SWEEPS, layers
     zs = n + 2 * depth
     tiles = rows // ROWS
-    d, drifts = lax.axis_index("drift"), lax.axis_size("drift")
+    odd = lax.rem(lax.axis_index("drift"), 2) == 1
     sub = lax.broadcasted_iota(jnp.int32, (ROWS, sector), 0)
-
-    odd = lax.rem(d, 2) == 1
     for k in range(depth):
-        for ref, half, to in ((ph, 0, (k, k)), (eh, depth, (k, 2 + k))):
-            one, two = inner[half + k], outer[half + k]
-            ref[0, to[0]] = jnp.where(odd, one, two)
-            ref[1, to[1]] = jnp.where(odd, two, one)
-    for k in range(2):
-        eh[0, depth + k] = ex[k]
-        eh[1, k] = ex[n - 2 + k]
-
+        one, two = inner[k], outer_phi[k]
+        ph[0, k] = jnp.where(odd, one, two)
+        ph[1, k] = jnp.where(odd, two, one)
     for k in range(depth - 1):
-        rec, inj, ready = geo[6], geo[7], swapped[k]
-        bb[0, k] = jnp.where(odd, ready, drift_charge(far[k], rec, inj, d - 1))
-        bb[1, k + 1] = jnp.where(odd, drift_charge(inner[2 * depth + k], rec, inj, d + 1), ready)
-    bb[0, depth - 1] = b_in[0, 0]
-    bb[1, 0] = b_in[1, depth - 1]
-    for side in range(2):
-
-        @pl.loop(0, depth)
-        def _(k, side=side):
-            zg = d * n - depth + (k + 1 if side == 0 else depth + n - 1 + k)
-            alive = jnp.where((zg >= 0) & (zg < drifts * n), 1.0, 0.0)
-
-            def put(at, values, twice):
-                for j, value in enumerate(values):
-                    wb[j, side, k, at] = value
-                bb[side, k, at] = bb[side, k, at] * twice
-
-            coupling_rows(k + 1, lambda i, s: eh[side, i, s], k + 2, k, geo, alive, tiles, sub, put)
+        ready = swapped[k]
+        bb[0, k] = bb_in[0, k] * jnp.where(odd, ready, 1.0)
+        bb[1, k + 1] = bb_in[1, k + 1] * jnp.where(odd, 1.0, ready)
+    bb[0, depth - 1] = bb_in[0, depth - 1] * b_in[0]
+    bb[1, 0] = bb_in[1, 0] * b_in[n - 1]
 
     def phi_at(s, e):
         if s == 0:
@@ -350,7 +368,7 @@
                 z = e - depth
                 if 0 < z < n - 1:
                     w_at = lambda j, at, z=z: w[j, z, at]
-                    b_at = lambda at, z=z: b_in[0, z, at] if z < n // 2 else b_in[1, z - (n - depth), at]
+                    b_at = lambda at, z=z: b_in[z, at]
                 else:
                     at_layer = e - 1 if side == 0 else e - (zs - depth - 1)
                     w_at = lambda j, at, side=side, i=at_layer: wb[j, side, i, at]
@@ -464,33 +482,44 @@
     rows = band + sides * ROWS
     dma = pltpu.SemaphoreType.DMA
     ends = depth - 1
-    row_block = 2 * layers + layers // 2 + 2 * ends + 2
+    row_block = 2 * layers + 2 * ends + 2
     far_args = (potential_guess, permittivity, ions, recombination, rate_index, gap_mask, rate_table)
     phi, eps, ions_far, *pad_args = [pltpu.with_memory_space_constraint(x, pltpu.HBM) for x in far_args]
 
     moved = shifted(ions, "drift", 2)
+
+    def swap_rows(blocks):
+        if sides == 1:
+            return [lax.ppermute(blocks[0], "radius", [(0, 1), (1, 0)])]
+        return [shifted(blocks[0], "radius", -1), shifted(blocks[1], "radius", 1)]
+
+    ion_blocks = kernel(
+        ion_rows_kernel,
+        [plane(layers // 2, ROWS, sector)] * sides,
+        [ANYWHERE],
+        scratch=[near(layers, ROWS, sector)] * sides + [dma((sides,))],
+        mb=3,
+    )(ions_far)
+    ion_raws = swap_rows(ion_blocks)
     *blocks, pads = kernel(
         rows_kernel,
         [plane(row_block, ROWS, sector)] * sides + [plane(2, band, sector)],
         [ANYWHERE] * 7,
-        scratch=[near(layers, ROWS, sector)] * sides
-        + [
+        scratch=[
             near(band, sector),
             pltpu.VMEM((band, sector), jnp.int32),
             pltpu.VMEM((band, sector), jnp.int32),
             pltpu.SMEM(rate_table.shape, F32),
-            dma((3 * sides,)),
+            dma((4 * sides,)),
             dma((4,)),
         ],
         mb=5,
     )(phi, eps, ions_far, *pad_args)
-    if sides == 1:
-        raws = [lax.ppermute(blocks[0], "radius", [(0, 1), (1, 0)])]
-    else:
-        raws = [shifted(blocks[0], "radius", -1), shifted(blocks[1], "radius", 1)]
-    to_core, to_chip, beyond = kernel(
+    raws = swap_rows(blocks)
+    rows_moved = [shifted(raw, "drift", 2) for raw in ion_raws]
+    to_core, eps_block, phi_block, beyond = kernel(
         functools.partial(halo_kernel, sides),
-        [plane(3 * depth - 1, rows, sector), plane(2 * depth, rows, sector), plane(depth - 1, rows, sector)],
+        [plane(k, rows, sector) for k in (3 * depth - 1, depth, depth, depth - 1)],
         [ANYWHERE] * 3 + [IN_VMEM] * sides,
         scratch=[dma((6 * (1 + sides),))],
         mb=6,
@@ -499,10 +528,10 @@
     assert count % 2 == 0
     partners = [(i, i ^ 1) for i in range(count)]
     chips = [(i, i + 1 if i % 2 else i - 1) for i in range(1, count - 1)]
-    rows_moved = [shifted(raw[2 * layers : 2 * layers + layers // 2], "drift", 2) for raw in raws]
-    outer = lax.ppermute(to_chip, "drift", chips)
+    outer_eps = lax.ppermute(eps_block, "drift", chips)
     far = lax.ppermute(beyond, "drift", [(i - 3, i) for i in range(4, count, 2)])
     inner = lax.ppermute(to_core, "drift", partners)
+    outer_phi = lax.ppermute(phi_block, "drift", chips)
 
     box = plane(layers, rows, sector)
     p0, ex, w, inv2, geo = kernel(
@@ -512,34 +541,43 @@
         mb=20,
     )(potential_guess, permittivity, pads, *raws)
     p0, ex, w, inv2, geo = [fetched(x) for x in (p0, ex, w, inv2, geo)]
-    charge, swap, middle, sums, state, b = kernel(
-        functools.partial(inner_relax_kernel, sides),
+    wb, bb = kernel(
+        outer_coupling_kernel,
+        [plane(6, 2, depth, rows, sector), plane(2, depth, rows, sector)],
+        [IN_VMEM] * 5,
+        scratch=[near(2, depth + 2, rows, sector)],
+        mb=12,
+    )(inner, outer_eps, far, ex, geo)
+    wb, bb = fetched(wb), fetched(bb)
+    raw, swap, b = kernel(
+        functools.partial(charge_kernel, sides),
+        [box, plane(depth - 1, rows, sector), box],
+        [IN_VMEM] * (3 + sides),
+        mb=8,
+    )(moved, inv2, geo, *rows_moved)
+    raw, b = fetched(raw), fetched(b)
+    swapped = lax.ppermute(swap, "drift", partners)
+    charge, middle, sums, state = kernel(
+        inner_relax_kernel,
         [
             plane(layers, band, sector),
-            plane(depth - 1, rows, sector),
             plane(layers - 2 * depth, rows, sector),
             plane(rows, sector),
             plane(2, depth - 1, 2, rows, sector),
-            plane(2, depth, rows, sector),
         ],
-        [IN_VMEM] * (5 + sides),
-        scratch=[near(layers, rows, sector)] * 5,
-        mb=16,
-    )(moved, p0, w, inv2, geo, *rows_moved)
-    swapped = lax.ppermute(swap, "drift", partners)
+        [IN_VMEM] * 4,
+        [ANYWHERE] + [IN_VMEM] * 3,
+        scratch=[near(layers, rows, sector)] * 3 + [dma],
+        mb=12,
+    )(p0, w, b, raw)
+    state, sums = fetched(state), fetched(sums)
     low, high, sums = kernel(
         outer_relax_kernel,
         [plane(depth, rows, sector), plane(depth, rows, sector), plane(rows, sector)],
-        [IN_VMEM] * 11,
-        scratch=[
-            near(2, depth, rows, sector),
-            near(2, depth + 2, rows, sector),
-            near(6, 2, depth, rows, sector),
-            near(2, depth, rows, sector),
-            near(depth - 1, 2, depth, rows, sector),
-        ],
-        mb=16,
-    )(inner, outer, far, swapped, p0, ex, w, geo, fetched(state), fetched(b), fetched(sums))
+        [IN_VMEM] * 10,
+        scratch=[near(2, depth, rows, sector), near(2, depth, rows, sector), near(depth - 1, 2, depth, rows, sector)],
+        mb=12,
+    )(inner, outer_phi, swapped, p0, w, wb, bb, state, b, sums)
     potential, local = kernel(
         local_kernel,
         [plane(layers, band, sector), plane(2, layers, band, sector)],

time: 69.3 us -> 68.3 us (0.986)
  waiting for transfers between devices: 25.8 us -> 20.9 us
  starting transfers between devices: 25.5 us -> 29.9 us
    ppermute x2, waiting for transfers between devices: 9.09 us -> 5.49 us  [shifted(): return lax.ppermute(block, axis, route)]
    ppermute x2 -> x4, starting transfers between devices: 2.28 us -> 4.51 us  [the longest x2 3.16 us: swap_rows(): return [lax.ppermute(blocks[0], 'radius', [(0, 1), (1, 0)])]]
    pallas_call x1, Pallas kernels: 3.14 us -> 1.86 us  [body(): kernel(outer_relax_kernel, [plane(depth, rows, sector), plane(depth, rows...]
    ppermute x1, waiting for transfers between devices: 1.09 us -> 0.01 us  [body(): swapped = lax.ppermute(swap, 'drift', partners)]
    ppermute x2, starting transfers between devices: 10.2 us -> 11 us  [shifted(): return lax.ppermute(block, axis, route)]
    ppermute x1, starting transfers between devices: 5.31 us -> 6 us  [body(): swapped = lax.ppermute(swap, 'drift', partners)]
    pallas_call x2 -> x5, Pallas kernels: 6.2 us -> 6.84 us  [the longest x1 2.29 us: body(): kernel(inner_relax_kernel, [plane(layers, band, sector), plane(layers - 2...]
    ppermute x2 -> x4, waiting for transfers between devices: 9.06 us -> 9.2 us  [the longest x2 9.19 us: swap_rows(): return [lax.ppermute(blocks[0], 'radius', [(0, 1), (1, 0)])]]
  transfers between devices with their start and end apart: 11 -> 13, of which waited for: 6 -> 6; matrix products, arithmetic and copies ran while one was open for 0% -> 0% of each run, Pallas kernels for 18% -> 19%
where the time goes in v5:
time: 68.3 us; the launch traced here: 68 us
  starting transfers between devices  29.9 us (44%)
  waiting for transfers between devices  20.9 us (31%)
  Pallas kernels  16.4 us (24%)
  between operations  0.83 us (1%)
    ppermute x2, starting transfers between devices, shifted(): return lax.ppermute(block, axis, route)  11 us
    ppermute x2, waiting for transfers between devices, swap_rows(): return [lax.ppermute(blocks[0], 'radius', [(0, 1), (1, 0)])]  9.19 us
    ppermute x4, starting transfers between devices, sums_below(): other = lax.ppermute(total, 'drift', [(i, i ^ step) for i in range(count)])  7.64 us
    ppermute x4, waiting for transfers between devices, sums_below(): other = lax.ppermute(total, 'drift', [(i, i ^ step) for i in range(count)])  6.17 us
    ppermute x1, starting transfers between devices, body(): swapped = lax.ppermute(swap, 'drift', partners)  6 us
    ppermute x2, waiting for transfers between devices, shifted(): return lax.ppermute(block, axis, route)  5.49 us
    ppermute x2, starting transfers between devices, swap_rows(): return [lax.ppermute(blocks[0], 'radius', [(0, 1), (1, 0)])]  3.16 us
    pallas_call x1, Pallas kernels, body(): kernel(local_kernel, [plane(layers, band, sector), plane(2, layers, band,...  2.62 us
  transfers between devices with their start and end apart: 13, of which 6 were waited for; matrix products, arithmetic and copies ran while one was open for 0% of the time, Pallas kernels for 19%

profile of v5, /device:TPU:0, one launch (start us, length us, event | category | flops | bytes accessed | tf_op | source)
XLA Modules:
  0.0 68.0 jit_solution(11670101844639496931)
XLA Ops:
  0.6 4.9 %collective-permute-start.1 = (f32[16,64,256]{2,1,0:T(8,128)}, f32[16,64,256]{2,1,0:T(8,128)S(1)}, u32[]{:S(2)}, u32[]{:S(2)}) collective-permute-start(f32[16,64,256]{2,1,0:T(8,128)} %ions.5), channel_id=1, source_target_pairs={{0,4},{2,6},{4,8},{6,10},{8,12},{10,14},{12,16},{14,18},{16,20},{1... | collective-permute-start | bytes 3145736 | tf_op jit(solution)/shard_map/ppermute | solution.py:32
  5.6 1.2 %shard_map.94 = (f32[40,8,256]{2,1,0:T(8,128)S(1)}, f32[2,64,256]{2,1,0:T(8,128)S(1)}) custom-call(f32[16,64,256]{2,1,0:T(8,128)} %phi.5, f32[16,64,256]{2,1,0:T(8,128)} %eps.5, f32[16,64,256]{2,1,0:T(8,128)} %ions.5, f32[64,256]{1,0:T(8,128)} %rec.1, s32[64,256]{1,0:T(8,128)} %index.1, s32[64,256]{1,0:T(8,128)} %gap.1, f32[16]{0:T(128)} %table.1), custom_call_target="tpu_custom_call" | custom-call | tf_op jit(solution)/shard_map/pallas_call | solution.py:504
  6.8 1.6 %collective-permute-start = (f32[40,8,256]{2,1,0:T(8,128)S(1)}, f32[40,8,256]{2,1,0:T(8,128)S(1)}, u32[]{:S(2)}, u32[]{:S(2)}) collective-permute-start(f32[40,8,256]{2,1,0:T(8,128)S(1)} %get-tuple-element.29), channel_id=1, source_target_pairs={{0,1},{1,0},{2,3},{3,2},{4,5},{5,4},{6,7},{7,6},{8,9},{9,8},{10,11... | collective-permute-start | bytes 983048 | tf_op jit(solution)/shard_map/ppermute | solution.py:493
  8.4 7.7 %collective-permute-done.refs_0_ = f32[40,8,256]{2,1,0:T(8,128)S(1)} collective-permute-done((f32[40,8,256]{2,1,0:T(8,128)S(1)}, f32[40,8,256]{2,1,0:T(8,128)S(1)}, u32[]{:S(2)}, u32[]{:S(2)}) %collective-permute-start) | collective-permute-done | bytes 327712 | tf_op jit(solution)/shard_map/ppermute | solution.py:493
  16.0 1.5 %shard_map.99 = (f32[11,72,256]{2,1,0:T(8,128)S(1)}, f32[4,72,256]{2,1,0:T(8,128)S(1)}, f32[4,72,256]{2,1,0:T(8,128)S(1)}, f32[3,72,256]{2,1,0:T(8,128)S(1)}) custom-call(f32[16,64,256]{2,1,0:T(8,128)} %phi.5, f32[16,64,256]{2,1,0:T(8,128)} %eps.5, f32[16,64,256]{2,1,0:T(8,128)} %ions.5, f32[40,8,256]{2,1,0:T(8,128)S(1)} %collective-permute-done.refs_0_), custom_call_target="tpu_custom_call" | custom-call | tf_op jit(solution)/shard_map/pallas_call | solution.py:520
  17.6 1.0 %shard_map.96 = f32[8,8,256]{2,1,0:T(8,128)S(1)} custom-call(f32[16,64,256]{2,1,0:T(8,128)} %ions.5), custom_call_target="tpu_custom_call" | custom-call | tf_op jit(solution)/shard_map/pallas_call | solution.py:496
  18.7 1.6 %collective-permute-start.2 = (f32[8,8,256]{2,1,0:T(8,128)S(1)}, f32[8,8,256]{2,1,0:T(8,128)S(1)}, u32[]{:S(2)}, u32[]{:S(2)}) collective-permute-start(f32[8,8,256]{2,1,0:T(8,128)S(1)} %shard_map.96), channel_id=1, source_target_pairs={{0,1},{1,0},{2,3},{3,2},{4,5},{5,4},{6,7},{7,6},{8,9},{9,8},{10,11... | collective-permute-start | bytes 196616 | tf_op jit(solution)/shard_map/ppermute | solution.py:493
  20.9 0.7 collective-permute-start.5
  21.6 1.5 %collective-permute-done.2 = f32[8,8,256]{2,1,0:T(8,128)S(1)} collective-permute-done((f32[8,8,256]{2,1,0:T(8,128)S(1)}, f32[8,8,256]{2,1,0:T(8,128)S(1)}, u32[]{:S(2)}, u32[]{:S(2)}) %collective-permute-start.2) | collective-permute-done | bytes 65568 | tf_op jit(solution)/shard_map/ppermute | solution.py:493
  23.1 6.1 %collective-permute-start.3 = (f32[8,8,256]{2,1,0:T(8,128)S(1)}, f32[8,8,256]{2,1,0:T(8,128)S(1)}, u32[]{:S(2)}, u32[]{:S(2)}) collective-permute-start(f32[8,8,256]{2,1,0:T(8,128)S(1)} %collective-permute-done.2), channel_id=1, source_target_pairs={{0,4},{2,6},{4,8},{6,10},{8,12},{10,14},{12,16},{14,18},{16,20},{1... | collective-permute-start | bytes 196616 | tf_op jit(solution)/shard_map/ppermute | solution.py:32
  29.2 2.2 %shard_map.95 = (f32[16,72,256]{2,1,0:T(8,128)S(1)}, f32[16,72,256]{2,1,0:T(8,128)S(1)}, f32[6,16,72,256]{3,2,1,0:T(8,128)S(1)}, f32[16,72,256]{2,1,0:T(8,128)S(1)}, f32[10,72,256]{2,1,0:T(8,128)S(1)}) custom-call(f32[16,64,256]{2,1,0:T(8,128)S(1)} %copy-done, f32[16,64,256]{2,1,0:T(8,128)S(1)} %copy-done.1, f32[2,64,256]{2,1,0:T(8,128)S(1)} %get-tuple-element.28.pads, ...), custom_call_target="tpu_custom_call" | custom-call | tf_op jit(solution)/shard_map/pallas_call | solution.py:537
  31.5 5.5 %collective-permute-done.3.refs_0_ = f32[8,8,256]{2,1,0:T(8,128)S(1)} collective-permute-done((f32[8,8,256]{2,1,0:T(8,128)S(1)}, f32[8,8,256]{2,1,0:T(8,128)S(1)}, u32[]{:S(2)}, u32[]{:S(2)}) %collective-permute-start.3) | collective-permute-done | bytes 65568 | tf_op jit(solution)/shard_map/ppermute | solution.py:32
  38.3 6.0 %collective-permute-start.6 = (f32[3,72,256]{2,1,0:T(8,128)S(1)}, f32[3,72,256]{2,1,0:T(8,128)S(1)}, u32[]{:S(2)}, u32[]{:S(2)}) collective-permute-start(f32[3,72,256]{2,1,0:T(8,128)S(1)} %get-tuple-element.39), channel_id=1, source_target_pairs={{0,2},{2,0},{4,6},{6,4},{8,10},{10,8},{12,14},{14,12},{16,18},{18,... | collective-permute-start | bytes 663560 | tf_op jit(solution)/shard_map/ppermute | solution.py:559
  44.3 2.3 %shard_map.98 = (f32[16,64,256]{2,1,0:T(8,128)}, f32[8,72,256]{2,1,0:T(8,128)S(1)}, f32[72,256]{1,0:T(8,128)S(1)}, f32[2,3,2,72,256]{4,3,2,1,0:T(8,128)S(1)}) custom-call(f32[16,72,256]{2,1,0:T(8,128)S(1)} %get-tuple-element.30.p0, f32[6,16,72,256]{3,2,1,0:T(8,128)S(1)} %get-tuple-element.31.w, f32[16,72,256]{2,1,0:T(8,128)S(1)} %get-tuple-element.34.b.b_in, ...), custom_call_target="tpu_custom_call" | custom-call | tf_op jit(solution)/shard_map/pallas_call | solution.py:560
  46.6 1.4 %shard_map.100 = (f32[6,2,4,72,256]{4,3,2,1,0:T(8,128)S(1)}, f32[2,4,72,256]{3,2,1,0:T(8,128)S(1)}) custom-call(f32[11,72,256]{2,1,0:T(8,128)S(1)} %collective-permute-done.4.inner, f32[4,72,256]{2,1,0:T(8,128)S(1)} %collective-permute-done.7.outer_eps, f32[3,72,256]{2,1,0:T(8,128)S(1)} %collective-permute-done.8.far, ...), custom_call_target="tpu_custom_call" | custom-call | tf_op jit(solution)/shard_map/pallas_call | solution.py:544
  48.1 1.9 %shard_map.101 = (f32[4,72,256]{2,1,0:T(8,128)S(1)}, f32[4,72,256]{2,1,0:T(8,128)S(1)}, f32[72,256]{1,0:T(8,128)S(1)}) custom-call(f32[11,72,256]{2,1,0:T(8,128)S(1)} %collective-permute-done.4.inner, f32[4,72,256]{2,1,0:T(8,128)S(1)} %collective-permute-done.5.outer_phi, f32[3,72,256]{2,1,0:T(8,128)S(1)} %collective-permute-done.6.swapped, ...), custom_call_target="tpu_custom_call" | custom-call | tf_op jit(solution)/shard_map/pallas_call | solution.py:574
  50.0 1.2 %collective-permute-done.9 = f32[72,256]{1,0:T(8,128)S(1)} collective-permute-done((f32[72,256]{1,0:T(8,128)S(1)}, f32[72,256]{1,0:T(8,128)S(1)}, u32[]{:S(2)}, u32[]{:S(2)}) %collective-permute-start.9) | collective-permute-done | bytes 73760 | tf_op jit(solution)/shard_map/ppermute | solution.py:460
  51.3 2.3 %collective-permute-start.10 = (f32[72,256]{1,0:T(8,128)S(1)}, f32[72,256]{1,0:T(8,128)S(1)}, u32[]{:S(2)}, u32[]{:S(2)}) collective-permute-start(f32[72,256]{1,0:T(8,128)S(1)} %add.18), channel_id=1, source_target_pairs={{0,4},{2,6},{4,0},{6,2},{8,12},{10,14},{12,8},{14,10},{16,20},{18,... | collective-permute-start | bytes 221192 | tf_op jit(solution)/shard_map/ppermute | solution.py:460
  53.5 2.6 %collective-permute-done.10 = f32[72,256]{1,0:T(8,128)S(1)} collective-permute-done((f32[72,256]{1,0:T(8,128)S(1)}, f32[72,256]{1,0:T(8,128)S(1)}, u32[]{:S(2)}, u32[]{:S(2)}) %collective-permute-start.10) | collective-permute-done | bytes 73760 | tf_op jit(solution)/shard_map/ppermute | solution.py:460
  56.1 2.2 %collective-permute-start.11 = (f32[72,256]{1,0:T(8,128)S(1)}, f32[72,256]{1,0:T(8,128)S(1)}, u32[]{:S(2)}, u32[]{:S(2)}) collective-permute-start(f32[72,256]{1,0:T(8,128)S(1)} %add.20), channel_id=1, source_target_pairs={{0,8},{2,10},{4,12},{6,14},{8,0},{10,2},{12,4},{14,6},{16,24},{18,... | collective-permute-start | bytes 221192 | tf_op jit(solution)/shard_map/ppermute | solution.py:460
  58.3 2.3 %collective-permute-done.11 = f32[72,256]{1,0:T(8,128)S(1)} collective-permute-done((f32[72,256]{1,0:T(8,128)S(1)}, f32[72,256]{1,0:T(8,128)S(1)}, u32[]{:S(2)}, u32[]{:S(2)}) %collective-permute-start.11) | collective-permute-done | bytes 73760 | tf_op jit(solution)/shard_map/ppermute | solution.py:460
  60.7 3.1 %collective-permute-start.12 = (f32[72,256]{1,0:T(8,128)S(1)}, f32[72,256]{1,0:T(8,128)S(1)}, u32[]{:S(2)}, u32[]{:S(2)}) collective-permute-start(f32[72,256]{1,0:T(8,128)S(1)} %add.22), channel_id=1, source_target_pairs={{0,16},{2,18},{4,20},{6,22},{8,24},{10,26},{12,28},{14,30},{16,0},... | collective-permute-start | bytes 221192 | tf_op jit(solution)/shard_map/ppermute | solution.py:460
  63.8 2.6 %shard_map.102 = (f32[16,64,256]{2,1,0:T(8,128)}, f32[2,16,64,256]{3,2,1,0:T(8,128)S(1)}) custom-call(f32[4,72,256]{2,1,0:T(8,128)S(1)} %get-tuple-element.47.low, f32[8,72,256]{2,1,0:T(8,128)S(1)} %get-tuple-element.48.inner, f32[4,72,256]{2,1,0:T(8,128)S(1)} %get-tuple-element.49.high), custom_call_target="tpu_custom_call" | custom-call | tf_op jit(solution)/shard_map/pallas_call | solution.py:581
  66.4 1.6 %shard_map.103 = f32[2,16,64,256]{3,2,1,0:T(8,128)} custom-call(f32[2,16,64,256]{3,2,1,0:T(8,128)S(1)} %get-tuple-element.51.local, f32[72,256]{1,0:T(8,128)S(1)} %select_add_fusion.prefix), custom_call_target="tpu_custom_call" | custom-call | tf_op jit(solution)/shard_map/pallas_call | solution.py:589
  (20 shorter events, 2.2 us)
Async XLA Ops:
  0.6 37.0 %collective-permute-start.1 = (f32[16,64,256]{2,1,0:T(8,128)}, f32[16,64,256]{2,1,0:T(8,128)S(1)}, u32[]{:S(2)}, u32[]{:S(2)}) collective-permute-start(f32[16,64,256]{2,1,0:T(8,128)} %ions.5), channel_id=1, source_target_pairs={{0,4},{2,6},{4,8},{6,10},{8,12},{10,14},{12,16},{14,18},{16,20},{1... | collective-permute-start | bytes 3145736 | tf_op jit(solution)/shard_map/ppermute | solution.py:32
  6.8 9.2 %collective-permute-start = (f32[40,8,256]{2,1,0:T(8,128)S(1)}, f32[40,8,256]{2,1,0:T(8,128)S(1)}, u32[]{:S(2)}, u32[]{:S(2)}) collective-permute-start(f32[40,8,256]{2,1,0:T(8,128)S(1)} %get-tuple-element.29), channel_id=1, source_target_pairs={{0,1},{1,0},{2,3},{3,2},{4,5},{5,4},{6,7},{7,6},{8,9},{9,8},{10,11... | collective-permute-start | bytes 983048 | tf_op jit(solution)/shard_map/ppermute | solution.py:493
  16.0 13.2 %copy-start.1 = (f32[16,64,256]{2,1,0:T(8,128)S(1)}, f32[16,64,256]{2,1,0:T(8,128)}, u32[]{:S(2)}) copy-start(f32[16,64,256]{2,1,0:T(8,128)} %eps.5) | copy-start | bytes 3145732
  17.6 11.7 %copy-start = (f32[16,64,256]{2,1,0:T(8,128)S(1)}, f32[16,64,256]{2,1,0:T(8,128)}, u32[]{:S(2)}) copy-start(f32[16,64,256]{2,1,0:T(8,128)} %phi.5) | copy-start | bytes 3145732
  17.6 29.1 %collective-permute-start.4 = (f32[11,72,256]{2,1,0:T(8,128)S(1)}, f32[11,72,256]{2,1,0:T(8,128)S(1)}, u32[]{:S(2)}, u32[]{:S(2)}) collective-permute-start(f32[11,72,256]{2,1,0:T(8,128)S(1)} %get-tuple-element.37), channel_id=1, source_target_pairs={{0,2},{2,0},{4,6},{6,4},{8,10},{10,8},{12,14},{14,12},{16,18},{18,... | collective-permute-start | bytes 2433032 | tf_op jit(solution)/shard_map/ppermute | solution.py:533
  18.7 4.5 %collective-permute-start.2 = (f32[8,8,256]{2,1,0:T(8,128)S(1)}, f32[8,8,256]{2,1,0:T(8,128)S(1)}, u32[]{:S(2)}, u32[]{:S(2)}) collective-permute-start(f32[8,8,256]{2,1,0:T(8,128)S(1)} %shard_map.96), channel_id=1, source_target_pairs={{0,1},{1,0},{2,3},{3,2},{4,5},{5,4},{6,7},{7,6},{8,9},{9,8},{10,11... | collective-permute-start | bytes 196616 | tf_op jit(solution)/shard_map/ppermute | solution.py:493
  20.2 26.4 %collective-permute-start.7 = (f32[4,72,256]{2,1,0:T(8,128)S(1)}, f32[4,72,256]{2,1,0:T(8,128)S(1)}, u32[]{:S(2)}, u32[]{:S(2)}) collective-permute-start(f32[4,72,256]{2,1,0:T(8,128)S(1)} %get-tuple-element.40), channel_id=1, source_target_pairs={{2,4},{4,2},{6,8},{8,6},{10,12},{12,10},{14,16},{16,14},{18,20},{2... | collective-permute-start | bytes 884744 | tf_op jit(solution)/shard_map/ppermute | solution.py:531
  20.9 27.1 %collective-permute-start.5 = (f32[4,72,256]{2,1,0:T(8,128)S(1)}, f32[4,72,256]{2,1,0:T(8,128)S(1)}, u32[]{:S(2)}, u32[]{:S(2)}) collective-permute-start(f32[4,72,256]{2,1,0:T(8,128)S(1)} %get-tuple-element.38), channel_id=1, source_target_pairs={{2,4},{4,2},{6,8},{8,6},{10,12},{12,10},{14,16},{16,14},{18,20},{2... | collective-permute-start | bytes 884744 | tf_op jit(solution)/shard_map/ppermute | solution.py:534
  23.1 13.8 %collective-permute-start.3 = (f32[8,8,256]{2,1,0:T(8,128)S(1)}, f32[8,8,256]{2,1,0:T(8,128)S(1)}, u32[]{:S(2)}, u32[]{:S(2)}) collective-permute-start(f32[8,8,256]{2,1,0:T(8,128)S(1)} %collective-permute-done.2), channel_id=1, source_target_pairs={{0,4},{2,6},{4,8},{6,10},{8,12},{10,14},{12,16},{14,18},{16,20},{1... | collective-permute-start | bytes 196616 | tf_op jit(solution)/shard_map/ppermute | solution.py:32
  37.0 9.6 %collective-permute-start.8 = (f32[3,72,256]{2,1,0:T(8,128)S(1)}, f32[3,72,256]{2,1,0:T(8,128)S(1)}, u32[]{:S(2)}, u32[]{:S(2)}) collective-permute-start(f32[3,72,256]{2,1,0:T(8,128)S(1)} %get-tuple-element.41), channel_id=1, source_target_pairs={{2,8},{6,12},{10,16},{14,20},{18,24},{22,28},{3,9},{7,13},{11,17},... | collective-permute-start | bytes 663560 | tf_op jit(solution)/shard_map/ppermute | solution.py:532
  38.3 9.7 %collective-permute-start.6 = (f32[3,72,256]{2,1,0:T(8,128)S(1)}, f32[3,72,256]{2,1,0:T(8,128)S(1)}, u32[]{:S(2)}, u32[]{:S(2)}) collective-permute-start(f32[3,72,256]{2,1,0:T(8,128)S(1)} %get-tuple-element.39), channel_id=1, source_target_pairs={{0,2},{2,0},{4,6},{6,4},{8,10},{10,8},{12,14},{14,12},{16,18},{18,... | collective-permute-start | bytes 663560 | tf_op jit(solution)/shard_map/ppermute | solution.py:559
  49.9 1.3 %collective-permute-start.9 = (f32[72,256]{1,0:T(8,128)S(1)}, f32[72,256]{1,0:T(8,128)S(1)}, u32[]{:S(2)}, u32[]{:S(2)}) collective-permute-start(f32[72,256]{1,0:T(8,128)S(1)} %get-tuple-element.52), channel_id=1, source_target_pairs={{0,2},{2,0},{4,6},{6,4},{8,10},{10,8},{12,14},{14,12},{16,18},{18,... | collective-permute-start | bytes 221192 | tf_op jit(solution)/shard_map/ppermute | solution.py:460
  51.3 4.8 %collective-permute-start.10 = (f32[72,256]{1,0:T(8,128)S(1)}, f32[72,256]{1,0:T(8,128)S(1)}, u32[]{:S(2)}, u32[]{:S(2)}) collective-permute-start(f32[72,256]{1,0:T(8,128)S(1)} %add.18), channel_id=1, source_target_pairs={{0,4},{2,6},{4,0},{6,2},{8,12},{10,14},{12,8},{14,10},{16,20},{18,... | collective-permute-start | bytes 221192 | tf_op jit(solution)/shard_map/ppermute | solution.py:460
  56.1 4.5 %collective-permute-start.11 = (f32[72,256]{1,0:T(8,128)S(1)}, f32[72,256]{1,0:T(8,128)S(1)}, u32[]{:S(2)}, u32[]{:S(2)}) collective-permute-start(f32[72,256]{1,0:T(8,128)S(1)} %add.20), channel_id=1, source_target_pairs={{0,8},{2,10},{4,12},{6,14},{8,0},{10,2},{12,4},{14,6},{16,24},{18,... | collective-permute-start | bytes 221192 | tf_op jit(solution)/shard_map/ppermute | solution.py:460
  60.7 5.7 %collective-permute-start.12 = (f32[72,256]{1,0:T(8,128)S(1)}, f32[72,256]{1,0:T(8,128)S(1)}, u32[]{:S(2)}, u32[]{:S(2)}) collective-permute-start(f32[72,256]{1,0:T(8,128)S(1)} %add.22), channel_id=1, source_target_pairs={{0,16},{2,18},{4,20},{6,22},{8,24},{10,26},{12,28},{14,30},{16,0},... | collective-permute-start | bytes 221192 | tf_op jit(solution)/shard_map/ppermute | solution.py:460

commit v6 on v5

--- a/solution.py
+++ b/solution.py
@@ -288,114 +288,137 @@
     charge_copy.wait()
 
 
+class Wedge:
+    def __init__(self, near, layers):
+        d = lax.axis_index("drift")
+        odd = lax.rem(d, 2)
+        self.n, self.d = layers, d
+        self.high = (1 - odd) if near else odd
+        self.is_high = self.high == 1
+
+    def own(self, q):
+        return jnp.where(self.is_high, self.n - 1 - q, q)
+
+    def sent(self, q, count):
+        return jnp.where(self.is_high, -q - 1, count + q)
+
+    def alive(self, q):
+        z = self.d * self.n + self.own(q)
+        return jnp.where((z >= 0) & (z < lax.axis_size("drift") * self.n), 1.0, 0.0)
+
+
+def wedge_couplings(wedge, halo, halo_at, charge, ex, geo, wb, bb, eh):
+    depth = SWEEPS
+    rows, sector = eh.shape[1:]
+    sub = lax.broadcasted_iota(jnp.int32, (ROWS, sector), 0)
+    for q in range(-depth, 2):
+        eh[depth + q] = halo[halo_at + wedge.sent(q, depth)] if q < 0 else ex[wedge.own(q)]
+    for k in range(depth):
+        q = k + 1 - depth
+        bb[k] = charge(q) if q < 0 else jnp.ones_like(bb[0])
+
+        def put(at, values, twice, k=k):
+            for j, value in enumerate(values):
+                wb[j, k, at] = value
+            bb[k, at] = bb[k, at] * twice
+
+        coupling_rows(
+            k + 1, lambda i, at: eh[i, at], k + 2, k, geo, wedge.alive(q), rows // ROWS, sub, put
+        )
+
+
+def wedge_sweeps(wedge, halo, p0, w, wb, bb, state, b_in, q_buf, out, sums):
+    depth = SWEEPS
+    rows, sector = p0.shape[1:]
+    sub = lax.broadcasted_iota(jnp.int32, (ROWS, sector), 0)
+
+    def phi_at(s, q):
+        if s == 0:
+            if q < 0:
+                spot = wedge.sent(q, depth)
+                return lambda at: halo[spot, at]
+            spot = wedge.own(q)
+            return lambda at: p0[spot, at]
+        if q >= s:
+            spot = jnp.where(wedge.is_high, 1 - (q - s), q - s)
+            return lambda at: state[wedge.high, s - 1, spot, at]
+        return lambda at: q_buf[s - 1, q - s + depth, at]
+
+    def coupling(q):
+        if q <= 0:
+            return lambda j, at: wb[j, q + depth - 1, at]
+        z = wedge.own(q)
+        inward, outward = wedge.high, 1 - wedge.high
+        return lambda j, at: w[(inward, outward, 2, 3, 4, 5)[j], z, at]
+
+    for s in range(1, depth + 1):
+        for q in range(s - depth, s):
+            if q <= 0:
+                b_at = lambda at, q=q: bb[q + depth - 1, at]
+            else:
+                b_at = lambda at, z=wedge.own(q): b_in[z, at]
+
+            def put(at, total, s=s, q=q):
+                if s < depth:
+                    q_buf[s - 1, q - s + depth, at] = total
+                else:
+                    out[jnp.where(wedge.is_high, depth - 1 - q, q), at] = total
+                    sums[at] += total
+
+            sources = phi_at(s - 1, q), phi_at(s - 1, q + 1), phi_at(s - 1, q - 1)
+            sweep_layer(*sources, coupling(q), b_at, rows // ROWS, sub, put)
+
+
+def near_kernel(inner, swapped, ex, geo, p0, w, state, b_in, sums_in, out, sums_out, wb, bb, eh, q_buf):
+    wedge = Wedge(True, p0.shape[0])
+    ends = SWEEPS - 1
+    wedge_couplings(
+        wedge, inner, SWEEPS, lambda q: swapped[wedge.sent(q, ends)], ex, geo, wb, bb, eh
+    )
+    bb[ends] = bb[ends] * b_in[wedge.own(0)]
+    sums_out[...] = sums_in[...]
+    wedge_sweeps(wedge, inner, p0, w, wb, bb, state, b_in, q_buf, out, sums_out)
+
+
 def outer_coupling_kernel(inner, outer_eps, far, ex, geo, wb, bb, eh):
-    layers, rows, sector = ex.shape
-    depth, n = SWEEPS, layers
-    tiles = rows // ROWS
-    d, drifts = lax.axis_index("drift"), lax.axis_size("drift")
-    odd = lax.rem(d, 2) == 1
-    sub = lax.broadcasted_iota(jnp.int32, (ROWS, sector), 0)
-
-    for k in range(depth):
-        one, two = inner[depth + k], outer_eps[k]
-        eh[0, k] = jnp.where(odd, one, two)
-        eh[1, 2 + k] = jnp.where(odd, two, one)
-    for k in range(2):
-        eh[0, depth + k] = ex[k]
-        eh[1, k] = ex[n - 2 + k]
-
-    for k in range(depth - 1):
-        rec, inj = geo[6], geo[7]
-        bb[0, k] = jnp.where(odd, 1.0, drift_charge(far[k], rec, inj, d - 1))
-        bb[1, k + 1] = jnp.where(odd, drift_charge(inner[2 * depth + k], rec, inj, d + 1), 1.0)
-    bb[0, depth - 1] = jnp.ones_like(bb[0, 0])
-    bb[1, 0] = jnp.ones_like(bb[1, 0])
-    for side in range(2):
-
-        @pl.loop(0, depth)
-        def _(k, side=side):
-            zg = d * n - depth + (k + 1 if side == 0 else depth + n - 1 + k)
-            alive = jnp.where((zg >= 0) & (zg < drifts * n), 1.0, 0.0)
-
-            def put(at, values, twice):
-                for j, value in enumerate(values):
-                    wb[j, side, k, at] = value
-                bb[side, k, at] = bb[side, k, at] * twice
-
-            coupling_rows(k + 1, lambda i, s: eh[side, i, s], k + 2, k, geo, alive, tiles, sub, put)
-
-
-def outer_relax_kernel(
-    inner, outer_phi, swapped, p0, w, wb, bb_in, state, b_in, sums_in, low_out, high_out, sums_out, ph, bb, q
-):
-    layers, rows, sector = p0.shape
-    depth, n = SWEEPS, layers
-    zs = n + 2 * depth
-    tiles = rows // ROWS
-    odd = lax.rem(lax.axis_index("drift"), 2) == 1
-    sub = lax.broadcasted_iota(jnp.int32, (ROWS, sector), 0)
-    for k in range(depth):
-        one, two = inner[k], outer_phi[k]
-        ph[0, k] = jnp.where(odd, one, two)
-        ph[1, k] = jnp.where(odd, two, one)
-    for k in range(depth - 1):
-        ready = swapped[k]
-        bb[0, k] = bb_in[0, k] * jnp.where(odd, ready, 1.0)
-        bb[1, k + 1] = bb_in[1, k + 1] * jnp.where(odd, 1.0, ready)
-    bb[0, depth - 1] = bb_in[0, depth - 1] * b_in[0]
-    bb[1, 0] = bb_in[1, 0] * b_in[n - 1]
-
-    def phi_at(s, e):
-        if s == 0:
-            if e < depth:
-                return lambda at: ph[0, e, at]
-            if e >= depth + n:
-                return lambda at: ph[1, e - depth - n, at]
-            return lambda at: p0[e - depth, at]
-        z = e - depth
-        if s <= z < n - s:
-            if z < n // 2:
-                return lambda at: state[0, s - 1, z - s, at]
-            return lambda at: state[1, s - 1, z - (n - s - 2), at]
-        side = 0 if e < zs // 2 else 1
-        return lambda at: q[s - 1, side, (e - s) if side == 0 else e - (zs - s - depth), at]
-
+    wedge = Wedge(False, ex.shape[0])
+    ends = SWEEPS - 1
+
+    def charge(q):
+        spot = wedge.sent(q, ends)
+        ions = jnp.where(wedge.is_high, inner[2 * SWEEPS + spot], far[spot])
+        return drift_charge(ions, geo[6], geo[7], jnp.where(wedge.is_high, wedge.d + 1, wedge.d - 1))
+
+    wedge_couplings(wedge, outer_eps, 0, charge, ex, geo, wb, bb, eh)
+
+
+def outer_relax_kernel(outer_phi, p0, w, wb, bb_in, state, b_in, sums_in, out, sums_out, bb, q_buf):
+    wedge = Wedge(False, p0.shape[0])
+    ends = SWEEPS - 1
+    for k in range(ends):
+        bb[k] = bb_in[k]
+    bb[ends] = bb_in[ends] * b_in[wedge.own(0)]
     sums_out[...] = sums_in[...]
-    for s in range(1, depth + 1):
-        for side in range(2):
-            for k in range(depth):
-                e = s + k if side == 0 else zs - s - depth + k
-                z = e - depth
-                if 0 < z < n - 1:
-                    w_at = lambda j, at, z=z: w[j, z, at]
-                    b_at = lambda at, z=z: b_in[z, at]
-                else:
-                    at_layer = e - 1 if side == 0 else e - (zs - depth - 1)
-                    w_at = lambda j, at, side=side, i=at_layer: wb[j, side, i, at]
-                    b_at = lambda at, side=side, i=at_layer: bb[side, i, at]
-
-                def put(at, total, s=s, side=side, k=k):
-                    if s < depth:
-                        q[s - 1, side, k, at] = total
-                    else:
-                        (low_out, high_out)[side][k, at] = total
-                        sums_out[at] += total
-
-                sweep_layer(phi_at(s - 1, e), phi_at(s - 1, e + 1), phi_at(s - 1, e - 1), w_at, b_at, tiles, sub, put)
-
-
-def local_kernel(low, inner, high, potential, out, run):
+    wedge_sweeps(wedge, outer_phi, p0, w, wb, bb, state, b_in, q_buf, out, sums_out)
+
+
+def local_kernel(near, inner, far, potential, out, run):
     _, band, _ = potential.shape
     tiles = run.shape[0] // ROWS
     run[...] = jnp.zeros_like(run)
+    odd = lax.rem(lax.axis_index("drift"), 2) == 1
     base = 0
-    for window in (low, inner, high):
-
-        @pl.loop(0, window.shape[0])
-        def _(k, window=window, base=base):
+    for count, value_of in (
+        (near.shape[0], lambda k, at: jnp.where(odd, near[k, at], far[k, at])),
+        (inner.shape[0], lambda k, at: inner[k, at]),
+        (far.shape[0], lambda k, at: jnp.where(odd, far[k, at], near[k, at])),
+    ):
+
+        @pl.loop(0, count)
+        def _(k, value_of=value_of, base=base):
             for t in range(tiles):
                 at = slice(t * ROWS, (t + 1) * ROWS)
-                value = window[k, at]
+                value = value_of(k, at)
                 run[at] += value
                 if t < band // ROWS:
                     potential[base + k, at] = value
@@ -406,7 +429,7 @@
 
             ratios_of(run, band, put)
 
-        base += window.shape[0]
+        base += count
 
 
 def ratios_of(field, band, put):
@@ -541,11 +564,13 @@
         mb=20,
     )(potential_guess, permittivity, pads, *raws)
     p0, ex, w, inv2, geo = [fetched(x) for x in (p0, ex, w, inv2, geo)]
+    wedge = plane(depth, rows, sector)
+    wedge_box, wedge_couplings_box = near(depth, rows, sector), near(6, depth, rows, sector)
     wb, bb = kernel(
         outer_coupling_kernel,
-        [plane(6, 2, depth, rows, sector), plane(2, depth, rows, sector)],
+        [plane(6, depth, rows, sector), wedge],
         [IN_VMEM] * 5,
-        scratch=[near(2, depth + 2, rows, sector)],
+        scratch=[near(depth + 2, rows, sector)],
         mb=12,
     )(inner, outer_eps, far, ex, geo)
     wb, bb = fetched(wb), fetched(bb)
@@ -571,20 +596,27 @@
         mb=12,
     )(p0, w, b, raw)
     state, sums = fetched(state), fetched(sums)
-    low, high, sums = kernel(
+    near_out, sums = kernel(
+        near_kernel,
+        [wedge, plane(rows, sector)],
+        [IN_VMEM] * 9,
+        scratch=[wedge_couplings_box, wedge_box, near(depth + 2, rows, sector), near(depth - 1, depth, rows, sector)],
+        mb=12,
+    )(inner, swapped, ex, geo, p0, w, state, b, sums)
+    far_out, sums = kernel(
         outer_relax_kernel,
-        [plane(depth, rows, sector), plane(depth, rows, sector), plane(rows, sector)],
-        [IN_VMEM] * 10,
-        scratch=[near(2, depth, rows, sector), near(2, depth, rows, sector), near(depth - 1, 2, depth, rows, sector)],
+        [wedge, plane(rows, sector)],
+        [IN_VMEM] * 8,
+        scratch=[wedge_box, near(depth - 1, depth, rows, sector)],
         mb=12,
-    )(inner, outer_phi, swapped, p0, w, wb, bb, state, b, sums)
+    )(outer_phi, p0, w, wb, bb, state, b, fetched(sums))
     potential, local = kernel(
         local_kernel,
         [plane(layers, band, sector), plane(2, layers, band, sector)],
         [IN_VMEM] * 3,
         scratch=[near(rows, sector)],
         mb=16,
-    )(low, middle, high)
+    )(near_out, middle, far_out)
     below_sums = sums_below(sums)
     distortion = kernel(
         offset_kernel,

time: 68.3 us -> 67.9 us (level)
    pallas_call x2 -> x3, Pallas kernels: 3.25 us -> 2.81 us  [the longest x1 1.36 us: body(): kernel(near_kernel, [wedge, plane(rows, sector)], [IN_VMEM] * 9, scratch=...]
  transfers between devices with their start and end apart: 13 -> 13, of which waited for: 6 -> 6; matrix products, arithmetic and copies ran while one was open for 0% -> 0% of each run, Pallas kernels for 19% -> 20%
where the time goes in v6:
time: 67.9 us; the launch traced here: 67.6 us
  starting transfers between devices  30 us (44%)
  waiting for transfers between devices  20.9 us (31%)
  Pallas kernels  15.9 us (23%)
  between operations  0.83 us (1%)
    ppermute x2, starting transfers between devices, shifted(): return lax.ppermute(block, axis, route)  11 us
    ppermute x2, waiting for transfers between devices, swap_rows(): return [lax.ppermute(blocks[0], 'radius', [(0, 1), (1, 0)])]  9.19 us
    ppermute x4, starting transfers between devices, sums_below(): other = lax.ppermute(total, 'drift', [(i, i ^ step) for i in range(count)])  7.72 us
    ppermute x4, waiting for transfers between devices, sums_below(): other = lax.ppermute(total, 'drift', [(i, i ^ step) for i in range(count)])  6.18 us
    ppermute x1, starting transfers between devices, body(): swapped = lax.ppermute(swap, 'drift', partners)  6 us
    ppermute x2, waiting for transfers between devices, shifted(): return lax.ppermute(block, axis, route)  5.49 us
    ppermute x2, starting transfers between devices, swap_rows(): return [lax.ppermute(blocks[0], 'radius', [(0, 1), (1, 0)])]  3.16 us
    pallas_call x1, Pallas kernels, body(): kernel(local_kernel, [plane(layers, band, sector), plane(2, layers, band,...  2.64 us
  transfers between devices with their start and end apart: 13, of which 6 were waited for; matrix products, arithmetic and copies ran while one was open for 0% of the time, Pallas kernels for 20%

profile of v6, /device:TPU:0, one launch (start us, length us, event | category | flops | bytes accessed | tf_op | source)
XLA Modules:
  0.0 67.6 jit_solution(6091159972722403154)
XLA Ops:
  0.6 4.9 %collective-permute-start.1 = (f32[16,64,256]{2,1,0:T(8,128)}, f32[16,64,256]{2,1,0:T(8,128)S(1)}, u32[]{:S(2)}, u32[]{:S(2)}) collective-permute-start(f32[16,64,256]{2,1,0:T(8,128)} %ions.5), channel_id=1, source_target_pairs={{0,4},{2,6},{4,8},{6,10},{8,12},{10,14},{12,16},{14,18},{16,20},{1... | collective-permute-start | bytes 3145736 | tf_op jit(solution)/shard_map/ppermute | solution.py:32
  5.6 1.2 %shard_map.94 = (f32[40,8,256]{2,1,0:T(8,128)S(1)}, f32[2,64,256]{2,1,0:T(8,128)S(1)}) custom-call(f32[16,64,256]{2,1,0:T(8,128)} %phi.5, f32[16,64,256]{2,1,0:T(8,128)} %eps.5, f32[16,64,256]{2,1,0:T(8,128)} %ions.5, f32[64,256]{1,0:T(8,128)} %rec.1, s32[64,256]{1,0:T(8,128)} %index.1, s32[64,256]{1,0:T(8,128)} %gap.1, f32[16]{0:T(128)} %table.1), custom_call_target="tpu_custom_call" | custom-call | tf_op jit(solution)/shard_map/pallas_call | solution.py:527
  6.8 1.6 %collective-permute-start = (f32[40,8,256]{2,1,0:T(8,128)S(1)}, f32[40,8,256]{2,1,0:T(8,128)S(1)}, u32[]{:S(2)}, u32[]{:S(2)}) collective-permute-start(f32[40,8,256]{2,1,0:T(8,128)S(1)} %get-tuple-element.30), channel_id=1, source_target_pairs={{0,1},{1,0},{2,3},{3,2},{4,5},{5,4},{6,7},{7,6},{8,9},{9,8},{10,11... | collective-permute-start | bytes 983048 | tf_op jit(solution)/shard_map/ppermute | solution.py:516
  8.4 7.7 %collective-permute-done.refs_0_ = f32[40,8,256]{2,1,0:T(8,128)S(1)} collective-permute-done((f32[40,8,256]{2,1,0:T(8,128)S(1)}, f32[40,8,256]{2,1,0:T(8,128)S(1)}, u32[]{:S(2)}, u32[]{:S(2)}) %collective-permute-start) | collective-permute-done | bytes 327712 | tf_op jit(solution)/shard_map/ppermute | solution.py:516
  16.0 1.5 %shard_map.99 = (f32[11,72,256]{2,1,0:T(8,128)S(1)}, f32[4,72,256]{2,1,0:T(8,128)S(1)}, f32[4,72,256]{2,1,0:T(8,128)S(1)}, f32[3,72,256]{2,1,0:T(8,128)S(1)}) custom-call(f32[16,64,256]{2,1,0:T(8,128)} %phi.5, f32[16,64,256]{2,1,0:T(8,128)} %eps.5, f32[16,64,256]{2,1,0:T(8,128)} %ions.5, f32[40,8,256]{2,1,0:T(8,128)S(1)} %collective-permute-done.refs_0_), custom_call_target="tpu_custom_call" | custom-call | tf_op jit(solution)/shard_map/pallas_call | solution.py:543
  17.6 1.0 %shard_map.96 = f32[8,8,256]{2,1,0:T(8,128)S(1)} custom-call(f32[16,64,256]{2,1,0:T(8,128)} %ions.5), custom_call_target="tpu_custom_call" | custom-call | tf_op jit(solution)/shard_map/pallas_call | solution.py:519
  18.7 1.6 %collective-permute-start.2 = (f32[8,8,256]{2,1,0:T(8,128)S(1)}, f32[8,8,256]{2,1,0:T(8,128)S(1)}, u32[]{:S(2)}, u32[]{:S(2)}) collective-permute-start(f32[8,8,256]{2,1,0:T(8,128)S(1)} %shard_map.96), channel_id=1, source_target_pairs={{0,1},{1,0},{2,3},{3,2},{4,5},{5,4},{6,7},{7,6},{8,9},{9,8},{10,11... | collective-permute-start | bytes 196616 | tf_op jit(solution)/shard_map/ppermute | solution.py:516
  20.9 0.7 %collective-permute-start.6 = (f32[4,72,256]{2,1,0:T(8,128)S(1)}, f32[4,72,256]{2,1,0:T(8,128)S(1)}, u32[]{:S(2)}, u32[]{:S(2)}) collective-permute-start(f32[4,72,256]{2,1,0:T(8,128)S(1)} %get-tuple-element.45), channel_id=1, source_target_pairs={{2,4},{4,2},{6,8},{8,6},{10,12},{12,10},{14,16},{16,14},{18,20},{2... | collective-permute-start | bytes 884744 | tf_op jit(solution)/shard_map/ppermute | solution.py:557
  21.6 1.5 %collective-permute-done.2 = f32[8,8,256]{2,1,0:T(8,128)S(1)} collective-permute-done((f32[8,8,256]{2,1,0:T(8,128)S(1)}, f32[8,8,256]{2,1,0:T(8,128)S(1)}, u32[]{:S(2)}, u32[]{:S(2)}) %collective-permute-start.2) | collective-permute-done | bytes 65568 | tf_op jit(solution)/shard_map/ppermute | solution.py:516
  23.1 6.1 %collective-permute-start.3 = (f32[8,8,256]{2,1,0:T(8,128)S(1)}, f32[8,8,256]{2,1,0:T(8,128)S(1)}, u32[]{:S(2)}, u32[]{:S(2)}) collective-permute-start(f32[8,8,256]{2,1,0:T(8,128)S(1)} %collective-permute-done.2), channel_id=1, source_target_pairs={{0,4},{2,6},{4,8},{6,10},{8,12},{10,14},{12,16},{14,18},{16,20},{1... | collective-permute-start | bytes 196616 | tf_op jit(solution)/shard_map/ppermute | solution.py:32
  29.2 2.2 %shard_map.95 = (f32[16,72,256]{2,1,0:T(8,128)S(1)}, f32[16,72,256]{2,1,0:T(8,128)S(1)}, f32[6,16,72,256]{3,2,1,0:T(8,128)S(1)}, f32[16,72,256]{2,1,0:T(8,128)S(1)}, f32[10,72,256]{2,1,0:T(8,128)S(1)}) custom-call(f32[16,64,256]{2,1,0:T(8,128)S(1)} %copy-done, f32[16,64,256]{2,1,0:T(8,128)S(1)} %copy-done.1, f32[2,64,256]{2,1,0:T(8,128)S(1)} %get-tuple-element.29.pads, ...), custom_call_target="tpu_custom_call" | custom-call | tf_op jit(solution)/shard_map/pallas_call | solution.py:560
  31.5 5.5 %collective-permute-done.3.refs_0_ = f32[8,8,256]{2,1,0:T(8,128)S(1)} collective-permute-done((f32[8,8,256]{2,1,0:T(8,128)S(1)}, f32[8,8,256]{2,1,0:T(8,128)S(1)}, u32[]{:S(2)}, u32[]{:S(2)}) %collective-permute-start.3) | collective-permute-done | bytes 65568 | tf_op jit(solution)/shard_map/ppermute | solution.py:32
  38.3 6.0 %collective-permute-start.5 = (f32[3,72,256]{2,1,0:T(8,128)S(1)}, f32[3,72,256]{2,1,0:T(8,128)S(1)}, u32[]{:S(2)}, u32[]{:S(2)}) collective-permute-start(f32[3,72,256]{2,1,0:T(8,128)S(1)} %get-tuple-element.39), channel_id=1, source_target_pairs={{0,2},{2,0},{4,6},{6,4},{8,10},{10,8},{12,14},{14,12},{16,18},{18,... | collective-permute-start | bytes 663560 | tf_op jit(solution)/shard_map/ppermute | solution.py:584
  44.3 2.2 %shard_map.98 = (f32[16,64,256]{2,1,0:T(8,128)}, f32[8,72,256]{2,1,0:T(8,128)S(1)}, f32[72,256]{1,0:T(8,128)S(1)}, f32[2,3,2,72,256]{4,3,2,1,0:T(8,128)S(1)}) custom-call(f32[16,72,256]{2,1,0:T(8,128)S(1)} %get-tuple-element.31.p0, f32[6,16,72,256]{3,2,1,0:T(8,128)S(1)} %get-tuple-element.32.w, f32[16,72,256]{2,1,0:T(8,128)S(1)} %get-tuple-element.35.b.b_in, ...), custom_call_target="tpu_custom_call" | custom-call | tf_op jit(solution)/shard_map/pallas_call | solution.py:585
  47.1 1.4 %shard_map.100 = (f32[4,72,256]{2,1,0:T(8,128)S(1)}, f32[72,256]{1,0:T(8,128)S(1)}) custom-call(f32[11,72,256]{2,1,0:T(8,128)S(1)} %collective-permute-done.4.inner, f32[3,72,256]{2,1,0:T(8,128)S(1)} %collective-permute-done.5.swapped, f32[16,72,256]{2,1,0:T(8,128)S(1)} %get-tuple-element.40.ex, f32[10,72,256]{2,1,0:T(8,128)S(1)} %get-tuple-element.34.geo, ...), custom_call_target="tpu_custom_call" | custom-call | tf_op jit(solution)/shard_map/pallas_call | solution.py:599
  48.5 0.9 %shard_map.102 = (f32[4,72,256]{2,1,0:T(8,128)S(1)}, f32[72,256]{1,0:T(8,128)S(1)}) custom-call(f32[4,72,256]{2,1,0:T(8,128)S(1)} %collective-permute-done.6.outer_phi, f32[16,72,256]{2,1,0:T(8,128)S(1)} %get-tuple-element.31.p0, f32[6,16,72,256]{3,2,1,0:T(8,128)S(1)} %get-tuple-element.32.w, f32[6,4,72,256]{3,2,1,0:T(8,128)S(1)} %get-tuple-element.48.wb, ...), custom_call_target="tpu_custom_call" | custom-call | tf_op jit(solution)/shard_map/pallas_call | solution.py:606
  49.5 1.3 %collective-permute-done.9 = f32[72,256]{1,0:T(8,128)S(1)} collective-permute-done((f32[72,256]{1,0:T(8,128)S(1)}, f32[72,256]{1,0:T(8,128)S(1)}, u32[]{:S(2)}, u32[]{:S(2)}) %collective-permute-start.9) | collective-permute-done | bytes 73760 | tf_op jit(solution)/shard_map/ppermute | solution.py:483
  50.7 2.3 %collective-permute-start.10 = (f32[72,256]{1,0:T(8,128)S(1)}, f32[72,256]{1,0:T(8,128)S(1)}, u32[]{:S(2)}, u32[]{:S(2)}) collective-permute-start(f32[72,256]{1,0:T(8,128)S(1)} %add.18), channel_id=1, source_target_pairs={{0,4},{2,6},{4,0},{6,2},{8,12},{10,14},{12,8},{14,10},{16,20},{18,... | collective-permute-start | bytes 221192 | tf_op jit(solution)/shard_map/ppermute | solution.py:483
  53.0 2.6 %collective-permute-done.10 = f32[72,256]{1,0:T(8,128)S(1)} collective-permute-done((f32[72,256]{1,0:T(8,128)S(1)}, f32[72,256]{1,0:T(8,128)S(1)}, u32[]{:S(2)}, u32[]{:S(2)}) %collective-permute-start.10) | collective-permute-done | bytes 73760 | tf_op jit(solution)/shard_map/ppermute | solution.py:483
  55.6 2.3 %collective-permute-start.11 = (f32[72,256]{1,0:T(8,128)S(1)}, f32[72,256]{1,0:T(8,128)S(1)}, u32[]{:S(2)}, u32[]{:S(2)}) collective-permute-start(f32[72,256]{1,0:T(8,128)S(1)} %add.20), channel_id=1, source_target_pairs={{0,8},{2,10},{4,12},{6,14},{8,0},{10,2},{12,4},{14,6},{16,24},{18,... | collective-permute-start | bytes 221192 | tf_op jit(solution)/shard_map/ppermute | solution.py:483
  57.9 2.3 %collective-permute-done.11 = f32[72,256]{1,0:T(8,128)S(1)} collective-permute-done((f32[72,256]{1,0:T(8,128)S(1)}, f32[72,256]{1,0:T(8,128)S(1)}, u32[]{:S(2)}, u32[]{:S(2)}) %collective-permute-start.11) | collective-permute-done | bytes 73760 | tf_op jit(solution)/shard_map/ppermute | solution.py:483
  60.2 3.1 %collective-permute-start.12 = (f32[72,256]{1,0:T(8,128)S(1)}, f32[72,256]{1,0:T(8,128)S(1)}, u32[]{:S(2)}, u32[]{:S(2)}) collective-permute-start(f32[72,256]{1,0:T(8,128)S(1)} %add.22), channel_id=1, source_target_pairs={{0,16},{2,18},{4,20},{6,22},{8,24},{10,26},{12,28},{14,30},{16,0},... | collective-permute-start | bytes 221192 | tf_op jit(solution)/shard_map/ppermute | solution.py:483
  63.3 2.6 %shard_map.103 = (f32[16,64,256]{2,1,0:T(8,128)}, f32[2,16,64,256]{3,2,1,0:T(8,128)S(1)}) custom-call(f32[4,72,256]{2,1,0:T(8,128)S(1)} %get-tuple-element.43.near, f32[8,72,256]{2,1,0:T(8,128)S(1)} %get-tuple-element.44.inner, f32[4,72,256]{2,1,0:T(8,128)S(1)} %get-tuple-element.51.far), custom_call_target="tpu_custom_call" | custom-call | tf_op jit(solution)/shard_map/pallas_call | solution.py:613
  66.0 1.6 %shard_map.104 = f32[2,16,64,256]{3,2,1,0:T(8,128)} custom-call(f32[2,16,64,256]{3,2,1,0:T(8,128)S(1)} %get-tuple-element.53.local, f32[72,256]{1,0:T(8,128)S(1)} %select_add_fusion.prefix), custom_call_target="tpu_custom_call" | custom-call | tf_op jit(solution)/shard_map/pallas_call | solution.py:621
  (21 shorter events, 2.7 us)
Async XLA Ops:
  0.6 37.0 %collective-permute-start.1 = (f32[16,64,256]{2,1,0:T(8,128)}, f32[16,64,256]{2,1,0:T(8,128)S(1)}, u32[]{:S(2)}, u32[]{:S(2)}) collective-permute-start(f32[16,64,256]{2,1,0:T(8,128)} %ions.5), channel_id=1, source_target_pairs={{0,4},{2,6},{4,8},{6,10},{8,12},{10,14},{12,16},{14,18},{16,20},{1... | collective-permute-start | bytes 3145736 | tf_op jit(solution)/shard_map/ppermute | solution.py:32
  6.8 9.2 %collective-permute-start = (f32[40,8,256]{2,1,0:T(8,128)S(1)}, f32[40,8,256]{2,1,0:T(8,128)S(1)}, u32[]{:S(2)}, u32[]{:S(2)}) collective-permute-start(f32[40,8,256]{2,1,0:T(8,128)S(1)} %get-tuple-element.30), channel_id=1, source_target_pairs={{0,1},{1,0},{2,3},{3,2},{4,5},{5,4},{6,7},{7,6},{8,9},{9,8},{10,11... | collective-permute-start | bytes 983048 | tf_op jit(solution)/shard_map/ppermute | solution.py:516
  16.0 13.2 %copy-start.1 = (f32[16,64,256]{2,1,0:T(8,128)S(1)}, f32[16,64,256]{2,1,0:T(8,128)}, u32[]{:S(2)}) copy-start(f32[16,64,256]{2,1,0:T(8,128)} %eps.5) | copy-start | bytes 3145732
  17.6 11.7 %copy-start = (f32[16,64,256]{2,1,0:T(8,128)S(1)}, f32[16,64,256]{2,1,0:T(8,128)}, u32[]{:S(2)}) copy-start(f32[16,64,256]{2,1,0:T(8,128)} %phi.5) | copy-start | bytes 3145732
  17.6 29.0 %collective-permute-start.4 = (f32[11,72,256]{2,1,0:T(8,128)S(1)}, f32[11,72,256]{2,1,0:T(8,128)S(1)}, u32[]{:S(2)}, u32[]{:S(2)}) collective-permute-start(f32[11,72,256]{2,1,0:T(8,128)S(1)} %get-tuple-element.38), channel_id=1, source_target_pairs={{0,2},{2,0},{4,6},{6,4},{8,10},{10,8},{12,14},{14,12},{16,18},{18,... | collective-permute-start | bytes 2433032 | tf_op jit(solution)/shard_map/ppermute | solution.py:556
  18.7 4.5 %collective-permute-start.2 = (f32[8,8,256]{2,1,0:T(8,128)S(1)}, f32[8,8,256]{2,1,0:T(8,128)S(1)}, u32[]{:S(2)}, u32[]{:S(2)}) collective-permute-start(f32[8,8,256]{2,1,0:T(8,128)S(1)} %shard_map.96), channel_id=1, source_target_pairs={{0,1},{1,0},{2,3},{3,2},{4,5},{5,4},{6,7},{7,6},{8,9},{9,8},{10,11... | collective-permute-start | bytes 196616 | tf_op jit(solution)/shard_map/ppermute | solution.py:516
  20.2 26.3 %collective-permute-start.7 = (f32[4,72,256]{2,1,0:T(8,128)S(1)}, f32[4,72,256]{2,1,0:T(8,128)S(1)}, u32[]{:S(2)}, u32[]{:S(2)}) collective-permute-start(f32[4,72,256]{2,1,0:T(8,128)S(1)} %get-tuple-element.46), channel_id=1, source_target_pairs={{2,4},{4,2},{6,8},{8,6},{10,12},{12,10},{14,16},{16,14},{18,20},{2... | collective-permute-start | bytes 884744 | tf_op jit(solution)/shard_map/ppermute | solution.py:554
  20.9 27.6 %collective-permute-start.6 = (f32[4,72,256]{2,1,0:T(8,128)S(1)}, f32[4,72,256]{2,1,0:T(8,128)S(1)}, u32[]{:S(2)}, u32[]{:S(2)}) collective-permute-start(f32[4,72,256]{2,1,0:T(8,128)S(1)} %get-tuple-element.45), channel_id=1, source_target_pairs={{2,4},{4,2},{6,8},{8,6},{10,12},{12,10},{14,16},{16,14},{18,20},{2... | collective-permute-start | bytes 884744 | tf_op jit(solution)/shard_map/ppermute | solution.py:557
  23.1 13.8 %collective-permute-start.3 = (f32[8,8,256]{2,1,0:T(8,128)S(1)}, f32[8,8,256]{2,1,0:T(8,128)S(1)}, u32[]{:S(2)}, u32[]{:S(2)}) collective-permute-start(f32[8,8,256]{2,1,0:T(8,128)S(1)} %collective-permute-done.2), channel_id=1, source_target_pairs={{0,4},{2,6},{4,8},{6,10},{8,12},{10,14},{12,16},{14,18},{16,20},{1... | collective-permute-start | bytes 196616 | tf_op jit(solution)/shard_map/ppermute | solution.py:32
  37.0 9.6 %collective-permute-start.8 = (f32[3,72,256]{2,1,0:T(8,128)S(1)}, f32[3,72,256]{2,1,0:T(8,128)S(1)}, u32[]{:S(2)}, u32[]{:S(2)}) collective-permute-start(f32[3,72,256]{2,1,0:T(8,128)S(1)} %get-tuple-element.47), channel_id=1, source_target_pairs={{2,8},{6,12},{10,16},{14,20},{18,24},{22,28},{3,9},{7,13},{11,17},... | collective-permute-start | bytes 663560 | tf_op jit(solution)/shard_map/ppermute | solution.py:555
  38.3 8.8 %collective-permute-start.5 = (f32[3,72,256]{2,1,0:T(8,128)S(1)}, f32[3,72,256]{2,1,0:T(8,128)S(1)}, u32[]{:S(2)}, u32[]{:S(2)}) collective-permute-start(f32[3,72,256]{2,1,0:T(8,128)S(1)} %get-tuple-element.39), channel_id=1, source_target_pairs={{0,2},{2,0},{4,6},{6,4},{8,10},{10,8},{12,14},{14,12},{16,18},{18,... | collective-permute-start | bytes 663560 | tf_op jit(solution)/shard_map/ppermute | solution.py:584
  49.4 1.3 %collective-permute-start.9 = (f32[72,256]{1,0:T(8,128)S(1)}, f32[72,256]{1,0:T(8,128)S(1)}, u32[]{:S(2)}, u32[]{:S(2)}) collective-permute-start(f32[72,256]{1,0:T(8,128)S(1)} %get-tuple-element.54), channel_id=1, source_target_pairs={{0,2},{2,0},{4,6},{6,4},{8,10},{10,8},{12,14},{14,12},{16,18},{18,... | collective-permute-start | bytes 221192 | tf_op jit(solution)/shard_map/ppermute | solution.py:483
  50.7 4.8 %collective-permute-start.10 = (f32[72,256]{1,0:T(8,128)S(1)}, f32[72,256]{1,0:T(8,128)S(1)}, u32[]{:S(2)}, u32[]{:S(2)}) collective-permute-start(f32[72,256]{1,0:T(8,128)S(1)} %add.18), channel_id=1, source_target_pairs={{0,4},{2,6},{4,0},{6,2},{8,12},{10,14},{12,8},{14,10},{16,20},{18,... | collective-permute-start | bytes 221192 | tf_op jit(solution)/shard_map/ppermute | solution.py:483
  55.6 4.6 %collective-permute-start.11 = (f32[72,256]{1,0:T(8,128)S(1)}, f32[72,256]{1,0:T(8,128)S(1)}, u32[]{:S(2)}, u32[]{:S(2)}) collective-permute-start(f32[72,256]{1,0:T(8,128)S(1)} %add.20), channel_id=1, source_target_pairs={{0,8},{2,10},{4,12},{6,14},{8,0},{10,2},{12,4},{14,6},{16,24},{18,... | collective-permute-start | bytes 221192 | tf_op jit(solution)/shard_map/ppermute | solution.py:483
  60.2 5.7 %collective-permute-start.12 = (f32[72,256]{1,0:T(8,128)S(1)}, f32[72,256]{1,0:T(8,128)S(1)}, u32[]{:S(2)}, u32[]{:S(2)}) collective-permute-start(f32[72,256]{1,0:T(8,128)S(1)} %add.22), channel_id=1, source_target_pairs={{0,16},{2,18},{4,20},{6,22},{8,24},{10,26},{12,28},{14,30},{16,0},... | collective-permute-start | bytes 221192 | tf_op jit(solution)/shard_map/ppermute | solution.py:483

commit v7 on v6

--- a/solution.py
+++ b/solution.py
@@ -135,8 +135,6 @@
         (inner, 0, 0, near_at, near_at, depth),
         (inner, depth, 1, near_at, layers + near_at, depth),
         (inner, 2 * depth, 2, 0, ends, depth - 1),
-        (outer_eps, 0, 1, far_at, layers + far_at, depth),
-        (outer_phi, 0, 0, far_at, far_at, depth),
         (far, 0, 2, layers - depth + 1, ends + depth - 1, depth - 1),
     ):
         src = (phi, eps, ions)[k]
@@ -144,8 +142,37 @@
         for side, raw in enumerate(raws):
             rows = slice(band + side * ROWS, band + (side + 1) * ROWS)
             copies.append((raw.at[pl.ds(raw_at, count)], dst.at[at : at + count, rows]))
-    for copy in run_all(copies, sems):
+    for dst, src in ((outer_eps, eps), (outer_phi, phi)):
+        for k in range(depth):
+            copies.append((src.at[far_at + k], dst.at[k * band : (k + 1) * band]))
+    running = run_all(copies, sems)
+    sector = phi.shape[2]
+    first_half = lax.broadcasted_iota(jnp.int32, (ROWS, sector), 0) < ROWS // 2
+    for side, raw in enumerate(raws):
+        above = (lax.axis_index("radius") == 0) if sides == 1 else side == 0
+        for dst, base in ((outer_eps, layers), (outer_phi, 0)):
+            for j in range(depth // 2):
+                one, two = raw[base + far_at + 2 * j], raw[base + far_at + 2 * j + 1]
+                from_above = jnp.where(first_half, one, roll(two, ROWS // 2, 0))
+                from_below = jnp.where(first_half, roll(one, ROWS // 2, 0), two)
+                at = depth * band + (side * (depth // 2) + j) * ROWS
+                dst[at : at + ROWS] = jnp.where(above, from_above, from_below)
+    for copy in running:
         copy.wait()
+
+
+def unpack_halo(packed, halo, band):
+    depth = SWEEPS
+    sides = (halo.shape[1] - band) // ROWS
+    for k in range(depth):
+        halo[k, 0:band] = packed[k * band : (k + 1) * band]
+        for side in range(sides):
+            above = (lax.axis_index("radius") == 0) if sides == 1 else side == 0
+            at = depth * band + (side * (depth // 2) + k // 2) * ROWS
+            two = packed[at : at + ROWS]
+            turned = roll(two, ROWS // 2, 0)
+            rows = slice(band + side * ROWS, band + (side + 1) * ROWS)
+            halo[k, rows] = jnp.where(above, two, turned) if k % 2 == 0 else jnp.where(above, turned, two)
 
 
 def coupling_rows(z, ex, z_up, z_down, geo, alive, tiles, sub, put):
@@ -380,7 +407,7 @@
     wedge_sweeps(wedge, inner, p0, w, wb, bb, state, b_in, q_buf, out, sums_out)
 
 
-def outer_coupling_kernel(inner, outer_eps, far, ex, geo, wb, bb, eh):
+def outer_coupling_kernel(band, inner, outer_eps, far, ex, geo, wb, bb, eh, halo):
     wedge = Wedge(False, ex.shape[0])
     ends = SWEEPS - 1
 
@@ -389,17 +416,19 @@
         ions = jnp.where(wedge.is_high, inner[2 * SWEEPS + spot], far[spot])
         return drift_charge(ions, geo[6], geo[7], jnp.where(wedge.is_high, wedge.d + 1, wedge.d - 1))
 
-    wedge_couplings(wedge, outer_eps, 0, charge, ex, geo, wb, bb, eh)
-
-
-def outer_relax_kernel(outer_phi, p0, w, wb, bb_in, state, b_in, sums_in, out, sums_out, bb, q_buf):
+    unpack_halo(outer_eps, halo, band)
+    wedge_couplings(wedge, halo, 0, charge, ex, geo, wb, bb, eh)
+
+
+def outer_relax_kernel(band, outer_phi, p0, w, wb, bb_in, state, b_in, sums_in, out, sums_out, bb, q_buf, halo):
     wedge = Wedge(False, p0.shape[0])
     ends = SWEEPS - 1
     for k in range(ends):
         bb[k] = bb_in[k]
     bb[ends] = bb_in[ends] * b_in[wedge.own(0)]
     sums_out[...] = sums_in[...]
-    wedge_sweeps(wedge, outer_phi, p0, w, wb, bb, state, b_in, q_buf, out, sums_out)
+    unpack_halo(outer_phi, halo, band)
+    wedge_sweeps(wedge, halo, p0, w, wb, bb, state, b_in, q_buf, out, sums_out)
 
 
 def local_kernel(near, inner, far, potential, out, run):
@@ -540,11 +569,17 @@
     )(phi, eps, ions_far, *pad_args)
     raws = swap_rows(blocks)
     rows_moved = [shifted(raw, "drift", 2) for raw in ion_raws]
+    packed = depth * band + sides * (depth // 2) * ROWS
     to_core, eps_block, phi_block, beyond = kernel(
         functools.partial(halo_kernel, sides),
-        [plane(k, rows, sector) for k in (3 * depth - 1, depth, depth, depth - 1)],
+        [
+            plane(3 * depth - 1, rows, sector),
+            plane(packed, sector),
+            plane(packed, sector),
+            plane(depth - 1, rows, sector),
+        ],
         [ANYWHERE] * 3 + [IN_VMEM] * sides,
-        scratch=[dma((6 * (1 + sides),))],
+        scratch=[dma((4 * (1 + sides) + 2 * depth,))],
         mb=6,
     )(phi, eps, ions_far, *raws)
     count = lax.axis_size("drift")
@@ -567,10 +602,10 @@
     wedge = plane(depth, rows, sector)
     wedge_box, wedge_couplings_box = near(depth, rows, sector), near(6, depth, rows, sector)
     wb, bb = kernel(
-        outer_coupling_kernel,
+        functools.partial(outer_coupling_kernel, band),
         [plane(6, depth, rows, sector), wedge],
         [IN_VMEM] * 5,
-        scratch=[near(depth + 2, rows, sector)],
+        scratch=[near(depth + 2, rows, sector), wedge_box],
         mb=12,
     )(inner, outer_eps, far, ex, geo)
     wb, bb = fetched(wb), fetched(bb)
@@ -604,10 +639,10 @@
         mb=12,
     )(inner, swapped, ex, geo, p0, w, state, b, sums)
     far_out, sums = kernel(
-        outer_relax_kernel,
+        functools.partial(outer_relax_kernel, band),
         [wedge, plane(rows, sector)],
         [IN_VMEM] * 8,
-        scratch=[wedge_box, near(depth - 1, depth, rows, sector)],
+        scratch=[wedge_box, near(depth - 1, depth, rows, sector), wedge_box],
         mb=12,
     )(outer_phi, p0, w, wb, bb, state, b, fetched(sums))
     potential, local = kernel(

time: 67.9 us -> 62.8 us (0.925)
  waiting for transfers between devices: 20.9 us -> 17.5 us
  starting transfers between devices: 30 us -> 28.2 us
    ppermute x2, waiting for transfers between devices: 5.49 us -> 0.01 us  [shifted(): return lax.ppermute(block, axis, route)]
    ppermute x2, starting transfers between devices: 11 us -> 8.32 us  [shifted(): return lax.ppermute(block, axis, route)]
    ppermute x1, starting transfers between devices: 6 us -> 8.11 us  [body(): swapped = lax.ppermute(swap, 'drift', partners)]
    ppermute x2, waiting for transfers between devices: 9.19 us -> 10.6 us  [swap_rows(): return [lax.ppermute(blocks[0], 'radius', [(0, 1), (1, 0)])]]
    ppermute x4, starting transfers between devices: 7.72 us -> 6.54 us  [sums_below(): other = lax.ppermute(total, 'drift', [(i, i ^ step) for i in range(count)])]
    ppermute x4, waiting for transfers between devices: 6.18 us -> 6.94 us  [sums_below(): other = lax.ppermute(total, 'drift', [(i, i ^ step) for i in range(count)])]
  transfers between devices with their start and end apart: 13 -> 13, of which waited for: 6 -> 5; matrix products, arithmetic and copies ran while one was open for 0% -> 0% of each run, Pallas kernels for 20% -> 21%
where the time goes in v7:
time: 62.8 us; the launch traced here: 62.6 us
  starting transfers between devices  28.2 us (45%)
  waiting for transfers between devices  17.5 us (28%)
  Pallas kernels  15.9 us (25%)
  between operations  0.85 us (1%)
    ppermute x2, waiting for transfers between devices, swap_rows(): return [lax.ppermute(blocks[0], 'radius', [(0, 1), (1, 0)])]  10.6 us
    ppermute x2, starting transfers between devices, shifted(): return lax.ppermute(block, axis, route)  8.32 us
    ppermute x1, starting transfers between devices, body(): swapped = lax.ppermute(swap, 'drift', partners)  8.11 us
    ppermute x4, waiting for transfers between devices, sums_below(): other = lax.ppermute(total, 'drift', [(i, i ^ step) for i in range(count)])  6.94 us
    ppermute x4, starting transfers between devices, sums_below(): other = lax.ppermute(total, 'drift', [(i, i ^ step) for i in range(count)])  6.54 us
    ppermute x2, starting transfers between devices, swap_rows(): return [lax.ppermute(blocks[0], 'radius', [(0, 1), (1, 0)])]  3.16 us
    pallas_call x1, Pallas kernels, body(): kernel(local_kernel, [plane(layers, band, sector), plane(2, layers, band,...  2.64 us
    pallas_call x1, Pallas kernels, body(): kernel(functools.partial(inner_coupling_kernel, sides), [box, box, plane(...  2.25 us
  transfers between devices with their start and end apart: 13, of which 5 were waited for; matrix products, arithmetic and copies ran while one was open for 0% of the time, Pallas kernels for 21%

profile of v7, /device:TPU:0, one launch (start us, length us, event | category | flops | bytes accessed | tf_op | source)
XLA Modules:
  0.0 62.6 jit_solution(366424097450839911)
XLA Ops:
  0.6 4.9 %collective-permute-start.1 = (f32[16,64,256]{2,1,0:T(8,128)}, f32[16,64,256]{2,1,0:T(8,128)S(1)}, u32[]{:S(2)}, u32[]{:S(2)}) collective-permute-start(f32[16,64,256]{2,1,0:T(8,128)} %ions.5), channel_id=1, source_target_pairs={{0,4},{2,6},{4,8},{6,10},{8,12},{10,14},{12,16},{14,18},{16,20},{1... | collective-permute-start | bytes 3145736 | tf_op jit(solution)/shard_map/ppermute | solution.py:32
  5.6 1.2 %shard_map.94 = (f32[40,8,256]{2,1,0:T(8,128)S(1)}, f32[2,64,256]{2,1,0:T(8,128)S(1)}) custom-call(f32[16,64,256]{2,1,0:T(8,128)} %phi.5, f32[16,64,256]{2,1,0:T(8,128)} %eps.5, f32[16,64,256]{2,1,0:T(8,128)} %ions.5, f32[64,256]{1,0:T(8,128)} %rec.1, s32[64,256]{1,0:T(8,128)} %index.1, s32[64,256]{1,0:T(8,128)} %gap.1, f32[16]{0:T(128)} %table.1), custom_call_target="tpu_custom_call" | custom-call | tf_op jit(solution)/shard_map/pallas_call | solution.py:556
  6.8 1.6 %collective-permute-start = (f32[40,8,256]{2,1,0:T(8,128)S(1)}, f32[40,8,256]{2,1,0:T(8,128)S(1)}, u32[]{:S(2)}, u32[]{:S(2)}) collective-permute-start(f32[40,8,256]{2,1,0:T(8,128)S(1)} %get-tuple-element.30), channel_id=1, source_target_pairs={{0,1},{1,0},{2,3},{3,2},{4,5},{5,4},{6,7},{7,6},{8,9},{9,8},{10,11... | collective-permute-start | bytes 983048 | tf_op jit(solution)/shard_map/ppermute | solution.py:545
  8.4 7.7 %collective-permute-done.refs_0_ = f32[40,8,256]{2,1,0:T(8,128)S(1)} collective-permute-done((f32[40,8,256]{2,1,0:T(8,128)S(1)}, f32[40,8,256]{2,1,0:T(8,128)S(1)}, u32[]{:S(2)}, u32[]{:S(2)}) %collective-permute-start) | collective-permute-done | bytes 327712 | tf_op jit(solution)/shard_map/ppermute | solution.py:545
  16.0 1.5 %shard_map.99 = (f32[11,72,256]{2,1,0:T(8,128)S(1)}, f32[272,256]{1,0:T(8,128)S(1)}, f32[272,256]{1,0:T(8,128)S(1)}, f32[3,72,256]{2,1,0:T(8,128)S(1)}) custom-call(f32[16,64,256]{2,1,0:T(8,128)} %phi.5, f32[16,64,256]{2,1,0:T(8,128)} %eps.5, f32[16,64,256]{2,1,0:T(8,128)} %ions.5, f32[40,8,256]{2,1,0:T(8,128)S(1)} %collective-permute-done.refs_0_), custom_call_target="tpu_custom_call" | custom-call | tf_op jit(solution)/shard_map/pallas_call | solution.py:573
  17.6 1.0 %shard_map.96 = f32[8,8,256]{2,1,0:T(8,128)S(1)} custom-call(f32[16,64,256]{2,1,0:T(8,128)} %ions.5), custom_call_target="tpu_custom_call" | custom-call | tf_op jit(solution)/shard_map/pallas_call | solution.py:548
  18.6 1.6 %collective-permute-start.2 = (f32[8,8,256]{2,1,0:T(8,128)S(1)}, f32[8,8,256]{2,1,0:T(8,128)S(1)}, u32[]{:S(2)}, u32[]{:S(2)}) collective-permute-start(f32[8,8,256]{2,1,0:T(8,128)S(1)} %shard_map.96), channel_id=1, source_target_pairs={{0,1},{1,0},{2,3},{3,2},{4,5},{5,4},{6,7},{7,6},{8,9},{9,8},{10,11... | collective-permute-start | bytes 196616 | tf_op jit(solution)/shard_map/ppermute | solution.py:545
  20.2 2.9 %collective-permute-done.2 = f32[8,8,256]{2,1,0:T(8,128)S(1)} collective-permute-done((f32[8,8,256]{2,1,0:T(8,128)S(1)}, f32[8,8,256]{2,1,0:T(8,128)S(1)}, u32[]{:S(2)}, u32[]{:S(2)}) %collective-permute-start.2) | collective-permute-done | bytes 65568 | tf_op jit(solution)/shard_map/ppermute | solution.py:545
  23.1 3.4 %collective-permute-start.3 = (f32[8,8,256]{2,1,0:T(8,128)S(1)}, f32[8,8,256]{2,1,0:T(8,128)S(1)}, u32[]{:S(2)}, u32[]{:S(2)}) collective-permute-start(f32[8,8,256]{2,1,0:T(8,128)S(1)} %collective-permute-done.2), channel_id=1, source_target_pairs={{0,4},{2,6},{4,8},{6,10},{8,12},{10,14},{12,16},{14,18},{16,20},{1... | collective-permute-start | bytes 196616 | tf_op jit(solution)/shard_map/ppermute | solution.py:32
  26.5 0.7 %collective-permute-start.7 = (f32[272,256]{1,0:T(8,128)S(1)}, f32[272,256]{1,0:T(8,128)S(1)}, u32[]{:S(2)}, u32[]{:S(2)}) collective-permute-start(f32[272,256]{1,0:T(8,128)S(1)} %get-tuple-element.46), channel_id=1, source_target_pairs={{2,4},{4,2},{6,8},{8,6},{10,12},{12,10},{14,16},{16,14},{18,20},{2... | collective-permute-start | bytes 835592 | tf_op jit(solution)/shard_map/ppermute | solution.py:589
  27.2 0.7 %collective-permute-start.6 = (f32[272,256]{1,0:T(8,128)S(1)}, f32[272,256]{1,0:T(8,128)S(1)}, u32[]{:S(2)}, u32[]{:S(2)}) collective-permute-start(f32[272,256]{1,0:T(8,128)S(1)} %get-tuple-element.45), channel_id=1, source_target_pairs={{2,4},{4,2},{6,8},{8,6},{10,12},{12,10},{14,16},{16,14},{18,20},{2... | collective-permute-start | bytes 835592 | tf_op jit(solution)/shard_map/ppermute | solution.py:592
  27.9 2.2 %shard_map.95 = (f32[16,72,256]{2,1,0:T(8,128)S(1)}, f32[16,72,256]{2,1,0:T(8,128)S(1)}, f32[6,16,72,256]{3,2,1,0:T(8,128)S(1)}, f32[16,72,256]{2,1,0:T(8,128)S(1)}, f32[10,72,256]{2,1,0:T(8,128)S(1)}) custom-call(f32[16,64,256]{2,1,0:T(8,128)S(1)} %copy-done, f32[16,64,256]{2,1,0:T(8,128)S(1)} %copy-done.1, f32[2,64,256]{2,1,0:T(8,128)S(1)} %get-tuple-element.29.pads, ...), custom_call_target="tpu_custom_call" | custom-call | tf_op jit(solution)/shard_map/pallas_call | solution.py:595
  31.5 8.1 %collective-permute-start.5 = (f32[3,72,256]{2,1,0:T(8,128)S(1)}, f32[3,72,256]{2,1,0:T(8,128)S(1)}, u32[]{:S(2)}, u32[]{:S(2)}) collective-permute-start(f32[3,72,256]{2,1,0:T(8,128)S(1)} %get-tuple-element.39), channel_id=1, source_target_pairs={{0,2},{2,0},{4,6},{6,4},{8,10},{10,8},{12,14},{14,12},{16,18},{18,... | collective-permute-start | bytes 663560 | tf_op jit(solution)/shard_map/ppermute | solution.py:619
  39.6 2.2 %shard_map.98 = (f32[16,64,256]{2,1,0:T(8,128)}, f32[8,72,256]{2,1,0:T(8,128)S(1)}, f32[72,256]{1,0:T(8,128)S(1)}, f32[2,3,2,72,256]{4,3,2,1,0:T(8,128)S(1)}) custom-call(f32[16,72,256]{2,1,0:T(8,128)S(1)} %get-tuple-element.31.p0, f32[6,16,72,256]{3,2,1,0:T(8,128)S(1)} %get-tuple-element.32.w, f32[16,72,256]{2,1,0:T(8,128)S(1)} %get-tuple-element.35.b.b_in, ...), custom_call_target="tpu_custom_call" | custom-call | tf_op jit(solution)/shard_map/pallas_call | solution.py:620
  42.4 1.4 %shard_map.100 = (f32[4,72,256]{2,1,0:T(8,128)S(1)}, f32[72,256]{1,0:T(8,128)S(1)}) custom-call(f32[11,72,256]{2,1,0:T(8,128)S(1)} %collective-permute-done.4.inner, f32[3,72,256]{2,1,0:T(8,128)S(1)} %collective-permute-done.5.swapped, f32[16,72,256]{2,1,0:T(8,128)S(1)} %get-tuple-element.40.ex, f32[10,72,256]{2,1,0:T(8,128)S(1)} %get-tuple-element.34.geo, ...), custom_call_target="tpu_custom_call" | custom-call | tf_op jit(solution)/shard_map/pallas_call | solution.py:634
  43.8 1.0 %shard_map.102 = (f32[4,72,256]{2,1,0:T(8,128)S(1)}, f32[72,256]{1,0:T(8,128)S(1)}) custom-call(f32[272,256]{1,0:T(8,128)S(1)} %collective-permute-done.6.outer_phi, f32[16,72,256]{2,1,0:T(8,128)S(1)} %get-tuple-element.31.p0, f32[6,16,72,256]{3,2,1,0:T(8,128)S(1)} %get-tuple-element.32.w, f32[6,4,72,256]{3,2,1,0:T(8,128)S(1)} %get-tuple-element.48.wb, ...), custom_call_target="tpu_custom_call" | custom-call | tf_op jit(solution)/shard_map/pallas_call | solution.py:641
  44.9 1.3 %collective-permute-done.9 = f32[72,256]{1,0:T(8,128)S(1)} collective-permute-done((f32[72,256]{1,0:T(8,128)S(1)}, f32[72,256]{1,0:T(8,128)S(1)}, u32[]{:S(2)}, u32[]{:S(2)}) %collective-permute-start.9) | collective-permute-done | bytes 73760 | tf_op jit(solution)/shard_map/ppermute | solution.py:512
  46.1 1.1 %collective-permute-start.10 = (f32[72,256]{1,0:T(8,128)S(1)}, f32[72,256]{1,0:T(8,128)S(1)}, u32[]{:S(2)}, u32[]{:S(2)}) collective-permute-start(f32[72,256]{1,0:T(8,128)S(1)} %add.18), channel_id=1, source_target_pairs={{0,4},{2,6},{4,0},{6,2},{8,12},{10,14},{12,8},{14,10},{16,20},{18,... | collective-permute-start | bytes 221192 | tf_op jit(solution)/shard_map/ppermute | solution.py:512
  47.2 3.4 %collective-permute-done.10 = f32[72,256]{1,0:T(8,128)S(1)} collective-permute-done((f32[72,256]{1,0:T(8,128)S(1)}, f32[72,256]{1,0:T(8,128)S(1)}, u32[]{:S(2)}, u32[]{:S(2)}) %collective-permute-start.10) | collective-permute-done | bytes 73760 | tf_op jit(solution)/shard_map/ppermute | solution.py:512
  50.6 2.3 %collective-permute-start.11 = (f32[72,256]{1,0:T(8,128)S(1)}, f32[72,256]{1,0:T(8,128)S(1)}, u32[]{:S(2)}, u32[]{:S(2)}) collective-permute-start(f32[72,256]{1,0:T(8,128)S(1)} %add.20), channel_id=1, source_target_pairs={{0,8},{2,10},{4,12},{6,14},{8,0},{10,2},{12,4},{14,6},{16,24},{18,... | collective-permute-start | bytes 221192 | tf_op jit(solution)/shard_map/ppermute | solution.py:512
  52.9 2.3 %collective-permute-done.11 = f32[72,256]{1,0:T(8,128)S(1)} collective-permute-done((f32[72,256]{1,0:T(8,128)S(1)}, f32[72,256]{1,0:T(8,128)S(1)}, u32[]{:S(2)}, u32[]{:S(2)}) %collective-permute-start.11) | collective-permute-done | bytes 73760 | tf_op jit(solution)/shard_map/ppermute | solution.py:512
  55.2 3.1 %collective-permute-start.12 = (f32[72,256]{1,0:T(8,128)S(1)}, f32[72,256]{1,0:T(8,128)S(1)}, u32[]{:S(2)}, u32[]{:S(2)}) collective-permute-start(f32[72,256]{1,0:T(8,128)S(1)} %add.22), channel_id=1, source_target_pairs={{0,16},{2,18},{4,20},{6,22},{8,24},{10,26},{12,28},{14,30},{16,0},... | collective-permute-start | bytes 221192 | tf_op jit(solution)/shard_map/ppermute | solution.py:512
  58.3 2.6 %shard_map.103 = (f32[16,64,256]{2,1,0:T(8,128)}, f32[2,16,64,256]{3,2,1,0:T(8,128)S(1)}) custom-call(f32[4,72,256]{2,1,0:T(8,128)S(1)} %get-tuple-element.43.near, f32[8,72,256]{2,1,0:T(8,128)S(1)} %get-tuple-element.44.inner, f32[4,72,256]{2,1,0:T(8,128)S(1)} %get-tuple-element.51.far), custom_call_target="tpu_custom_call" | custom-call | tf_op jit(solution)/shard_map/pallas_call | solution.py:648
  61.0 1.6 %shard_map.104 = f32[2,16,64,256]{3,2,1,0:T(8,128)} custom-call(f32[2,16,64,256]{3,2,1,0:T(8,128)S(1)} %get-tuple-element.53.local, f32[72,256]{1,0:T(8,128)S(1)} %select_add_fusion.prefix), custom_call_target="tpu_custom_call" | custom-call | tf_op jit(solution)/shard_map/pallas_call | solution.py:656
  (21 shorter events, 2.1 us)
Async XLA Ops:
  0.6 30.2 %collective-permute-start.1 = (f32[16,64,256]{2,1,0:T(8,128)}, f32[16,64,256]{2,1,0:T(8,128)S(1)}, u32[]{:S(2)}, u32[]{:S(2)}) collective-permute-start(f32[16,64,256]{2,1,0:T(8,128)} %ions.5), channel_id=1, source_target_pairs={{0,4},{2,6},{4,8},{6,10},{8,12},{10,14},{12,16},{14,18},{16,20},{1... | collective-permute-start | bytes 3145736 | tf_op jit(solution)/shard_map/ppermute | solution.py:32
  6.8 9.2 %collective-permute-start = (f32[40,8,256]{2,1,0:T(8,128)S(1)}, f32[40,8,256]{2,1,0:T(8,128)S(1)}, u32[]{:S(2)}, u32[]{:S(2)}) collective-permute-start(f32[40,8,256]{2,1,0:T(8,128)S(1)} %get-tuple-element.30), channel_id=1, source_target_pairs={{0,1},{1,0},{2,3},{3,2},{4,5},{5,4},{6,7},{7,6},{8,9},{9,8},{10,11... | collective-permute-start | bytes 983048 | tf_op jit(solution)/shard_map/ppermute | solution.py:545
  16.0 11.8 %copy-start.1 = (f32[16,64,256]{2,1,0:T(8,128)S(1)}, f32[16,64,256]{2,1,0:T(8,128)}, u32[]{:S(2)}) copy-start(f32[16,64,256]{2,1,0:T(8,128)} %eps.5) | copy-start | bytes 3145732
  17.5 10.4 %copy-start = (f32[16,64,256]{2,1,0:T(8,128)S(1)}, f32[16,64,256]{2,1,0:T(8,128)}, u32[]{:S(2)}) copy-start(f32[16,64,256]{2,1,0:T(8,128)} %phi.5) | copy-start | bytes 3145732
  17.6 24.3 %collective-permute-start.4 = (f32[11,72,256]{2,1,0:T(8,128)S(1)}, f32[11,72,256]{2,1,0:T(8,128)S(1)}, u32[]{:S(2)}, u32[]{:S(2)}) collective-permute-start(f32[11,72,256]{2,1,0:T(8,128)S(1)} %get-tuple-element.38), channel_id=1, source_target_pairs={{0,2},{2,0},{4,6},{6,4},{8,10},{10,8},{12,14},{14,12},{16,18},{18,... | collective-permute-start | bytes 2433032 | tf_op jit(solution)/shard_map/ppermute | solution.py:591
  18.6 4.5 %collective-permute-start.2 = (f32[8,8,256]{2,1,0:T(8,128)S(1)}, f32[8,8,256]{2,1,0:T(8,128)S(1)}, u32[]{:S(2)}, u32[]{:S(2)}) collective-permute-start(f32[8,8,256]{2,1,0:T(8,128)S(1)} %shard_map.96), channel_id=1, source_target_pairs={{0,1},{1,0},{2,3},{3,2},{4,5},{5,4},{6,7},{7,6},{8,9},{9,8},{10,11... | collective-permute-start | bytes 196616 | tf_op jit(solution)/shard_map/ppermute | solution.py:545
  23.1 7.0 %collective-permute-start.3 = (f32[8,8,256]{2,1,0:T(8,128)S(1)}, f32[8,8,256]{2,1,0:T(8,128)S(1)}, u32[]{:S(2)}, u32[]{:S(2)}) collective-permute-start(f32[8,8,256]{2,1,0:T(8,128)S(1)} %collective-permute-done.2), channel_id=1, source_target_pairs={{0,4},{2,6},{4,8},{6,10},{8,12},{10,14},{12,16},{14,18},{16,20},{1... | collective-permute-start | bytes 196616 | tf_op jit(solution)/shard_map/ppermute | solution.py:32
  26.5 15.3 %collective-permute-start.7 = (f32[272,256]{1,0:T(8,128)S(1)}, f32[272,256]{1,0:T(8,128)S(1)}, u32[]{:S(2)}, u32[]{:S(2)}) collective-permute-start(f32[272,256]{1,0:T(8,128)S(1)} %get-tuple-element.46), channel_id=1, source_target_pairs={{2,4},{4,2},{6,8},{8,6},{10,12},{12,10},{14,16},{16,14},{18,20},{2... | collective-permute-start | bytes 835592 | tf_op jit(solution)/shard_map/ppermute | solution.py:589
  27.2 16.6 %collective-permute-start.6 = (f32[272,256]{1,0:T(8,128)S(1)}, f32[272,256]{1,0:T(8,128)S(1)}, u32[]{:S(2)}, u32[]{:S(2)}) collective-permute-start(f32[272,256]{1,0:T(8,128)S(1)} %get-tuple-element.45), channel_id=1, source_target_pairs={{2,4},{4,2},{6,8},{8,6},{10,12},{12,10},{14,16},{16,14},{18,20},{2... | collective-permute-start | bytes 835592 | tf_op jit(solution)/shard_map/ppermute | solution.py:592
  30.2 11.7 %collective-permute-start.8 = (f32[3,72,256]{2,1,0:T(8,128)S(1)}, f32[3,72,256]{2,1,0:T(8,128)S(1)}, u32[]{:S(2)}, u32[]{:S(2)}) collective-permute-start(f32[3,72,256]{2,1,0:T(8,128)S(1)} %get-tuple-element.47), channel_id=1, source_target_pairs={{2,8},{6,12},{10,16},{14,20},{18,24},{22,28},{3,9},{7,13},{11,17},... | collective-permute-start | bytes 663560 | tf_op jit(solution)/shard_map/ppermute | solution.py:590
  31.5 10.9 %collective-permute-start.5 = (f32[3,72,256]{2,1,0:T(8,128)S(1)}, f32[3,72,256]{2,1,0:T(8,128)S(1)}, u32[]{:S(2)}, u32[]{:S(2)}) collective-permute-start(f32[3,72,256]{2,1,0:T(8,128)S(1)} %get-tuple-element.39), channel_id=1, source_target_pairs={{0,2},{2,0},{4,6},{6,4},{8,10},{10,8},{12,14},{14,12},{16,18},{18,... | collective-permute-start | bytes 663560 | tf_op jit(solution)/shard_map/ppermute | solution.py:619
  44.8 1.3 %collective-permute-start.9 = (f32[72,256]{1,0:T(8,128)S(1)}, f32[72,256]{1,0:T(8,128)S(1)}, u32[]{:S(2)}, u32[]{:S(2)}) collective-permute-start(f32[72,256]{1,0:T(8,128)S(1)} %get-tuple-element.54), channel_id=1, source_target_pairs={{0,2},{2,0},{4,6},{6,4},{8,10},{10,8},{12,14},{14,12},{16,18},{18,... | collective-permute-start | bytes 221192 | tf_op jit(solution)/shard_map/ppermute | solution.py:512
  46.1 4.4 %collective-permute-start.10 = (f32[72,256]{1,0:T(8,128)S(1)}, f32[72,256]{1,0:T(8,128)S(1)}, u32[]{:S(2)}, u32[]{:S(2)}) collective-permute-start(f32[72,256]{1,0:T(8,128)S(1)} %add.18), channel_id=1, source_target_pairs={{0,4},{2,6},{4,0},{6,2},{8,12},{10,14},{12,8},{14,10},{16,20},{18,... | collective-permute-start | bytes 221192 | tf_op jit(solution)/shard_map/ppermute | solution.py:512
  50.6 4.6 %collective-permute-start.11 = (f32[72,256]{1,0:T(8,128)S(1)}, f32[72,256]{1,0:T(8,128)S(1)}, u32[]{:S(2)}, u32[]{:S(2)}) collective-permute-start(f32[72,256]{1,0:T(8,128)S(1)} %add.20), channel_id=1, source_target_pairs={{0,8},{2,10},{4,12},{6,14},{8,0},{10,2},{12,4},{14,6},{16,24},{18,... | collective-permute-start | bytes 221192 | tf_op jit(solution)/shard_map/ppermute | solution.py:512
  55.2 5.7 %collective-permute-start.12 = (f32[72,256]{1,0:T(8,128)S(1)}, f32[72,256]{1,0:T(8,128)S(1)}, u32[]{:S(2)}, u32[]{:S(2)}) collective-permute-start(f32[72,256]{1,0:T(8,128)S(1)} %add.22), channel_id=1, source_target_pairs={{0,16},{2,18},{4,20},{6,22},{8,24},{10,26},{12,28},{14,30},{16,0},... | collective-permute-start | bytes 221192 | tf_op jit(solution)/shard_map/ppermute | solution.py:512

commit v8 on v7

--- a/solution.py
+++ b/solution.py
@@ -396,13 +396,17 @@
             sweep_layer(*sources, coupling(q), b_at, rows // ROWS, sub, put)
 
 
-def near_kernel(inner, swapped, ex, geo, p0, w, state, b_in, sums_in, out, sums_out, wb, bb, eh, q_buf):
+def near_coupling_kernel(inner, ex, geo, wb, bb, eh):
+    wedge = Wedge(True, ex.shape[0])
+    wedge_couplings(wedge, inner, SWEEPS, lambda q: jnp.ones_like(bb[0]), ex, geo, wb, bb, eh)
+
+
+def near_kernel(inner, swapped, p0, w, wb, bb_in, state, b_in, sums_in, out, sums_out, bb, q_buf):
     wedge = Wedge(True, p0.shape[0])
     ends = SWEEPS - 1
-    wedge_couplings(
-        wedge, inner, SWEEPS, lambda q: swapped[wedge.sent(q, ends)], ex, geo, wb, bb, eh
-    )
-    bb[ends] = bb[ends] * b_in[wedge.own(0)]
+    for k in range(ends):
+        bb[k] = bb_in[k] * swapped[wedge.sent(k - ends, ends)]
+    bb[ends] = bb_in[ends] * b_in[wedge.own(0)]
     sums_out[...] = sums_in[...]
     wedge_sweeps(wedge, inner, p0, w, wb, bb, state, b_in, q_buf, out, sums_out)
 
@@ -600,7 +604,15 @@
     )(potential_guess, permittivity, pads, *raws)
     p0, ex, w, inv2, geo = [fetched(x) for x in (p0, ex, w, inv2, geo)]
     wedge = plane(depth, rows, sector)
-    wedge_box, wedge_couplings_box = near(depth, rows, sector), near(6, depth, rows, sector)
+    wedge_box = near(depth, rows, sector)
+    near_w, near_b = kernel(
+        near_coupling_kernel,
+        [plane(6, depth, rows, sector), wedge],
+        [IN_VMEM] * 3,
+        scratch=[near(depth + 2, rows, sector)],
+        mb=12,
+    )(inner, ex, geo)
+    near_w, near_b = fetched(near_w), fetched(near_b)
     wb, bb = kernel(
         functools.partial(outer_coupling_kernel, band),
         [plane(6, depth, rows, sector), wedge],
@@ -635,9 +647,9 @@
         near_kernel,
         [wedge, plane(rows, sector)],
         [IN_VMEM] * 9,
-        scratch=[wedge_couplings_box, wedge_box, near(depth + 2, rows, sector), near(depth - 1, depth, rows, sector)],
+        scratch=[wedge_box, near(depth - 1, depth, rows, sector)],
         mb=12,
-    )(inner, swapped, ex, geo, p0, w, state, b, sums)
+    )(inner, swapped, p0, w, near_w, near_b, state, b, sums)
     far_out, sums = kernel(
         functools.partial(outer_relax_kernel, band),
         [wedge, plane(rows, sector)],

time: 62.8 us -> 62.3 us (level)
  starting transfers between devices: 28.2 us -> 27.5 us
    ppermute x4, starting transfers between devices: 6.54 us -> 5.79 us  [sums_below(): other = lax.ppermute(total, 'drift', [(i, i ^ step) for i in range(count)])]
where the time goes in v8:
time: 62.3 us; the launch traced here: 62 us
  starting transfers between devices  27.5 us (44%)
  waiting for transfers between devices  17.9 us (29%)
  Pallas kernels  15.8 us (25%)
  between operations  0.85 us (1%)
    ppermute x2, waiting for transfers between devices, swap_rows(): return [lax.ppermute(blocks[0], 'radius', [(0, 1), (1, 0)])]  10.6 us
    ppermute x2, starting transfers between devices, shifted(): return lax.ppermute(block, axis, route)  8.32 us
    ppermute x1, starting transfers between devices, body(): swapped = lax.ppermute(swap, 'drift', partners)  8.11 us
    ppermute x4, waiting for transfers between devices, sums_below(): other = lax.ppermute(total, 'drift', [(i, i ^ step) for i in range(count)])  7.22 us
    ppermute x4, starting transfers between devices, sums_below(): other = lax.ppermute(total, 'drift', [(i, i ^ step) for i in range(count)])  5.79 us
    ppermute x2, starting transfers between devices, swap_rows(): return [lax.ppermute(blocks[0], 'radius', [(0, 1), (1, 0)])]  3.16 us
    pallas_call x1, Pallas kernels, body(): kernel(local_kernel, [plane(layers, band, sector), plane(2, layers, band,...  2.64 us
    pallas_call x1, Pallas kernels, body(): kernel(functools.partial(inner_coupling_kernel, sides), [box, box, plane(...  2.25 us
  transfers between devices with their start and end apart: 13, of which 5 were waited for; matrix products, arithmetic and copies ran while one was open for 0% of the time, Pallas kernels for 21%

profile of v8, /device:TPU:0, one launch (start us, length us, event | category | flops | bytes accessed | tf_op | source)
XLA Modules:
  0.0 62.0 jit_solution(929168075263175299)
XLA Ops:
  0.6 4.9 %collective-permute-start.1 = (f32[16,64,256]{2,1,0:T(8,128)}, f32[16,64,256]{2,1,0:T(8,128)S(1)}, u32[]{:S(2)}, u32[]{:S(2)}) collective-permute-start(f32[16,64,256]{2,1,0:T(8,128)} %ions.5), channel_id=1, source_target_pairs={{0,4},{2,6},{4,8},{6,10},{8,12},{10,14},{12,16},{14,18},{16,20},{1... | collective-permute-start | bytes 3145736 | tf_op jit(solution)/shard_map/ppermute | solution.py:32
  5.6 1.2 %shard_map.94 = (f32[40,8,256]{2,1,0:T(8,128)S(1)}, f32[2,64,256]{2,1,0:T(8,128)S(1)}) custom-call(f32[16,64,256]{2,1,0:T(8,128)} %phi.5, f32[16,64,256]{2,1,0:T(8,128)} %eps.5, f32[16,64,256]{2,1,0:T(8,128)} %ions.5, f32[64,256]{1,0:T(8,128)} %rec.1, s32[64,256]{1,0:T(8,128)} %index.1, s32[64,256]{1,0:T(8,128)} %gap.1, f32[16]{0:T(128)} %table.1), custom_call_target="tpu_custom_call" | custom-call | tf_op jit(solution)/shard_map/pallas_call | solution.py:560
  6.8 1.6 %collective-permute-start = (f32[40,8,256]{2,1,0:T(8,128)S(1)}, f32[40,8,256]{2,1,0:T(8,128)S(1)}, u32[]{:S(2)}, u32[]{:S(2)}) collective-permute-start(f32[40,8,256]{2,1,0:T(8,128)S(1)} %get-tuple-element.32), channel_id=1, source_target_pairs={{0,1},{1,0},{2,3},{3,2},{4,5},{5,4},{6,7},{7,6},{8,9},{9,8},{10,11... | collective-permute-start | bytes 983048 | tf_op jit(solution)/shard_map/ppermute | solution.py:549
  8.4 7.7 %collective-permute-done.refs_0_ = f32[40,8,256]{2,1,0:T(8,128)S(1)} collective-permute-done((f32[40,8,256]{2,1,0:T(8,128)S(1)}, f32[40,8,256]{2,1,0:T(8,128)S(1)}, u32[]{:S(2)}, u32[]{:S(2)}) %collective-permute-start) | collective-permute-done | bytes 327712 | tf_op jit(solution)/shard_map/ppermute | solution.py:549
  16.1 1.4 %shard_map.99 = (f32[11,72,256]{2,1,0:T(8,128)S(1)}, f32[272,256]{1,0:T(8,128)S(1)}, f32[272,256]{1,0:T(8,128)S(1)}, f32[3,72,256]{2,1,0:T(8,128)S(1)}) custom-call(f32[16,64,256]{2,1,0:T(8,128)} %phi.5, f32[16,64,256]{2,1,0:T(8,128)} %eps.5, f32[16,64,256]{2,1,0:T(8,128)} %ions.5, f32[40,8,256]{2,1,0:T(8,128)S(1)} %collective-permute-done.refs_0_), custom_call_target="tpu_custom_call" | custom-call | tf_op jit(solution)/shard_map/pallas_call | solution.py:577
  17.6 0.9 %shard_map.96 = f32[8,8,256]{2,1,0:T(8,128)S(1)} custom-call(f32[16,64,256]{2,1,0:T(8,128)} %ions.5), custom_call_target="tpu_custom_call" | custom-call | tf_op jit(solution)/shard_map/pallas_call | solution.py:552
  18.5 1.6 %collective-permute-start.2 = (f32[8,8,256]{2,1,0:T(8,128)S(1)}, f32[8,8,256]{2,1,0:T(8,128)S(1)}, u32[]{:S(2)}, u32[]{:S(2)}) collective-permute-start(f32[8,8,256]{2,1,0:T(8,128)S(1)} %shard_map.96), channel_id=1, source_target_pairs={{0,1},{1,0},{2,3},{3,2},{4,5},{5,4},{6,7},{7,6},{8,9},{9,8},{10,11... | collective-permute-start | bytes 196616 | tf_op jit(solution)/shard_map/ppermute | solution.py:549
  20.1 3.0 %collective-permute-done.2 = f32[8,8,256]{2,1,0:T(8,128)S(1)} collective-permute-done((f32[8,8,256]{2,1,0:T(8,128)S(1)}, f32[8,8,256]{2,1,0:T(8,128)S(1)}, u32[]{:S(2)}, u32[]{:S(2)}) %collective-permute-start.2) | collective-permute-done | bytes 65568 | tf_op jit(solution)/shard_map/ppermute | solution.py:549
  23.0 3.4 %collective-permute-start.3 = (f32[8,8,256]{2,1,0:T(8,128)S(1)}, f32[8,8,256]{2,1,0:T(8,128)S(1)}, u32[]{:S(2)}, u32[]{:S(2)}) collective-permute-start(f32[8,8,256]{2,1,0:T(8,128)S(1)} %collective-permute-done.2), channel_id=1, source_target_pairs={{0,4},{2,6},{4,8},{6,10},{8,12},{10,14},{12,16},{14,18},{16,20},{1... | collective-permute-start | bytes 196616 | tf_op jit(solution)/shard_map/ppermute | solution.py:32
  26.4 0.7 %collective-permute-start.7 = (f32[272,256]{1,0:T(8,128)S(1)}, f32[272,256]{1,0:T(8,128)S(1)}, u32[]{:S(2)}, u32[]{:S(2)}) collective-permute-start(f32[272,256]{1,0:T(8,128)S(1)} %get-tuple-element.50), channel_id=1, source_target_pairs={{2,4},{4,2},{6,8},{8,6},{10,12},{12,10},{14,16},{16,14},{18,20},{2... | collective-permute-start | bytes 835592 | tf_op jit(solution)/shard_map/ppermute | solution.py:593
  27.1 0.7 %collective-permute-start.6 = (f32[272,256]{1,0:T(8,128)S(1)}, f32[272,256]{1,0:T(8,128)S(1)}, u32[]{:S(2)}, u32[]{:S(2)}) collective-permute-start(f32[272,256]{1,0:T(8,128)S(1)} %get-tuple-element.49), channel_id=1, source_target_pairs={{2,4},{4,2},{6,8},{8,6},{10,12},{12,10},{14,16},{16,14},{18,20},{2... | collective-permute-start | bytes 835592 | tf_op jit(solution)/shard_map/ppermute | solution.py:596
  27.8 2.2 %shard_map.95 = (f32[16,72,256]{2,1,0:T(8,128)S(1)}, f32[16,72,256]{2,1,0:T(8,128)S(1)}, f32[6,16,72,256]{3,2,1,0:T(8,128)S(1)}, f32[16,72,256]{2,1,0:T(8,128)S(1)}, f32[10,72,256]{2,1,0:T(8,128)S(1)}) custom-call(f32[16,64,256]{2,1,0:T(8,128)S(1)} %copy-done, f32[16,64,256]{2,1,0:T(8,128)S(1)} %copy-done.1, f32[2,64,256]{2,1,0:T(8,128)S(1)} %get-tuple-element.31.pads, ...), custom_call_target="tpu_custom_call" | custom-call | tf_op jit(solution)/shard_map/pallas_call | solution.py:599
  31.4 8.1 %collective-permute-start.5 = (f32[3,72,256]{2,1,0:T(8,128)S(1)}, f32[3,72,256]{2,1,0:T(8,128)S(1)}, u32[]{:S(2)}, u32[]{:S(2)}) collective-permute-start(f32[3,72,256]{2,1,0:T(8,128)S(1)} %get-tuple-element.41), channel_id=1, source_target_pairs={{0,2},{2,0},{4,6},{6,4},{8,10},{10,8},{12,14},{14,12},{16,18},{18,... | collective-permute-start | bytes 663560 | tf_op jit(solution)/shard_map/ppermute | solution.py:631
  39.5 2.2 %shard_map.98 = (f32[16,64,256]{2,1,0:T(8,128)}, f32[8,72,256]{2,1,0:T(8,128)S(1)}, f32[72,256]{1,0:T(8,128)S(1)}, f32[2,3,2,72,256]{4,3,2,1,0:T(8,128)S(1)}) custom-call(f32[16,72,256]{2,1,0:T(8,128)S(1)} %get-tuple-element.33.p0, f32[6,16,72,256]{3,2,1,0:T(8,128)S(1)} %get-tuple-element.34.w, f32[16,72,256]{2,1,0:T(8,128)S(1)} %get-tuple-element.37.b.b_in, ...), custom_call_target="tpu_custom_call" | custom-call | tf_op jit(solution)/shard_map/pallas_call | solution.py:632
  42.8 0.9 %shard_map.101 = (f32[4,72,256]{2,1,0:T(8,128)S(1)}, f32[72,256]{1,0:T(8,128)S(1)}) custom-call(f32[11,72,256]{2,1,0:T(8,128)S(1)} %collective-permute-done.4.inner, f32[3,72,256]{2,1,0:T(8,128)S(1)} %collective-permute-done.5.swapped, f32[16,72,256]{2,1,0:T(8,128)S(1)} %get-tuple-element.33.p0, f32[6,16,72,256]{3,2,1,0:T(8,128)S(1)} %get-tuple-element.34.w, ...), custom_call_target="tpu_custom_call" | custom-call | tf_op jit(solution)/shard_map/pallas_call | solution.py:646
  43.8 1.0 %shard_map.103 = (f32[4,72,256]{2,1,0:T(8,128)S(1)}, f32[72,256]{1,0:T(8,128)S(1)}) custom-call(f32[272,256]{1,0:T(8,128)S(1)} %collective-permute-done.6.outer_phi, f32[16,72,256]{2,1,0:T(8,128)S(1)} %get-tuple-element.33.p0, f32[6,16,72,256]{3,2,1,0:T(8,128)S(1)} %get-tuple-element.34.w, f32[6,4,72,256]{3,2,1,0:T(8,128)S(1)} %get-tuple-element.52.wb, ...), custom_call_target="tpu_custom_call" | custom-call | tf_op jit(solution)/shard_map/pallas_call | solution.py:653
  44.8 1.3 %collective-permute-done.9 = f32[72,256]{1,0:T(8,128)S(1)} collective-permute-done((f32[72,256]{1,0:T(8,128)S(1)}, f32[72,256]{1,0:T(8,128)S(1)}, u32[]{:S(2)}, u32[]{:S(2)}) %collective-permute-start.9) | collective-permute-done | bytes 73760 | tf_op jit(solution)/shard_map/ppermute | solution.py:516
  46.1 1.0 %collective-permute-start.10 = (f32[72,256]{1,0:T(8,128)S(1)}, f32[72,256]{1,0:T(8,128)S(1)}, u32[]{:S(2)}, u32[]{:S(2)}) collective-permute-start(f32[72,256]{1,0:T(8,128)S(1)} %add.18), channel_id=1, source_target_pairs={{0,4},{2,6},{4,0},{6,2},{8,12},{10,14},{12,8},{14,10},{16,20},{18,... | collective-permute-start | bytes 221192 | tf_op jit(solution)/shard_map/ppermute | solution.py:516
  47.1 3.4 %collective-permute-done.10 = f32[72,256]{1,0:T(8,128)S(1)} collective-permute-done((f32[72,256]{1,0:T(8,128)S(1)}, f32[72,256]{1,0:T(8,128)S(1)}, u32[]{:S(2)}, u32[]{:S(2)}) %collective-permute-start.10) | collective-permute-done | bytes 73760 | tf_op jit(solution)/shard_map/ppermute | solution.py:516
  50.5 1.8 %collective-permute-start.11 = (f32[72,256]{1,0:T(8,128)S(1)}, f32[72,256]{1,0:T(8,128)S(1)}, u32[]{:S(2)}, u32[]{:S(2)}) collective-permute-start(f32[72,256]{1,0:T(8,128)S(1)} %add.20), channel_id=1, source_target_pairs={{0,8},{2,10},{4,12},{6,14},{8,0},{10,2},{12,4},{14,6},{16,24},{18,... | collective-permute-start | bytes 221192 | tf_op jit(solution)/shard_map/ppermute | solution.py:516
  52.3 2.6 %collective-permute-done.11 = f32[72,256]{1,0:T(8,128)S(1)} collective-permute-done((f32[72,256]{1,0:T(8,128)S(1)}, f32[72,256]{1,0:T(8,128)S(1)}, u32[]{:S(2)}, u32[]{:S(2)}) %collective-permute-start.11) | collective-permute-done | bytes 73760 | tf_op jit(solution)/shard_map/ppermute | solution.py:516
  54.9 2.8 %collective-permute-start.12 = (f32[72,256]{1,0:T(8,128)S(1)}, f32[72,256]{1,0:T(8,128)S(1)}, u32[]{:S(2)}, u32[]{:S(2)}) collective-permute-start(f32[72,256]{1,0:T(8,128)S(1)} %add.22), channel_id=1, source_target_pairs={{0,16},{2,18},{4,20},{6,22},{8,24},{10,26},{12,28},{14,30},{16,0},... | collective-permute-start | bytes 221192 | tf_op jit(solution)/shard_map/ppermute | solution.py:516
  57.8 2.6 %shard_map.104 = (f32[16,64,256]{2,1,0:T(8,128)}, f32[2,16,64,256]{3,2,1,0:T(8,128)S(1)}) custom-call(f32[4,72,256]{2,1,0:T(8,128)S(1)} %get-tuple-element.47.near, f32[8,72,256]{2,1,0:T(8,128)S(1)} %get-tuple-element.48.inner, f32[4,72,256]{2,1,0:T(8,128)S(1)} %get-tuple-element.55.far), custom_call_target="tpu_custom_call" | custom-call | tf_op jit(solution)/shard_map/pallas_call | solution.py:660
  60.5 1.6 %shard_map.105 = f32[2,16,64,256]{3,2,1,0:T(8,128)} custom-call(f32[2,16,64,256]{3,2,1,0:T(8,128)S(1)} %get-tuple-element.57.local, f32[72,256]{1,0:T(8,128)S(1)} %select_add_fusion.prefix), custom_call_target="tpu_custom_call" | custom-call | tf_op jit(solution)/shard_map/pallas_call | solution.py:668
  (22 shorter events, 2.6 us)
Async XLA Ops:
  0.6 30.1 %collective-permute-start.1 = (f32[16,64,256]{2,1,0:T(8,128)}, f32[16,64,256]{2,1,0:T(8,128)S(1)}, u32[]{:S(2)}, u32[]{:S(2)}) collective-permute-start(f32[16,64,256]{2,1,0:T(8,128)} %ions.5), channel_id=1, source_target_pairs={{0,4},{2,6},{4,8},{6,10},{8,12},{10,14},{12,16},{14,18},{16,20},{1... | collective-permute-start | bytes 3145736 | tf_op jit(solution)/shard_map/ppermute | solution.py:32
  6.8 21.0 %copy-start = (f32[16,64,256]{2,1,0:T(8,128)S(1)}, f32[16,64,256]{2,1,0:T(8,128)}, u32[]{:S(2)}) copy-start(f32[16,64,256]{2,1,0:T(8,128)} %phi.5) | copy-start | bytes 3145732
  6.8 21.0 %copy-start.1 = (f32[16,64,256]{2,1,0:T(8,128)S(1)}, f32[16,64,256]{2,1,0:T(8,128)}, u32[]{:S(2)}) copy-start(f32[16,64,256]{2,1,0:T(8,128)} %eps.5) | copy-start | bytes 3145732
  6.8 9.2 %collective-permute-start = (f32[40,8,256]{2,1,0:T(8,128)S(1)}, f32[40,8,256]{2,1,0:T(8,128)S(1)}, u32[]{:S(2)}, u32[]{:S(2)}) collective-permute-start(f32[40,8,256]{2,1,0:T(8,128)S(1)} %get-tuple-element.32), channel_id=1, source_target_pairs={{0,1},{1,0},{2,3},{3,2},{4,5},{5,4},{6,7},{7,6},{8,9},{9,8},{10,11... | collective-permute-start | bytes 983048 | tf_op jit(solution)/shard_map/ppermute | solution.py:549
  17.5 24.3 %collective-permute-start.4 = (f32[11,72,256]{2,1,0:T(8,128)S(1)}, f32[11,72,256]{2,1,0:T(8,128)S(1)}, u32[]{:S(2)}, u32[]{:S(2)}) collective-permute-start(f32[11,72,256]{2,1,0:T(8,128)S(1)} %get-tuple-element.40), channel_id=1, source_target_pairs={{0,2},{2,0},{4,6},{6,4},{8,10},{10,8},{12,14},{14,12},{16,18},{18,... | collective-permute-start | bytes 2433032 | tf_op jit(solution)/shard_map/ppermute | solution.py:595
  18.5 4.5 %collective-permute-start.2 = (f32[8,8,256]{2,1,0:T(8,128)S(1)}, f32[8,8,256]{2,1,0:T(8,128)S(1)}, u32[]{:S(2)}, u32[]{:S(2)}) collective-permute-start(f32[8,8,256]{2,1,0:T(8,128)S(1)} %shard_map.96), channel_id=1, source_target_pairs={{0,1},{1,0},{2,3},{3,2},{4,5},{5,4},{6,7},{7,6},{8,9},{9,8},{10,11... | collective-permute-start | bytes 196616 | tf_op jit(solution)/shard_map/ppermute | solution.py:549
  23.0 7.0 %collective-permute-start.3 = (f32[8,8,256]{2,1,0:T(8,128)S(1)}, f32[8,8,256]{2,1,0:T(8,128)S(1)}, u32[]{:S(2)}, u32[]{:S(2)}) collective-permute-start(f32[8,8,256]{2,1,0:T(8,128)S(1)} %collective-permute-done.2), channel_id=1, source_target_pairs={{0,4},{2,6},{4,8},{6,10},{8,12},{10,14},{12,16},{14,18},{16,20},{1... | collective-permute-start | bytes 196616 | tf_op jit(solution)/shard_map/ppermute | solution.py:32
  26.4 15.8 %collective-permute-start.7 = (f32[272,256]{1,0:T(8,128)S(1)}, f32[272,256]{1,0:T(8,128)S(1)}, u32[]{:S(2)}, u32[]{:S(2)}) collective-permute-start(f32[272,256]{1,0:T(8,128)S(1)} %get-tuple-element.50), channel_id=1, source_target_pairs={{2,4},{4,2},{6,8},{8,6},{10,12},{12,10},{14,16},{16,14},{18,20},{2... | collective-permute-start | bytes 835592 | tf_op jit(solution)/shard_map/ppermute | solution.py:593
  27.1 16.6 %collective-permute-start.6 = (f32[272,256]{1,0:T(8,128)S(1)}, f32[272,256]{1,0:T(8,128)S(1)}, u32[]{:S(2)}, u32[]{:S(2)}) collective-permute-start(f32[272,256]{1,0:T(8,128)S(1)} %get-tuple-element.49), channel_id=1, source_target_pairs={{2,4},{4,2},{6,8},{8,6},{10,12},{12,10},{14,16},{16,14},{18,20},{2... | collective-permute-start | bytes 835592 | tf_op jit(solution)/shard_map/ppermute | solution.py:596
  30.1 12.2 %collective-permute-start.8 = (f32[3,72,256]{2,1,0:T(8,128)S(1)}, f32[3,72,256]{2,1,0:T(8,128)S(1)}, u32[]{:S(2)}, u32[]{:S(2)}) collective-permute-start(f32[3,72,256]{2,1,0:T(8,128)S(1)} %get-tuple-element.51), channel_id=1, source_target_pairs={{2,8},{6,12},{10,16},{14,20},{18,24},{22,28},{3,9},{7,13},{11,17},... | collective-permute-start | bytes 663560 | tf_op jit(solution)/shard_map/ppermute | solution.py:594
  31.4 11.4 %collective-permute-start.5 = (f32[3,72,256]{2,1,0:T(8,128)S(1)}, f32[3,72,256]{2,1,0:T(8,128)S(1)}, u32[]{:S(2)}, u32[]{:S(2)}) collective-permute-start(f32[3,72,256]{2,1,0:T(8,128)S(1)} %get-tuple-element.41), channel_id=1, source_target_pairs={{0,2},{2,0},{4,6},{6,4},{8,10},{10,8},{12,14},{14,12},{16,18},{18,... | collective-permute-start | bytes 663560 | tf_op jit(solution)/shard_map/ppermute | solution.py:631
  44.7 1.3 %collective-permute-start.9 = (f32[72,256]{1,0:T(8,128)S(1)}, f32[72,256]{1,0:T(8,128)S(1)}, u32[]{:S(2)}, u32[]{:S(2)}) collective-permute-start(f32[72,256]{1,0:T(8,128)S(1)} %get-tuple-element.58), channel_id=1, source_target_pairs={{0,2},{2,0},{4,6},{6,4},{8,10},{10,8},{12,14},{14,12},{16,18},{18,... | collective-permute-start | bytes 221192 | tf_op jit(solution)/shard_map/ppermute | solution.py:516
  46.1 4.4 %collective-permute-start.10 = (f32[72,256]{1,0:T(8,128)S(1)}, f32[72,256]{1,0:T(8,128)S(1)}, u32[]{:S(2)}, u32[]{:S(2)}) collective-permute-start(f32[72,256]{1,0:T(8,128)S(1)} %add.18), channel_id=1, source_target_pairs={{0,4},{2,6},{4,0},{6,2},{8,12},{10,14},{12,8},{14,10},{16,20},{18,... | collective-permute-start | bytes 221192 | tf_op jit(solution)/shard_map/ppermute | solution.py:516
  50.5 4.4 %collective-permute-start.11 = (f32[72,256]{1,0:T(8,128)S(1)}, f32[72,256]{1,0:T(8,128)S(1)}, u32[]{:S(2)}, u32[]{:S(2)}) collective-permute-start(f32[72,256]{1,0:T(8,128)S(1)} %add.20), channel_id=1, source_target_pairs={{0,8},{2,10},{4,12},{6,14},{8,0},{10,2},{12,4},{14,6},{16,24},{18,... | collective-permute-start | bytes 221192 | tf_op jit(solution)/shard_map/ppermute | solution.py:516
  54.9 5.5 %collective-permute-start.12 = (f32[72,256]{1,0:T(8,128)S(1)}, f32[72,256]{1,0:T(8,128)S(1)}, u32[]{:S(2)}, u32[]{:S(2)}) collective-permute-start(f32[72,256]{1,0:T(8,128)S(1)} %add.22), channel_id=1, source_target_pairs={{0,16},{2,18},{4,20},{6,22},{8,24},{10,26},{12,28},{14,30},{16,0},... | collective-permute-start | bytes 221192 | tf_op jit(solution)/shard_map/ppermute | solution.py:516
